TPU v7x, 128 devices: a whole 4x4x4 slice. The times are simulated.
128 devices in a mesh: layer: 16 (over y_hi, x, core), lat: 8 (over y_lo, z).
Axes of the slice: x: 4, y: 4 (y_hi: 2, y_lo: 2; y = y_hi * 2 + y_lo), z: 4, core: 2. Of those that a mesh axis runs over, the one named last changes fastest.
Arguments:
- source: float32 [16, 2, 1536, 128], P('layer', None, 'lat'), may hold values from -6 to 6
- wavenumber: float32 [16, 1536, 128], P('layer', 'lat'), may hold values from 0.1 to 1
- green_down: bfloat16 [16, 2, 1536, 3072], P('layer', None, 'lat'), may hold values from -0.109375 to 0.109375
- green_up: bfloat16 [16, 2, 1536, 3072], P('layer', None, 'lat'), may hold values from -0.109375 to 0.109375
Outputs:
- down_trace: float32 [16, 2, 1536, 128], P('layer', None, 'lat')
- up_trace: float32 [16, 2, 1536, 128], P('layer', None, 'lat')
All inputs are finite; a program needn't handle non-finite values.
Results may differ from a plain program's by a relative error of at most 0.017.
Values may be sent and summed in bfloat16 or wider, within the bound.
No kernel may reach another device: no remote copies, remote signals or barrier semaphores. Data moves between devices by JAX's collectives and lax.ppermute only.
A program may use at most 64 MiB of HBM per device.

v0:
```python
import functools

import jax
import jax.numpy as jnp
import numpy as np
from jax import lax
from jax.experimental import pallas as pl
from jax.experimental.pallas import tpu as pltpu
from jax.sharding import PartitionSpec as P


RELAX = 4
LAYERS = 16
LATS = 8
HALF = LAYERS // 2
BOTH = ("layer", "lat")
SHARED = ((1, 5), (2, 6), (3, 7), (4, 9), (10, 13), (11, 14), (12, 15))
FAN = 4
SWAP = 6
BATCHES = ((3, 1), (0,), (2,))


relax_weight = 0.8
damping = 0.5


def partner_of(layer, lat):
    return lat ^ 4 if layer % 2 == 0 else lat ^ 1


def target_of(layer, lat, r):
    y, z = lat >> 2, lat & 3
    a, b = r >> 1, r & 1
    if layer % 2 == 0:
        return (((z & 1) ^ a) << 2) | (y + 2 * ((z >> 1) ^ b))
    return ((z & 1) << 2) | ((y ^ a) + 2 * ((z >> 1) ^ b))


def edges_of(step):
    return [(step - 1, step), (LAYERS - step, LAYERS - 1 - step)]


def routes(step, r):
    steps = next(group for group in SHARED if step in group)
    edges = [edge for s in steps for edge in edges_of(s)]
    return [
        (src * LATS + j, dst * LATS + target_of(src, j, r)) for src, dst in edges for j in range(LATS)
    ]


def spread(step, r):
    return [
        (dst * LATS + j, dst * LATS + target_of(src, j, r))
        for src, dst in edges_of(step)
        for j in range(LATS)
    ]


def straight(step):
    return [(src * LATS + j, dst * LATS + j) for src, dst in edges_of(step) for j in range(LATS)]


PAIRS = [(l * LATS + j, l * LATS + partner_of(l, j)) for l in range(LAYERS) for j in range(LATS)]


def rank_table():
    table = np.zeros((2, LATS, FAN), np.int32)
    for parity in range(2):
        source = 1 - parity
        for j in range(LATS):
            pair = j % 4 if source % 2 == 0 else j // 2
            for r in range(FAN):
                table[parity, target_of(source, j, r), pair] = r
    return table


def padded_2(block, axis, dim, width):
    count = lax.axis_size(axis)
    forward = [(i, i + 1) for i in range(count - 1)]
    backward = [(target, source) for source, target in forward]
    last = lax.slice_in_dim(block, block.shape[dim] - width, None, axis=dim)
    low = lax.ppermute(last, axis, forward)
    high = lax.ppermute(lax.slice_in_dim(block, 0, width, axis=dim), axis, backward)
    return jnp.concatenate([low, block, high], axis=dim)


def relax_step(field, lateral_pad, forcing, diag_real, diag_imag, inverse_real, inverse_imag):
    along = jnp.pad(field, ((0, 0), (0, 0), (1, 1)))
    beside = lateral_pad[:, 2:] + lateral_pad[:, :-2] + along[:, :, 2:] + along[:, :, :-2]
    apply_real = diag_real * field[0] - diag_imag * field[1] - beside[0]
    apply_imag = diag_real * field[1] + diag_imag * field[0] - beside[1]
    res_real = forcing[0] - apply_real
    res_imag = forcing[1] - apply_imag
    step_real = res_real * inverse_real - res_imag * inverse_imag
    step_imag = res_real * inverse_imag + res_imag * inverse_real
    return field + relax_weight * jnp.stack([step_real, step_imag], 0)


def coefficients(wave_sq):
    diag_real = 4.0 - wave_sq
    diag_imag = damping * wave_sq
    denom = diag_real * diag_real + diag_imag * diag_imag
    return (diag_real, diag_imag, diag_real / denom, -diag_imag / denom)


def relaxed(forcing, wave_sq):
    slab = forcing.shape[1]
    width = slab * lax.axis_size("lat")
    stacked = jnp.concatenate([forcing, wave_sq[None]], 0)
    wide = padded_2(stacked.astype(jnp.bfloat16), "lat", 1, RELAX).astype(stacked.dtype)
    wide_forcing = wide[:2]
    diag_real, diag_imag, inverse_real, inverse_imag = coefficients(wide[2])
    position = lax.axis_index("lat") * slab - RELAX + lax.iota(jnp.int32, slab + 2 * RELAX)
    inside = ((position >= 0) & (position < width)).astype(jnp.float32)[None, :, None]
    field = jnp.zeros_like(wide_forcing)
    for _ in range(RELAX):
        padded = jnp.pad(field, ((0, 0), (1, 1), (0, 0)))
        field = (
            relax_step(
                field, padded, wide_forcing, diag_real, diag_imag, inverse_real, inverse_imag
            )
            * inside
        )
    return field[:, RELAX : RELAX + slab]


def load_kernel(info, own, other, out, first, second, sems):
    slab = first.shape[1]
    cells = first.shape[2] // 2
    copies = [
        pltpu.make_async_copy(own, first, sems.at[0]),
        pltpu.make_async_copy(other, second, sems.at[1]),
    ]
    for copy in copies:
        copy.start()
    for copy in copies:
        copy.wait()
    even = info[FAN] == 0
    band = slab // 3

    @pl.loop(0, 6)
    def _(step):
        part = lax.div(step, 3)
        start = lax.rem(step, 3) * band
        near = pl.ds(pl.multiple_of(start, band), band)
        for held, green in ((info[FAN + 1], first), (1 - info[FAN + 1], second)):
            base = held * 2 * slab + part * slab + start
            rows = pl.ds(pl.multiple_of(base, band), band)

            @pl.when(even)
            def _():
                for pair in range(FAN):
                    for column in range(2):
                        at = column * cells + pair * 2 * slab
                        out[info[pair], rows, column * 2 * slab : (column + 1) * 2 * slab] = green[
                            part, near, at : at + 2 * slab
                        ]

            @pl.when(jnp.logical_not(even))
            def _():
                for pair in range(FAN):
                    for column in range(2):
                        low = column * cells + pair * slab
                        high = low + cells // 2
                        left = green[part, near, low : low + slab]
                        right = green[part, near, high : high + slab]
                        out[info[pair], rows, column * 2 * slab : (column + 1) * 2 * slab] = (
                            jnp.concatenate([left, right], 1)
                        )


def loaded(info, own, other):
    slab, cells = own.shape[1], own.shape[2] // 2
    anywhere = pl.BlockSpec(memory_space=pl.ANY)
    return pl.pallas_call(
        load_kernel,
        out_shape=jax.ShapeDtypeStruct((FAN, 4 * slab, 2 * cells // FAN), own.dtype),
        in_specs=[pl.BlockSpec(memory_space=pltpu.SMEM), anywhere, anywhere],
        out_specs=pl.BlockSpec(memory_space=pltpu.VMEM),
        scratch_shapes=[
            pltpu.VMEM(own.shape, own.dtype),
            pltpu.VMEM(own.shape, own.dtype),
            pltpu.SemaphoreType.DMA((2,)),
        ],
        compiler_params=pltpu.CompilerParams(vmem_limit_bytes=16 * 1024 * 1024),
        cost_estimate=pl.CostEstimate(
            flops=0, bytes_accessed=8 * own.size, transcendentals=0
        ),
    )(info, own, other)


def is_live(step):
    layer = lax.axis_index("layer")
    return jnp.logical_or(layer == step, layer == LAYERS - 1 - step)


def product(batch, green, pieces, whole, total, sums):
    cells, lanes = pieces[0].shape
    half = lanes // 2
    for k, piece in enumerate(pieces):
        block = piece[...]
        whole[k, :cells] = block
        whole[k, cells:] = jnp.concatenate([block[:, half:], block[:, :half]], 1)
    rows = total.shape[0] // 2

    @pl.loop(0, 2)
    def _(part):
        at = pl.ds(pl.multiple_of(part * rows, rows), rows)
        terms = [part[at, :] for part in sums]
        for k, r in enumerate(batch):
            terms.append(jnp.dot(green[r, at, :], whole[k], preferred_element_type=jnp.float32))
        total[at, :] = functools.reduce(jnp.add, terms)


def early_kernel(batch, step, green, *refs):
    pieces, sums, (total, whole) = refs[: len(batch)], refs[len(batch) : -2], refs[-2:]

    @pl.when(is_live(step))
    def _():
        product(batch, green, pieces, whole, total, sums)


def late_kernel(batch, step, green, trace, before, sent, earlier, *refs):
    pieces, (after, rounded, whole, rest) = refs[: len(batch)], refs[len(batch) :]
    slab = trace.shape[0] // 2
    half = trace.shape[1] // 2

    @pl.when(is_live(step))
    def _():
        product(batch, green, pieces, whole, rest, (earlier,))
        lane = lax.broadcasted_iota(jnp.int32, (slab, 2 * half), 1)
        for side in range(2):
            rows = slice(side * slab, (side + 1) * slab)
            real = rest[2 * side * slab : (2 * side + 1) * slab, :]
            imag = rest[(2 * side + 1) * slab : (2 * side + 2) * slab, :]
            value = trace[rows, :] + jnp.where(lane < half, real, pltpu.roll(imag, half, 1))
            after[rows, :] = value
            rounded[rows, :] = value.astype(jnp.bfloat16)

    @pl.when(jnp.logical_not(is_live(step)))
    def _():
        after[...] = before[...]
        rounded[...] = sent[...]


def one_step(step, green, trace, before, sent, pieces):
    rows, lanes = trace.shape
    vmem = pl.BlockSpec(memory_space=pltpu.VMEM)
    *early, late = BATCHES
    params = pltpu.CompilerParams(vmem_limit_bytes=8 * 1024 * 1024)

    def cost(batch):
        work = 2 * green.shape[1] * green.shape[2] * lanes * len(batch)
        return pl.CostEstimate(flops=work, bytes_accessed=work // 128, transcendentals=0)

    def held(batch):
        return pltpu.VMEM((len(batch), 2 * rows, lanes), jnp.bfloat16)

    sums = []
    for batch in early:
        total = pl.pallas_call(
            functools.partial(early_kernel, batch, step),
            out_shape=jax.ShapeDtypeStruct((2 * rows, lanes), jnp.float32),
            in_specs=[vmem] * (1 + len(batch) + len(sums)),
            out_specs=vmem,
            scratch_shapes=[held(batch)],
            compiler_params=params,
            cost_estimate=cost(batch),
        )(green, *[pieces[r] for r in batch], *sums)
        sums = [total]
    return pl.pallas_call(
        functools.partial(late_kernel, late, step),
        out_shape=(
            jax.ShapeDtypeStruct((rows, lanes), jnp.float32),
            jax.ShapeDtypeStruct((rows, lanes), jnp.bfloat16),
        ),
        in_specs=[vmem] * (5 + len(late)),
        out_specs=(vmem, vmem),
        scratch_shapes=[held(late), pltpu.VMEM((2 * rows, lanes), jnp.float32)],
        compiler_params=params,
        cost_estimate=cost(late),
    )(green, trace, before, sent, *sums, *[pieces[r] for r in late])


def local(source, wavenumber, green_down, green_up):
    layer = lax.axis_index("layer")
    lat = lax.axis_index("lat")
    low = layer < HALF
    parity = layer & 1
    place = jnp.where(parity == 0, lat >> 2, lat & 1)
    upper = place == 1
    ranks = jnp.asarray(rank_table().reshape(2 * LATS, FAN))
    mine = lax.dynamic_index_in_dim(ranks, parity * LATS + lat, 0, keepdims=False)
    info = jnp.concatenate([mine, jnp.stack([parity, place])])

    own_first = jnp.where(low, green_down[0], green_up[0])
    own_first, source, wavenumber = lax.optimization_barrier((own_first, source, wavenumber))
    other_first = lax.ppermute(own_first, BOTH, PAIRS)

    traces = relaxed(source[0], wavenumber[0])
    half = traces.shape[2] // 2

    def packed(part):
        columns = slice(part * half, (part + 1) * half)
        return jnp.concatenate([traces[0, :, columns], traces[1, :, columns]], 1)

    keep = jnp.where(upper, packed(1), packed(0))
    give = jnp.where(upper, packed(0), packed(1))
    swapped = lax.ppermute(give, BOTH, PAIRS)
    trace = jnp.where(
        upper, jnp.concatenate([swapped, keep], 0), jnp.concatenate([keep, swapped], 0)
    )
    green_first = loaded(info, own_first, other_first)

    def advance(step, green, before, sent):
        if step == HALF:
            shifted = lax.ppermute(sent, BOTH, straight(step))
            pieces = [lax.ppermute(shifted, BOTH, spread(step, r)) for r in range(FAN)]
        else:
            pieces = [lax.ppermute(sent, BOTH, routes(step, r)) for r in range(FAN)]
        return one_step(step, green, trace, before, sent, pieces)

    slab = traces.shape[1]

    def joined(done):
        held = jnp.where(upper, done[slab:], done[:slab])
        got = lax.ppermute(jnp.where(upper, done[:slab], done[slab:]), BOTH, PAIRS)
        left = jnp.where(upper, got, held)
        right = jnp.where(upper, held, got)
        real = jnp.concatenate([left[:, :half], right[:, :half]], 1)
        imag = jnp.concatenate([left[:, half:], right[:, half:]], 1)
        return jnp.stack([real, imag], 0)

    first, sent = trace, trace.astype(jnp.bfloat16)
    for step in range(1, HALF):
        if step == SWAP:
            down_later, up_later, sent = lax.optimization_barrier((green_down, green_up, sent))
            own_second = jnp.where(low, up_later[0], down_later[0])
            other_second = lax.ppermute(own_second, BOTH, PAIRS)
        first, sent = advance(step, green_first, first, sent)
    green_second = loaded(info, own_second, other_second)
    near = joined(first)
    second = trace
    for step in range(HALF, LAYERS):
        second, sent = advance(step, green_second, second, sent)
    far = joined(second)
    down = jnp.where(low, near, far)
    up = jnp.where(low, far, near)
    return (down[None], up[None])


def solution(mesh):
    return jax.shard_map(
        local,
        mesh=mesh,
        in_specs=(
            P("layer", None, "lat", None),
            P("layer", "lat", None),
            P("layer", None, "lat", None),
            P("layer", None, "lat", None),
        ),
        out_specs=(P("layer", None, "lat", None), P("layer", None, "lat", None)),
        check_vma=False,
    )
```

profile of v0, /device:TPU:1, one launch (start us, length us, event | category | flops | bytes accessed | tf_op | source)
XLA Modules:
  0.0 220.3 jit_solution(17791429091568564368)
XLA Ops:
  0.7 2.0 select_bitcast_fusion.1.own
  2.7 4.4 %collective-permute-start.1 = (bf16[3,4,128]{2,1,0:T(4,128)(2,1)S(1)}, bf16[3,4,128]{2,1,0:T(4,128)(2,1)S(1)}, u32[]{:S(2)}, u32[]{:S(2)}) collective-permute-start(bf16[3,4,128]{2,1,0:T(4,128)(2,1)S(1)} %get-tuple-element.97), channel_id=1, source_target_pairs={{0,1},{1,2},{2,3},{3,4},{4,5},{5,6},{6,7},{8,9},{9,10},{10,11},{11... | collective-permute-start | bytes 9224 | tf_op jit(solution)/shard_map/ppermute | solution.py:82
  7.1 1.3 collective-permute-start.2
  8.4 2.3 %collective-permute-start = (bf16[2,192,3072]{2,1,0:T(8,128)(2,1)S(1)}, bf16[2,192,3072]{2,1,0:T(8,128)(2,1)}, u32[]{:S(2)}, u32[]{:S(2)}) collective-permute-start(bf16[2,192,3072]{2,1,0:T(8,128)(2,1)S(1)} %select_bitcast_fusion.1.own), channel_id=1, source_target_pairs={{0,4},{1,5},{2,6},{3,7},{4,0},{5,1},{6,2},{7,3},{8,9},{9,8},{10,11... | collective-permute-start | bytes 7077896 | tf_op jit(solution)/shard_map/ppermute | solution.py:298
  13.5 11.3 %collective-permute-start.3 = (f32[192,128]{1,0:T(8,128)S(1)}, f32[192,128]{1,0:T(8,128)S(1)}, u32[]{:S(2)}, u32[]{:S(2)}) collective-permute-start(f32[192,128]{1,0:T(8,128)S(1)} %get-tuple-element.88), channel_id=1, source_target_pairs={{0,4},{1,5},{2,6},{3,7},{4,0},{5,1},{6,2},{7,3},{8,9},{9,8},{10,11... | collective-permute-start | bytes 294920 | tf_op jit(solution)/shard_map/ppermute | solution.py:309
  25.5 12.9 %collective-permute-done.3 = f32[192,128]{1,0:T(8,128)S(1)} collective-permute-done((f32[192,128]{1,0:T(8,128)S(1)}, f32[192,128]{1,0:T(8,128)S(1)}, u32[]{:S(2)}, u32[]{:S(2)}) %collective-permute-start.3) | collective-permute-done | bytes 98336 | tf_op jit(solution)/shard_map/ppermute | solution.py:309
  38.5 1.3 collective-permute-start.5
  39.8 1.3 collective-permute-start.6
  41.1 1.3 collective-permute-start.4
  42.4 1.3 collective-permute-start.7
  43.8 4.1 %shard_map.68.green = bf16[4,768,768]{2,1,0:T(8,128)(2,1)S(1)} custom-call(s32[6]{0:T(128)S(1)} %pad_add_fusion.info, bf16[2,192,3072]{2,1,0:T(8,128)(2,1)S(1)} %select_bitcast_fusion.1.own, bf16[2,192,3072]{2,1,0:T(8,128)(2,1)} %collective-permute-done.other), custom_call_target="tpu_custom_call" | custom-call | bytes 9437184 | tf_op jit(solution)/shard_map/pallas_call | solution.py:175
  47.9 2.1 collective-permute-done.6.refs_1_
  50.0 1.1 shard_map.69.refs_1_
  51.1 0.7 shard_map.70.earlier
  51.9 0.9 shard_map.71
  52.8 1.3 collective-permute-start.10
  54.1 1.3 collective-permute-start.9
  55.4 1.3 collective-permute-start.8
  56.7 1.3 collective-permute-start.11
  58.3 1.3 collective-permute-done.11.refs_0_
  65.3 1.3 collective-permute-start.21
  66.6 1.3 collective-permute-start.22
  67.9 1.3 collective-permute-start.20
  69.2 1.3 collective-permute-start.23
  70.5 1.9 collective-permute-done.21.refs_0_
  72.4 2.3 %collective-permute-done.22.refs_1_ = bf16[384,128]{1,0:T(8,128)(2,1)S(1)} collective-permute-done((bf16[384,128]{1,0:T(8,128)(2,1)S(1)}, bf16[384,128]{1,0:T(8,128)(2,1)S(1)}, u32[]{:S(2)}, u32[]{:S(2)}) %collective-permute-start.22) | collective-permute-done | bytes 98336 | tf_op jit(solution)/shard_map/ppermute | solution.py:320
  74.8 1.1 collective-permute-done.23.refs_0_
  75.9 1.6 copy-done
  78.5 1.0 collective-permute-start.33
  79.5 3.8 %collective-permute-start.25 = (bf16[384,128]{1,0:T(8,128)(2,1)S(1)}, bf16[384,128]{1,0:T(8,128)(2,1)S(1)}, u32[]{:S(2)}, u32[]{:S(2)}) collective-permute-start(bf16[384,128]{1,0:T(8,128)(2,1)S(1)} %get-tuple-element.50.sent), channel_id=1, source_target_pairs={{8,19},{9,23},{10,17},{11,21},{12,18},{13,22},{14,16},{15,20},{112... | collective-permute-start | bytes 294920 | tf_op jit(solution)/shard_map/ppermute | solution.py:320
  83.3 1.9 collective-permute-start.26
  85.3 1.3 collective-permute-start.24
  86.6 1.3 collective-permute-start.27
  88.2 1.3 collective-permute-done.27.refs_0_
  95.9 10.6 %collective-permute-done.33.other = bf16[2,192,3072]{2,1,0:T(8,128)(2,1)S(1)} collective-permute-done((bf16[2,192,3072]{2,1,0:T(8,128)(2,1)S(1)}, bf16[2,192,3072]{2,1,0:T(8,128)(2,1)S(1)}, u32[]{:S(2)}, u32[]{:S(2)}) %collective-permute-start.33) | collective-permute-done | bytes 2359328 | tf_op jit(solution)/shard_map/ppermute | solution.py:339
  106.5 2.6 %shard_map.90.green = bf16[4,768,768]{2,1,0:T(8,128)(2,1)S(1)} custom-call(s32[6]{0:T(128)S(1)} %pad_add_fusion.info, bf16[2,192,3072]{2,1,0:T(8,128)(2,1)S(1)} %select_bitcast_fusion.own, bf16[2,192,3072]{2,1,0:T(8,128)(2,1)S(1)} %collective-permute-done.33.other), custom_call_target="tpu_custom_call" | custom-call | bytes 9437184 | tf_op jit(solution)/shard_map/pallas_call | solution.py:175
  115.0 1.3 collective-permute-start.48
  116.3 1.3 collective-permute-start.49
  117.6 1.3 collective-permute-start.47
  118.9 1.3 collective-permute-start.50
  120.2 26.6 %collective-permute-done.48.refs_0_ = bf16[384,128]{1,0:T(8,128)(2,1)S(1)} collective-permute-done((bf16[384,128]{1,0:T(8,128)(2,1)S(1)}, bf16[384,128]{1,0:T(8,128)(2,1)S(1)}, u32[]{:S(2)}, u32[]{:S(2)}) %collective-permute-start.48) | collective-permute-done | bytes 98336 | tf_op jit(solution)/shard_map/ppermute | solution.py:320
  146.8 1.6 collective-permute-done.49.refs_1_
  148.5 1.9 collective-permute-done.50.refs_0_
  150.5 1.3 collective-permute-start.52
  151.8 1.3 collective-permute-start.53
  153.1 1.3 collective-permute-start.51
  154.4 1.3 collective-permute-start.54
  155.9 1.4 collective-permute-done.54.refs_0_
  160.2 1.3 collective-permute-start.60
  161.5 1.3 collective-permute-start.61
  162.8 1.3 collective-permute-start.59
  164.1 1.3 collective-permute-start.62
  165.5 38.0 %collective-permute-done.60.refs_0_ = bf16[384,128]{1,0:T(8,128)(2,1)S(1)} collective-permute-done((bf16[384,128]{1,0:T(8,128)(2,1)S(1)}, bf16[384,128]{1,0:T(8,128)(2,1)S(1)}, u32[]{:S(2)}, u32[]{:S(2)}) %collective-permute-start.60) | collective-permute-done | bytes 98336 | tf_op jit(solution)/shard_map/ppermute | solution.py:320
  203.5 1.3 collective-permute-done.61.refs_1_
  204.8 1.1 shard_map.109.refs_1_
  205.9 0.7 shard_map.110.earlier
  206.7 0.9 shard_map.111
  207.6 1.3 collective-permute-start.64
  208.9 1.3 collective-permute-start.65
  210.2 1.3 collective-permute-start.63
  211.5 1.3 collective-permute-start.66
  212.9 2.0 collective-permute-done.66.refs_0_
  216.3 2.8 %collective-permute-done.67 = f32[192,128]{1,0:T(8,128)S(1)} collective-permute-done((f32[192,128]{1,0:T(8,128)S(1)}, f32[192,128]{1,0:T(8,128)S(1)}, u32[]{:S(2)}, u32[]{:S(2)}) %collective-permute-start.67) | collective-permute-done | bytes 98336 | tf_op jit(solution)/shard_map/ppermute | solution.py:327
  219.5 0.8 fusion.15
  (167 shorter events, 27.5 us)
Async XLA Ops:
  2.7 8.3 %collective-permute-start.1 = (bf16[3,4,128]{2,1,0:T(4,128)(2,1)S(1)}, bf16[3,4,128]{2,1,0:T(4,128)(2,1)S(1)}, u32[]{:S(2)}, u32[]{:S(2)}) collective-permute-start(bf16[3,4,128]{2,1,0:T(4,128)(2,1)S(1)} %get-tuple-element.97), channel_id=1, source_target_pairs={{0,1},{1,2},{2,3},{3,4},{4,5},{5,6},{6,7},{8,9},{9,10},{10,11},{11... | collective-permute-start | bytes 9224 | tf_op jit(solution)/shard_map/ppermute | solution.py:82
  7.1 4.5 %collective-permute-start.2 = (bf16[3,4,128]{2,1,0:T(4,128)(2,1)S(1)}, bf16[3,4,128]{2,1,0:T(4,128)(2,1)S(1)}, u32[]{:S(2)}, u32[]{:S(2)}) collective-permute-start(bf16[3,4,128]{2,1,0:T(4,128)(2,1)S(1)} %get-tuple-element.98), channel_id=1, source_target_pairs={{1,0},{2,1},{3,2},{4,3},{5,4},{6,5},{7,6},{9,8},{10,9},{11,10},{12... | collective-permute-start | bytes 9224 | tf_op jit(solution)/shard_map/ppermute | solution.py:83
  8.4 35.4 %collective-permute-start = (bf16[2,192,3072]{2,1,0:T(8,128)(2,1)S(1)}, bf16[2,192,3072]{2,1,0:T(8,128)(2,1)}, u32[]{:S(2)}, u32[]{:S(2)}) collective-permute-start(bf16[2,192,3072]{2,1,0:T(8,128)(2,1)S(1)} %select_bitcast_fusion.1.own), channel_id=1, source_target_pairs={{0,4},{1,5},{2,6},{3,7},{4,0},{5,1},{6,2},{7,3},{8,9},{9,8},{10,11... | collective-permute-start | bytes 7077896 | tf_op jit(solution)/shard_map/ppermute | solution.py:298
  13.5 25.0 %collective-permute-start.3 = (f32[192,128]{1,0:T(8,128)S(1)}, f32[192,128]{1,0:T(8,128)S(1)}, u32[]{:S(2)}, u32[]{:S(2)}) collective-permute-start(f32[192,128]{1,0:T(8,128)S(1)} %get-tuple-element.88), channel_id=1, source_target_pairs={{0,4},{1,5},{2,6},{3,7},{4,0},{5,1},{6,2},{7,3},{8,9},{9,8},{10,11... | collective-permute-start | bytes 294920 | tf_op jit(solution)/shard_map/ppermute | solution.py:309
  38.5 9.4 %collective-permute-start.5 = (bf16[384,128]{1,0:T(8,128)(2,1)S(1)}, bf16[384,128]{1,0:T(8,128)(2,1)S(1)}, u32[]{:S(2)}, u32[]{:S(2)}) collective-permute-start(bf16[384,128]{1,0:T(8,128)(2,1)S(1)} %get-tuple-element.72.sent), channel_id=1, source_target_pairs={{0,14},{1,10},{2,12},{3,8},{4,15},{5,11},{6,13},{7,9},{120,115},{1... | collective-permute-start | bytes 294920 | tf_op jit(solution)/shard_map/ppermute | solution.py:320
  39.8 10.3 %collective-permute-start.6 = (bf16[384,128]{1,0:T(8,128)(2,1)S(1)}, bf16[384,128]{1,0:T(8,128)(2,1)S(1)}, u32[]{:S(2)}, u32[]{:S(2)}) collective-permute-start(bf16[384,128]{1,0:T(8,128)(2,1)S(1)} %get-tuple-element.72.sent), channel_id=1, source_target_pairs={{0,10},{1,14},{2,8},{3,12},{4,11},{5,15},{6,9},{7,13},{120,114},{1... | collective-permute-start | bytes 294920 | tf_op jit(solution)/shard_map/ppermute | solution.py:320
  41.1 10.0 %collective-permute-start.4 = (bf16[384,128]{1,0:T(8,128)(2,1)S(1)}, bf16[384,128]{1,0:T(8,128)(2,1)S(1)}, u32[]{:S(2)}, u32[]{:S(2)}) collective-permute-start(bf16[384,128]{1,0:T(8,128)(2,1)S(1)} %get-tuple-element.72.sent), channel_id=1, source_target_pairs={{0,8},{1,12},{2,10},{3,14},{4,9},{5,13},{6,11},{7,15},{120,112},{1... | collective-permute-start | bytes 294920 | tf_op jit(solution)/shard_map/ppermute | solution.py:320
  42.4 9.5 %collective-permute-start.7 = (bf16[384,128]{1,0:T(8,128)(2,1)S(1)}, bf16[384,128]{1,0:T(8,128)(2,1)S(1)}, u32[]{:S(2)}, u32[]{:S(2)}) collective-permute-start(bf16[384,128]{1,0:T(8,128)(2,1)S(1)} %get-tuple-element.72.sent), channel_id=1, source_target_pairs={{0,12},{1,8},{2,14},{3,10},{4,13},{5,9},{6,15},{7,11},{120,113},{1... | collective-permute-start | bytes 294920 | tf_op jit(solution)/shard_map/ppermute | solution.py:320
  52.8 5.2 %collective-permute-start.10 = (bf16[384,128]{1,0:T(8,128)(2,1)S(1)}, bf16[384,128]{1,0:T(8,128)(2,1)S(1)}, u32[]{:S(2)}, u32[]{:S(2)}) collective-permute-start(bf16[384,128]{1,0:T(8,128)(2,1)S(1)} %get-tuple-element.41.sent), channel_id=1, source_target_pairs={{8,18},{9,22},{10,16},{11,20},{12,19},{13,23},{14,17},{15,21},{112... | collective-permute-start | bytes 294920 | tf_op jit(solution)/shard_map/ppermute | solution.py:320
  54.1 3.9 %collective-permute-start.9 = (bf16[384,128]{1,0:T(8,128)(2,1)S(1)}, bf16[384,128]{1,0:T(8,128)(2,1)S(1)}, u32[]{:S(2)}, u32[]{:S(2)}) collective-permute-start(bf16[384,128]{1,0:T(8,128)(2,1)S(1)} %get-tuple-element.41.sent), channel_id=1, source_target_pairs={{8,19},{9,23},{10,17},{11,21},{12,18},{13,22},{14,16},{15,20},{112... | collective-permute-start | bytes 294920 | tf_op jit(solution)/shard_map/ppermute | solution.py:320
  55.4 2.9 %collective-permute-start.8 = (bf16[384,128]{1,0:T(8,128)(2,1)S(1)}, bf16[384,128]{1,0:T(8,128)(2,1)S(1)}, u32[]{:S(2)}, u32[]{:S(2)}) collective-permute-start(bf16[384,128]{1,0:T(8,128)(2,1)S(1)} %get-tuple-element.41.sent), channel_id=1, source_target_pairs={{8,16},{9,20},{10,18},{11,22},{12,17},{13,21},{14,19},{15,23},{112... | collective-permute-start | bytes 294920 | tf_op jit(solution)/shard_map/ppermute | solution.py:320
  56.7 2.9 %collective-permute-start.11 = (bf16[384,128]{1,0:T(8,128)(2,1)S(1)}, bf16[384,128]{1,0:T(8,128)(2,1)S(1)}, u32[]{:S(2)}, u32[]{:S(2)}) collective-permute-start(bf16[384,128]{1,0:T(8,128)(2,1)S(1)} %get-tuple-element.41.sent), channel_id=1, source_target_pairs={{8,17},{9,21},{10,19},{11,23},{12,16},{13,20},{14,18},{15,22},{112... | collective-permute-start | bytes 294920 | tf_op jit(solution)/shard_map/ppermute | solution.py:320
  59.6 2.7 %collective-permute-start.13 = (bf16[384,128]{1,0:T(8,128)(2,1)S(1)}, bf16[384,128]{1,0:T(8,128)(2,1)S(1)}, u32[]{:S(2)}, u32[]{:S(2)}) collective-permute-start(bf16[384,128]{1,0:T(8,128)(2,1)S(1)} %get-tuple-element.43.sent), channel_id=1, source_target_pairs={{16,30},{17,26},{18,28},{19,24},{20,31},{21,27},{22,29},{23,25},{1... | collective-permute-start | bytes 294920 | tf_op jit(solution)/shard_map/ppermute | solution.py:320
  60.3 2.0 collective-permute-start.14
  61.0 1.4 collective-permute-start.12
  61.6 0.8 collective-permute-start.15
  62.5 2.7 %collective-permute-start.17 = (bf16[384,128]{1,0:T(8,128)(2,1)S(1)}, bf16[384,128]{1,0:T(8,128)(2,1)S(1)}, u32[]{:S(2)}, u32[]{:S(2)}) collective-permute-start(bf16[384,128]{1,0:T(8,128)(2,1)S(1)} %get-tuple-element.45.sent), channel_id=1, source_target_pairs={{24,35},{25,39},{26,33},{27,37},{28,34},{29,38},{30,32},{31,36},{9... | collective-permute-start | bytes 294920 | tf_op jit(solution)/shard_map/ppermute | solution.py:320
  63.1 2.0 collective-permute-start.18
  63.8 1.4 collective-permute-start.16
  65.3 7.1 %collective-permute-start.21 = (bf16[384,128]{1,0:T(8,128)(2,1)S(1)}, bf16[384,128]{1,0:T(8,128)(2,1)S(1)}, u32[]{:S(2)}, u32[]{:S(2)}) collective-permute-start(bf16[384,128]{1,0:T(8,128)(2,1)S(1)} %get-tuple-element.47.sent), channel_id=1, source_target_pairs={{0,14},{1,10},{2,12},{3,8},{4,15},{5,11},{6,13},{7,9},{120,115},{1... | collective-permute-start | bytes 294920 | tf_op jit(solution)/shard_map/ppermute | solution.py:320
  66.6 8.1 %collective-permute-start.22 = (bf16[384,128]{1,0:T(8,128)(2,1)S(1)}, bf16[384,128]{1,0:T(8,128)(2,1)S(1)}, u32[]{:S(2)}, u32[]{:S(2)}) collective-permute-start(bf16[384,128]{1,0:T(8,128)(2,1)S(1)} %get-tuple-element.47.sent), channel_id=1, source_target_pairs={{0,10},{1,14},{2,8},{3,12},{4,11},{5,15},{6,9},{7,13},{120,114},{1... | collective-permute-start | bytes 294920 | tf_op jit(solution)/shard_map/ppermute | solution.py:320
  67.9 6.9 %collective-permute-start.20 = (bf16[384,128]{1,0:T(8,128)(2,1)S(1)}, bf16[384,128]{1,0:T(8,128)(2,1)S(1)}, u32[]{:S(2)}, u32[]{:S(2)}) collective-permute-start(bf16[384,128]{1,0:T(8,128)(2,1)S(1)} %get-tuple-element.47.sent), channel_id=1, source_target_pairs={{0,8},{1,12},{2,10},{3,14},{4,9},{5,13},{6,11},{7,15},{120,112},{1... | collective-permute-start | bytes 294920 | tf_op jit(solution)/shard_map/ppermute | solution.py:320
  69.2 6.6 %collective-permute-start.23 = (bf16[384,128]{1,0:T(8,128)(2,1)S(1)}, bf16[384,128]{1,0:T(8,128)(2,1)S(1)}, u32[]{:S(2)}, u32[]{:S(2)}) collective-permute-start(bf16[384,128]{1,0:T(8,128)(2,1)S(1)} %get-tuple-element.47.sent), channel_id=1, source_target_pairs={{0,12},{1,8},{2,14},{3,10},{4,13},{5,9},{6,15},{7,11},{120,113},{1... | collective-permute-start | bytes 294920 | tf_op jit(solution)/shard_map/ppermute | solution.py:320
  78.5 28.1 %collective-permute-start.33 = (bf16[2,192,3072]{2,1,0:T(8,128)(2,1)S(1)}, bf16[2,192,3072]{2,1,0:T(8,128)(2,1)S(1)}, u32[]{:S(2)}, u32[]{:S(2)}) collective-permute-start(bf16[2,192,3072]{2,1,0:T(8,128)(2,1)S(1)} %select_bitcast_fusion.own), channel_id=1, source_target_pairs={{0,4},{1,5},{2,6},{3,7},{4,0},{5,1},{6,2},{7,3},{8,9},{9,8},{10,11... | collective-permute-start | bytes 7077896 | tf_op jit(solution)/shard_map/ppermute | solution.py:339
  79.5 8.4 %collective-permute-start.25 = (bf16[384,128]{1,0:T(8,128)(2,1)S(1)}, bf16[384,128]{1,0:T(8,128)(2,1)S(1)}, u32[]{:S(2)}, u32[]{:S(2)}) collective-permute-start(bf16[384,128]{1,0:T(8,128)(2,1)S(1)} %get-tuple-element.50.sent), channel_id=1, source_target_pairs={{8,19},{9,23},{10,17},{11,21},{12,18},{13,22},{14,16},{15,20},{112... | collective-permute-start | bytes 294920 | tf_op jit(solution)/shard_map/ppermute | solution.py:320
  83.3 4.6 %collective-permute-start.26 = (bf16[384,128]{1,0:T(8,128)(2,1)S(1)}, bf16[384,128]{1,0:T(8,128)(2,1)S(1)}, u32[]{:S(2)}, u32[]{:S(2)}) collective-permute-start(bf16[384,128]{1,0:T(8,128)(2,1)S(1)} %get-tuple-element.50.sent), channel_id=1, source_target_pairs={{8,18},{9,22},{10,16},{11,20},{12,19},{13,23},{14,17},{15,21},{112... | collective-permute-start | bytes 294920 | tf_op jit(solution)/shard_map/ppermute | solution.py:320
  85.3 2.9 %collective-permute-start.24 = (bf16[384,128]{1,0:T(8,128)(2,1)S(1)}, bf16[384,128]{1,0:T(8,128)(2,1)S(1)}, u32[]{:S(2)}, u32[]{:S(2)}) collective-permute-start(bf16[384,128]{1,0:T(8,128)(2,1)S(1)} %get-tuple-element.50.sent), channel_id=1, source_target_pairs={{8,16},{9,20},{10,18},{11,22},{12,17},{13,21},{14,19},{15,23},{112... | collective-permute-start | bytes 294920 | tf_op jit(solution)/shard_map/ppermute | solution.py:320
  86.6 2.9 %collective-permute-start.27 = (bf16[384,128]{1,0:T(8,128)(2,1)S(1)}, bf16[384,128]{1,0:T(8,128)(2,1)S(1)}, u32[]{:S(2)}, u32[]{:S(2)}) collective-permute-start(bf16[384,128]{1,0:T(8,128)(2,1)S(1)} %get-tuple-element.50.sent), channel_id=1, source_target_pairs={{8,17},{9,21},{10,19},{11,23},{12,16},{13,20},{14,18},{15,22},{112... | collective-permute-start | bytes 294920 | tf_op jit(solution)/shard_map/ppermute | solution.py:320
  89.5 2.7 %collective-permute-start.29 = (bf16[384,128]{1,0:T(8,128)(2,1)S(1)}, bf16[384,128]{1,0:T(8,128)(2,1)S(1)}, u32[]{:S(2)}, u32[]{:S(2)}) collective-permute-start(bf16[384,128]{1,0:T(8,128)(2,1)S(1)} %get-tuple-element.52.sent), channel_id=1, source_target_pairs={{16,30},{17,26},{18,28},{19,24},{20,31},{21,27},{22,29},{23,25},{1... | collective-permute-start | bytes 294920 | tf_op jit(solution)/shard_map/ppermute | solution.py:320
  90.2 2.0 collective-permute-start.30
  90.9 1.4 collective-permute-start.28
  91.5 0.9 collective-permute-start.31
  93.2 15.9 %collective-permute-start.36 = (bf16[384,128]{1,0:T(8,128)(2,1)S(1)}, bf16[384,128]{1,0:T(8,128)(2,1)S(1)}, u32[]{:S(2)}, u32[]{:S(2)}) collective-permute-start(bf16[384,128]{1,0:T(8,128)(2,1)S(1)} %collective-permute-done.34), channel_id=1, source_target_pairs={{64,67},{65,71},{66,65},{67,69},{68,66},{69,70},{70,64},{71,68},{5... | collective-permute-start | bytes 294920 | tf_op jit(solution)/shard_map/ppermute | solution.py:318
  93.9 15.3 %collective-permute-start.37 = (bf16[384,128]{1,0:T(8,128)(2,1)S(1)}, bf16[384,128]{1,0:T(8,128)(2,1)S(1)}, u32[]{:S(2)}, u32[]{:S(2)}) collective-permute-start(bf16[384,128]{1,0:T(8,128)(2,1)S(1)} %collective-permute-done.34), channel_id=1, source_target_pairs={{64,66},{65,70},{66,64},{67,68},{68,67},{69,71},{70,65},{71,69},{5... | collective-permute-start | bytes 294920 | tf_op jit(solution)/shard_map/ppermute | solution.py:318
  94.6 14.6 %collective-permute-start.35 = (bf16[384,128]{1,0:T(8,128)(2,1)S(1)}, bf16[384,128]{1,0:T(8,128)(2,1)S(1)}, u32[]{:S(2)}, u32[]{:S(2)}) collective-permute-start(bf16[384,128]{1,0:T(8,128)(2,1)S(1)} %collective-permute-done.34), channel_id=1, source_target_pairs={{64,64},{65,68},{66,66},{67,70},{68,65},{69,69},{70,67},{71,71},{5... | collective-permute-start | bytes 294920 | tf_op jit(solution)/shard_map/ppermute | solution.py:318
  95.2 14.0 %collective-permute-start.38 = (bf16[384,128]{1,0:T(8,128)(2,1)S(1)}, bf16[384,128]{1,0:T(8,128)(2,1)S(1)}, u32[]{:S(2)}, u32[]{:S(2)}) collective-permute-start(bf16[384,128]{1,0:T(8,128)(2,1)S(1)} %collective-permute-done.34), channel_id=1, source_target_pairs={{64,65},{65,69},{66,67},{67,71},{68,64},{69,68},{70,66},{71,70},{5... | collective-permute-start | bytes 294920 | tf_op jit(solution)/shard_map/ppermute | solution.py:318
  109.3 2.7 %collective-permute-start.40 = (bf16[384,128]{1,0:T(8,128)(2,1)S(1)}, bf16[384,128]{1,0:T(8,128)(2,1)S(1)}, u32[]{:S(2)}, u32[]{:S(2)}) collective-permute-start(bf16[384,128]{1,0:T(8,128)(2,1)S(1)} %get-tuple-element.58.sent), channel_id=1, source_target_pairs={{24,35},{25,39},{26,33},{27,37},{28,34},{29,38},{30,32},{31,36},{9... | collective-permute-start | bytes 294920 | tf_op jit(solution)/shard_map/ppermute | solution.py:320
  110.0 2.0 collective-permute-start.41
  110.7 1.4 collective-permute-start.39
  112.1 2.7 %collective-permute-start.44 = (bf16[384,128]{1,0:T(8,128)(2,1)S(1)}, bf16[384,128]{1,0:T(8,128)(2,1)S(1)}, u32[]{:S(2)}, u32[]{:S(2)}) collective-permute-start(bf16[384,128]{1,0:T(8,128)(2,1)S(1)} %get-tuple-element.60.sent), channel_id=1, source_target_pairs={{72,83},{73,87},{74,81},{75,85},{76,82},{77,86},{78,80},{79,84},{4... | collective-permute-start | bytes 294920 | tf_op jit(solution)/shard_map/ppermute | solution.py:320
  112.8 2.0 collective-permute-start.45
  113.5 1.4 collective-permute-start.43
  115.0 31.8 %collective-permute-start.48 = (bf16[384,128]{1,0:T(8,128)(2,1)S(1)}, bf16[384,128]{1,0:T(8,128)(2,1)S(1)}, u32[]{:S(2)}, u32[]{:S(2)}) collective-permute-start(bf16[384,128]{1,0:T(8,128)(2,1)S(1)} %get-tuple-element.62.sent), channel_id=1, source_target_pairs={{80,94},{81,90},{82,92},{83,88},{84,95},{85,91},{86,93},{87,89},{4... | collective-permute-start | bytes 294920 | tf_op jit(solution)/shard_map/ppermute | solution.py:320
  116.3 32.1 %collective-permute-start.49 = (bf16[384,128]{1,0:T(8,128)(2,1)S(1)}, bf16[384,128]{1,0:T(8,128)(2,1)S(1)}, u32[]{:S(2)}, u32[]{:S(2)}) collective-permute-start(bf16[384,128]{1,0:T(8,128)(2,1)S(1)} %get-tuple-element.62.sent), channel_id=1, source_target_pairs={{80,90},{81,94},{82,88},{83,92},{84,91},{85,95},{86,89},{87,93},{4... | collective-permute-start | bytes 294920 | tf_op jit(solution)/shard_map/ppermute | solution.py:320
  117.6 30.9 %collective-permute-start.47 = (bf16[384,128]{1,0:T(8,128)(2,1)S(1)}, bf16[384,128]{1,0:T(8,128)(2,1)S(1)}, u32[]{:S(2)}, u32[]{:S(2)}) collective-permute-start(bf16[384,128]{1,0:T(8,128)(2,1)S(1)} %get-tuple-element.62.sent), channel_id=1, source_target_pairs={{80,88},{81,92},{82,90},{83,94},{84,89},{85,93},{86,91},{87,95},{4... | collective-permute-start | bytes 294920 | tf_op jit(solution)/shard_map/ppermute | solution.py:320
  118.9 31.6 %collective-permute-start.50 = (bf16[384,128]{1,0:T(8,128)(2,1)S(1)}, bf16[384,128]{1,0:T(8,128)(2,1)S(1)}, u32[]{:S(2)}, u32[]{:S(2)}) collective-permute-start(bf16[384,128]{1,0:T(8,128)(2,1)S(1)} %get-tuple-element.62.sent), channel_id=1, source_target_pairs={{80,92},{81,88},{82,94},{83,90},{84,93},{85,89},{86,95},{87,91},{4... | collective-permute-start | bytes 294920 | tf_op jit(solution)/shard_map/ppermute | solution.py:320
  150.5 5.3 %collective-permute-start.52 = (bf16[384,128]{1,0:T(8,128)(2,1)S(1)}, bf16[384,128]{1,0:T(8,128)(2,1)S(1)}, u32[]{:S(2)}, u32[]{:S(2)}) collective-permute-start(bf16[384,128]{1,0:T(8,128)(2,1)S(1)} %get-tuple-element.64.sent), channel_id=1, source_target_pairs={{88,99},{89,103},{90,97},{91,101},{92,98},{93,102},{94,96},{95,100... | collective-permute-start | bytes 294920 | tf_op jit(solution)/shard_map/ppermute | solution.py:320
  151.8 4.0 %collective-permute-start.53 = (bf16[384,128]{1,0:T(8,128)(2,1)S(1)}, bf16[384,128]{1,0:T(8,128)(2,1)S(1)}, u32[]{:S(2)}, u32[]{:S(2)}) collective-permute-start(bf16[384,128]{1,0:T(8,128)(2,1)S(1)} %get-tuple-element.64.sent), channel_id=1, source_target_pairs={{88,98},{89,102},{90,96},{91,100},{92,99},{93,103},{94,97},{95,101... | collective-permute-start | bytes 294920 | tf_op jit(solution)/shard_map/ppermute | solution.py:320
  153.1 2.8 %collective-permute-start.51 = (bf16[384,128]{1,0:T(8,128)(2,1)S(1)}, bf16[384,128]{1,0:T(8,128)(2,1)S(1)}, u32[]{:S(2)}, u32[]{:S(2)}) collective-permute-start(bf16[384,128]{1,0:T(8,128)(2,1)S(1)} %get-tuple-element.64.sent), channel_id=1, source_target_pairs={{88,96},{89,100},{90,98},{91,102},{92,97},{93,101},{94,99},{95,103... | collective-permute-start | bytes 294920 | tf_op jit(solution)/shard_map/ppermute | solution.py:320
  154.4 2.9 %collective-permute-start.54 = (bf16[384,128]{1,0:T(8,128)(2,1)S(1)}, bf16[384,128]{1,0:T(8,128)(2,1)S(1)}, u32[]{:S(2)}, u32[]{:S(2)}) collective-permute-start(bf16[384,128]{1,0:T(8,128)(2,1)S(1)} %get-tuple-element.64.sent), channel_id=1, source_target_pairs={{88,97},{89,101},{90,99},{91,103},{92,96},{93,100},{94,98},{95,102... | collective-permute-start | bytes 294920 | tf_op jit(solution)/shard_map/ppermute | solution.py:320
  155.7 4.3 %collective-permute-start.32 = (f32[192,128]{1,0:T(8,128)S(1)}, f32[192,128]{1,0:T(8,128)S(1)}, u32[]{:S(2)}, u32[]{:S(2)}) collective-permute-start(f32[192,128]{1,0:T(8,128)S(1)} %slice_select_fusion.3), channel_id=1, source_target_pairs={{0,4},{1,5},{2,6},{3,7},{4,0},{5,1},{6,2},{7,3},{8,9},{9,8},{10,11... | collective-permute-start | bytes 294920 | tf_op jit(solution)/shard_map/ppermute | solution.py:327
  157.3 2.7 %collective-permute-start.56 = (bf16[384,128]{1,0:T(8,128)(2,1)S(1)}, bf16[384,128]{1,0:T(8,128)(2,1)S(1)}, u32[]{:S(2)}, u32[]{:S(2)}) collective-permute-start(bf16[384,128]{1,0:T(8,128)(2,1)S(1)} %get-tuple-element.66.sent), channel_id=1, source_target_pairs={{72,83},{73,87},{74,81},{75,85},{76,82},{77,86},{78,80},{79,84},{4... | collective-permute-start | bytes 294920 | tf_op jit(solution)/shard_map/ppermute | solution.py:320
  158.0 2.1 collective-permute-start.57
  158.7 1.4 collective-permute-start.55
  159.3 0.8 collective-permute-start.58
  160.2 43.3 %collective-permute-start.60 = (bf16[384,128]{1,0:T(8,128)(2,1)S(1)}, bf16[384,128]{1,0:T(8,128)(2,1)S(1)}, u32[]{:S(2)}, u32[]{:S(2)}) collective-permute-start(bf16[384,128]{1,0:T(8,128)(2,1)S(1)} %get-tuple-element.68.sent), channel_id=1, source_target_pairs={{80,94},{81,90},{82,92},{83,88},{84,95},{85,91},{86,93},{87,89},{4... | collective-permute-start | bytes 294920 | tf_op jit(solution)/shard_map/ppermute | solution.py:320
  161.5 43.3 %collective-permute-start.61 = (bf16[384,128]{1,0:T(8,128)(2,1)S(1)}, bf16[384,128]{1,0:T(8,128)(2,1)S(1)}, u32[]{:S(2)}, u32[]{:S(2)}) collective-permute-start(bf16[384,128]{1,0:T(8,128)(2,1)S(1)} %get-tuple-element.68.sent), channel_id=1, source_target_pairs={{80,90},{81,94},{82,88},{83,92},{84,91},{85,95},{86,89},{87,93},{4... | collective-permute-start | bytes 294920 | tf_op jit(solution)/shard_map/ppermute | solution.py:320
  162.8 43.1 %collective-permute-start.59 = (bf16[384,128]{1,0:T(8,128)(2,1)S(1)}, bf16[384,128]{1,0:T(8,128)(2,1)S(1)}, u32[]{:S(2)}, u32[]{:S(2)}) collective-permute-start(bf16[384,128]{1,0:T(8,128)(2,1)S(1)} %get-tuple-element.68.sent), channel_id=1, source_target_pairs={{80,88},{81,92},{82,90},{83,94},{84,89},{85,93},{86,91},{87,95},{4... | collective-permute-start | bytes 294920 | tf_op jit(solution)/shard_map/ppermute | solution.py:320
  164.1 42.6 %collective-permute-start.62 = (bf16[384,128]{1,0:T(8,128)(2,1)S(1)}, bf16[384,128]{1,0:T(8,128)(2,1)S(1)}, u32[]{:S(2)}, u32[]{:S(2)}) collective-permute-start(bf16[384,128]{1,0:T(8,128)(2,1)S(1)} %get-tuple-element.68.sent), channel_id=1, source_target_pairs={{80,92},{81,88},{82,94},{83,90},{84,93},{85,89},{86,95},{87,91},{4... | collective-permute-start | bytes 294920 | tf_op jit(solution)/shard_map/ppermute | solution.py:320
  207.6 5.3 %collective-permute-start.64 = (bf16[384,128]{1,0:T(8,128)(2,1)S(1)}, bf16[384,128]{1,0:T(8,128)(2,1)S(1)}, u32[]{:S(2)}, u32[]{:S(2)}) collective-permute-start(bf16[384,128]{1,0:T(8,128)(2,1)S(1)} %get-tuple-element.70.sent), channel_id=1, source_target_pairs={{88,99},{89,103},{90,97},{91,101},{92,98},{93,102},{94,96},{95,100... | collective-permute-start | bytes 294920 | tf_op jit(solution)/shard_map/ppermute | solution.py:320
  208.9 4.0 %collective-permute-start.65 = (bf16[384,128]{1,0:T(8,128)(2,1)S(1)}, bf16[384,128]{1,0:T(8,128)(2,1)S(1)}, u32[]{:S(2)}, u32[]{:S(2)}) collective-permute-start(bf16[384,128]{1,0:T(8,128)(2,1)S(1)} %get-tuple-element.70.sent), channel_id=1, source_target_pairs={{88,98},{89,102},{90,96},{91,100},{92,99},{93,103},{94,97},{95,101... | collective-permute-start | bytes 294920 | tf_op jit(solution)/shard_map/ppermute | solution.py:320
  210.2 2.8 %collective-permute-start.63 = (bf16[384,128]{1,0:T(8,128)(2,1)S(1)}, bf16[384,128]{1,0:T(8,128)(2,1)S(1)}, u32[]{:S(2)}, u32[]{:S(2)}) collective-permute-start(bf16[384,128]{1,0:T(8,128)(2,1)S(1)} %get-tuple-element.70.sent), channel_id=1, source_target_pairs={{88,96},{89,100},{90,98},{91,102},{92,97},{93,101},{94,99},{95,103... | collective-permute-start | bytes 294920 | tf_op jit(solution)/shard_map/ppermute | solution.py:320
  211.5 3.5 %collective-permute-start.66 = (bf16[384,128]{1,0:T(8,128)(2,1)S(1)}, bf16[384,128]{1,0:T(8,128)(2,1)S(1)}, u32[]{:S(2)}, u32[]{:S(2)}) collective-permute-start(bf16[384,128]{1,0:T(8,128)(2,1)S(1)} %get-tuple-element.70.sent), channel_id=1, source_target_pairs={{88,97},{89,101},{90,99},{91,103},{92,96},{93,100},{94,98},{95,102... | collective-permute-start | bytes 294920 | tf_op jit(solution)/shard_map/ppermute | solution.py:320
  215.6 3.5 %collective-permute-start.67 = (f32[192,128]{1,0:T(8,128)S(1)}, f32[192,128]{1,0:T(8,128)S(1)}, u32[]{:S(2)}, u32[]{:S(2)}) collective-permute-start(f32[192,128]{1,0:T(8,128)S(1)} %slice_select_fusion.1), channel_id=1, source_target_pairs={{0,4},{1,5},{2,6},{3,7},{4,0},{5,1},{6,2},{7,3},{8,9},{9,8},{10,11... | collective-permute-start | bytes 294920 | tf_op jit(solution)/shard_map/ppermute | solution.py:327
  (8 other events, 11.0 us)
where the time goes:
time: 224 us; the launch traced here: 220 us
  waiting for transfers between devices  111 us (50%)
  starting transfers between devices  85 us (38%)
  Pallas kernels  13.7 us (6%)
  other arithmetic  5.42 us (2%)
  local copies, waits for them, and re-layouts  3.4 us (2%)
    ppermute x56, waiting for transfers between devices, advance(): pieces = [lax.ppermute(sent, BOTH, routes(step, r)) for r in range(FAN)]  83.7 us
    ppermute x56, starting transfers between devices, advance(): pieces = [lax.ppermute(sent, BOTH, routes(step, r)) for r in range(FAN)]  60.6 us
    ppermute x1, waiting for transfers between devices, local(): swapped = lax.ppermute(give, BOTH, PAIRS)  12.9 us
    ppermute x1, starting transfers between devices, local(): swapped = lax.ppermute(give, BOTH, PAIRS)  11.3 us
    ppermute x1, waiting for transfers between devices, local(): other_second = lax.ppermute(own_second, BOTH, PAIRS)  10.6 us
    pallas_call x2, Pallas kernels, loaded(): pl.pallas_call(load_kernel, out_shape=jax.ShapeDtypeStruct((FAN, 4 * slab...  6.76 us
  transfers between devices with their start and end apart: 68, of which 20 were waited for; matrix products, arithmetic and copies ran while one was open for 1% of the time, Pallas kernels for 5%

commit v1 on v0

--- a/solution.py
+++ b/solution.py
@@ -14,7 +14,7 @@
 LATS = 8
 HALF = LAYERS // 2
 BOTH = ("layer", "lat")
-SHARED = ((1, 5), (2, 6), (3, 7), (4, 9), (10, 13), (11, 14), (12, 15))
+SHARED = ((1, 5), (2, 6), (3, 7, 11), (4, 9, 14), (10, 13), (12, 15))
 FAN = 4
 SWAP = 6
 BATCHES = ((3, 1), (0,), (2,))
@@ -61,6 +61,9 @@
 
 
 PAIRS = [(l * LATS + j, l * LATS + partner_of(l, j)) for l in range(LAYERS) for j in range(LATS)]
+
+
+INNER_PAIRS = [pair for pair in PAIRS if 0 < pair[0] // LATS < LAYERS - 1]
 
 
 def rank_table():
@@ -295,7 +298,7 @@
 
     own_first = jnp.where(low, green_down[0], green_up[0])
     own_first, source, wavenumber = lax.optimization_barrier((own_first, source, wavenumber))
-    other_first = lax.ppermute(own_first, BOTH, PAIRS)
+    other_first = lax.ppermute(own_first, BOTH, INNER_PAIRS)
 
     traces = relaxed(source[0], wavenumber[0])
     half = traces.shape[2] // 2
@@ -337,8 +340,10 @@
             down_later, up_later, sent = lax.optimization_barrier((green_down, green_up, sent))
             own_second = jnp.where(low, up_later[0], down_later[0])
             other_second = lax.ppermute(own_second, BOTH, PAIRS)
+        if step == HALF - 1:
+            green_second = loaded(info, own_second, other_second)
+            green_first, green_second = lax.optimization_barrier((green_first, green_second))
         first, sent = advance(step, green_first, first, sent)
-    green_second = loaded(info, own_second, other_second)
     near = joined(first)
     second = trace
     for step in range(HALF, LAYERS):

time: 224 us -> 234 us (1.045)
  the two profiles are of different devices: /device:TPU:1 before, /device:TPU:31 now
where the time goes in v1:
time: 234 us; the launch traced here: 233 us
  starting transfers between devices  107 us (46%)
  waiting for transfers between devices  103 us (44%)
  Pallas kernels  11.2 us (5%)
  other arithmetic  5.42 us (2%)
  local copies, waits for them, and re-layouts  3.41 us (1%)
    ppermute x56, starting transfers between devices, advance(): pieces = [lax.ppermute(sent, BOTH, routes(step, r)) for r in range(FAN)]  91 us
    ppermute x56, waiting for transfers between devices, advance(): pieces = [lax.ppermute(sent, BOTH, routes(step, r)) for r in range(FAN)]  71.2 us
    ppermute x1, waiting for transfers between devices, local(): other_second = lax.ppermute(own_second, BOTH, PAIRS)  21 us
    pallas_call x2, Pallas kernels, loaded(): pl.pallas_call(load_kernel, out_shape=jax.ShapeDtypeStruct((FAN, 4 * slab...  6.76 us
    ppermute x1, starting transfers between devices, padded_2(): lax.ppermute(lax.slice_in_dim(block, 0, width, axis=dim), axis, backward)  5.85 us
  transfers between devices with their start and end apart: 68, of which 11 were waited for; matrix products, arithmetic and copies ran while one was open for 1% of the time, Pallas kernels for 4%

profile of v1, /device:TPU:31, one launch (start us, length us, event | category | flops | bytes accessed | tf_op | source)
XLA Modules:
  0.0 232.8 jit_solution(13433934937718746826)
XLA Ops:
  0.7 2.0 select_bitcast_fusion.1.own
  2.6 2.0 collective-permute-start
  4.7 5.8 %collective-permute-start.2 = (bf16[3,4,128]{2,1,0:T(4,128)(2,1)S(1)}, bf16[3,4,128]{2,1,0:T(4,128)(2,1)S(1)}, u32[]{:S(2)}, u32[]{:S(2)}) collective-permute-start(bf16[3,4,128]{2,1,0:T(4,128)(2,1)S(1)} %get-tuple-element.102), channel_id=1, source_target_pairs={{1,0},{2,1},{3,2},{4,3},{5,4},{6,5},{7,6},{9,8},{10,9},{11,10},{12... | collective-permute-start | bytes 9224 | tf_op jit(solution)/shard_map/ppermute | solution.py:86
  10.6 1.9 collective-permute-start.1
  12.8 4.3 %collective-permute-done.1 = bf16[3,4,128]{2,1,0:T(4,128)(2,1)S(1)} collective-permute-done((bf16[3,4,128]{2,1,0:T(4,128)(2,1)S(1)}, bf16[3,4,128]{2,1,0:T(4,128)(2,1)S(1)}, u32[]{:S(2)}, u32[]{:S(2)}) %collective-permute-start.1) | collective-permute-done | bytes 3104 | tf_op jit(solution)/shard_map/ppermute | solution.py:85
  19.0 0.7 dynamic-slice_bitcast_fusion
  19.7 3.2 %collective-permute-done.3 = f32[192,128]{1,0:T(8,128)S(1)} collective-permute-done((f32[192,128]{1,0:T(8,128)S(1)}, f32[192,128]{1,0:T(8,128)S(1)}, u32[]{:S(2)}, u32[]{:S(2)}) %collective-permute-start.3) | collective-permute-done | bytes 98336 | tf_op jit(solution)/shard_map/ppermute | solution.py:312
  22.9 15.8 %collective-permute-start.4 = (bf16[384,128]{1,0:T(8,128)(2,1)S(1)}, bf16[384,128]{1,0:T(8,128)(2,1)S(1)}, u32[]{:S(2)}, u32[]{:S(2)}) collective-permute-start(bf16[384,128]{1,0:T(8,128)(2,1)S(1)} %get-tuple-element.76.sent), channel_id=1, source_target_pairs={{0,8},{1,12},{2,10},{3,14},{4,9},{5,13},{6,11},{7,15},{120,112},{1... | collective-permute-start | bytes 294920 | tf_op jit(solution)/shard_map/ppermute | solution.py:323
  38.8 3.3 %collective-permute-start.5 = (bf16[384,128]{1,0:T(8,128)(2,1)S(1)}, bf16[384,128]{1,0:T(8,128)(2,1)S(1)}, u32[]{:S(2)}, u32[]{:S(2)}) collective-permute-start(bf16[384,128]{1,0:T(8,128)(2,1)S(1)} %get-tuple-element.76.sent), channel_id=1, source_target_pairs={{0,14},{1,10},{2,12},{3,8},{4,15},{5,11},{6,13},{7,9},{120,115},{1... | collective-permute-start | bytes 294920 | tf_op jit(solution)/shard_map/ppermute | solution.py:323
  42.0 5.8 %collective-permute-start.6 = (bf16[384,128]{1,0:T(8,128)(2,1)S(1)}, bf16[384,128]{1,0:T(8,128)(2,1)S(1)}, u32[]{:S(2)}, u32[]{:S(2)}) collective-permute-start(bf16[384,128]{1,0:T(8,128)(2,1)S(1)} %get-tuple-element.76.sent), channel_id=1, source_target_pairs={{0,10},{1,14},{2,8},{3,12},{4,11},{5,15},{6,9},{7,13},{120,114},{1... | collective-permute-start | bytes 294920 | tf_op jit(solution)/shard_map/ppermute | solution.py:323
  47.9 1.8 collective-permute-start.7
  49.8 4.1 %shard_map.68.green = bf16[4,768,768]{2,1,0:T(8,128)(2,1)S(1)} custom-call(s32[6]{0:T(128)S(1)} %pad_add_fusion.info, bf16[2,192,3072]{2,1,0:T(8,128)(2,1)S(1)} %select_bitcast_fusion.1.own, bf16[2,192,3072]{2,1,0:T(8,128)(2,1)} %collective-permute-done.other), custom_call_target="tpu_custom_call" | custom-call | bytes 9437184 | tf_op jit(solution)/shard_map/pallas_call | solution.py:178
  54.0 0.7 collective-permute-start.9
  54.7 0.7 collective-permute-start.10
  55.4 0.7 collective-permute-start.8
  56.1 0.7 collective-permute-start.11
  56.9 0.7 collective-permute-start.13
  57.5 0.7 collective-permute-start.14
  58.2 0.7 collective-permute-start.12
  58.9 0.7 collective-permute-start.15
  59.7 0.7 collective-permute-start.17
  60.4 0.7 collective-permute-start.18
  61.1 0.7 collective-permute-start.16
  61.7 0.7 collective-permute-start.19
  62.5 23.4 %collective-permute-start.21 = (bf16[384,128]{1,0:T(8,128)(2,1)S(1)}, bf16[384,128]{1,0:T(8,128)(2,1)S(1)}, u32[]{:S(2)}, u32[]{:S(2)}) collective-permute-start(bf16[384,128]{1,0:T(8,128)(2,1)S(1)} %get-tuple-element.49.sent), channel_id=1, source_target_pairs={{0,14},{1,10},{2,12},{3,8},{4,15},{5,11},{6,13},{7,9},{120,115},{1... | collective-permute-start | bytes 294920 | tf_op jit(solution)/shard_map/ppermute | solution.py:323
  85.9 1.3 collective-permute-start.22
  87.3 1.3 collective-permute-start.20
  88.6 1.3 collective-permute-start.23
  90.2 1.3 collective-permute-done.23.refs_0_
  91.5 1.6 copy-done
  93.1 0.7 copy-done.1
  94.1 1.6 collective-permute-start.24
  96.4 0.7 collective-permute-start.27
  97.1 0.7 collective-permute-start.25
  97.7 0.7 collective-permute-start.28
  98.6 0.7 collective-permute-start.30
  99.2 0.7 collective-permute-start.31
  99.9 0.7 collective-permute-start.29
  100.6 0.7 collective-permute-start.32
  101.3 21.0 %collective-permute-done.24.other = bf16[2,192,3072]{2,1,0:T(8,128)(2,1)S(1)} collective-permute-done((bf16[2,192,3072]{2,1,0:T(8,128)(2,1)S(1)}, bf16[2,192,3072]{2,1,0:T(8,128)(2,1)S(1)}, u32[]{:S(2)}, u32[]{:S(2)}) %collective-permute-start.24) | collective-permute-done | bytes 2359328 | tf_op jit(solution)/shard_map/ppermute | solution.py:342
  122.3 2.6 %shard_map.84.green = bf16[4,768,768]{2,1,0:T(8,128)(2,1)S(1)} custom-call(s32[6]{0:T(128)S(1)} %pad_add_fusion.info, bf16[2,192,3072]{2,1,0:T(8,128)(2,1)S(1)} %select_bitcast_fusion.own, bf16[2,192,3072]{2,1,0:T(8,128)(2,1)S(1)} %collective-permute-done.24.other), custom_call_target="tpu_custom_call" | custom-call | bytes 9437184 | tf_op jit(solution)/shard_map/pallas_call | solution.py:178
  125.2 0.7 collective-permute-start.34
  125.9 0.7 collective-permute-start.36
  126.6 0.7 collective-permute-start.37
  135.1 0.7 collective-permute-start.49
  137.3 1.3 collective-permute-start.51
  138.6 1.3 collective-permute-start.52
  139.9 1.3 collective-permute-start.53
  141.2 1.3 collective-permute-start.54
  142.5 1.5 collective-permute-start.33
  144.0 10.5 %collective-permute-done.52.refs_0_ = bf16[384,128]{1,0:T(8,128)(2,1)S(1)} collective-permute-done((bf16[384,128]{1,0:T(8,128)(2,1)S(1)}, bf16[384,128]{1,0:T(8,128)(2,1)S(1)}, u32[]{:S(2)}, u32[]{:S(2)}) %collective-permute-start.52) | collective-permute-done | bytes 98336 | tf_op jit(solution)/shard_map/ppermute | solution.py:323
  154.5 1.1 collective-permute-done.53.refs_1_
  155.5 0.8 collective-permute-done.54.refs_0_
  162.1 1.3 collective-permute-start.63
  163.4 1.3 collective-permute-start.64
  164.7 1.3 collective-permute-start.65
  166.0 1.3 collective-permute-start.66
  167.4 56.1 %collective-permute-done.64.refs_0_ = bf16[384,128]{1,0:T(8,128)(2,1)S(1)} collective-permute-done((bf16[384,128]{1,0:T(8,128)(2,1)S(1)}, bf16[384,128]{1,0:T(8,128)(2,1)S(1)}, u32[]{:S(2)}, u32[]{:S(2)}) %collective-permute-start.64) | collective-permute-done | bytes 98336 | tf_op jit(solution)/shard_map/ppermute | solution.py:323
  223.5 1.2 collective-permute-done.65.refs_1_
  224.7 1.1 shard_map.112.refs_1_
  225.8 0.7 shard_map.113.earlier
  226.6 1.5 shard_map.114
  228.3 3.4 %collective-permute-done.67 = f32[192,128]{1,0:T(8,128)S(1)} collective-permute-done((f32[192,128]{1,0:T(8,128)S(1)}, f32[192,128]{1,0:T(8,128)S(1)}, u32[]{:S(2)}, u32[]{:S(2)}) %collective-permute-start.67) | collective-permute-done | bytes 98336 | tf_op jit(solution)/shard_map/ppermute | solution.py:330
  232.0 0.8 fusion.15
  (167 shorter events, 19.4 us)
Async XLA Ops:
  2.6 47.1 %collective-permute-start = (bf16[2,192,3072]{2,1,0:T(8,128)(2,1)S(1)}, bf16[2,192,3072]{2,1,0:T(8,128)(2,1)}, u32[]{:S(2)}, u32[]{:S(2)}) collective-permute-start(bf16[2,192,3072]{2,1,0:T(8,128)(2,1)S(1)} %select_bitcast_fusion.1.own), channel_id=1, source_target_pairs={{8,9},{9,8},{10,11},{11,10},{12,13},{13,12},{14,15},{15,14},{16,20... | collective-permute-start | bytes 7077896 | tf_op jit(solution)/shard_map/ppermute | solution.py:301
  4.7 8.0 %collective-permute-start.2 = (bf16[3,4,128]{2,1,0:T(4,128)(2,1)S(1)}, bf16[3,4,128]{2,1,0:T(4,128)(2,1)S(1)}, u32[]{:S(2)}, u32[]{:S(2)}) collective-permute-start(bf16[3,4,128]{2,1,0:T(4,128)(2,1)S(1)} %get-tuple-element.102), channel_id=1, source_target_pairs={{1,0},{2,1},{3,2},{4,3},{5,4},{6,5},{7,6},{9,8},{10,9},{11,10},{12... | collective-permute-start | bytes 9224 | tf_op jit(solution)/shard_map/ppermute | solution.py:86
  10.6 6.5 %collective-permute-start.1 = (bf16[3,4,128]{2,1,0:T(4,128)(2,1)S(1)}, bf16[3,4,128]{2,1,0:T(4,128)(2,1)S(1)}, u32[]{:S(2)}, u32[]{:S(2)}) collective-permute-start(bf16[3,4,128]{2,1,0:T(4,128)(2,1)S(1)} %get-tuple-element.101), channel_id=1, source_target_pairs={{0,1},{1,2},{2,3},{3,4},{4,5},{5,6},{6,7},{8,9},{9,10},{10,11},{11... | collective-permute-start | bytes 9224 | tf_op jit(solution)/shard_map/ppermute | solution.py:85
  19.0 3.9 %collective-permute-start.3 = (f32[192,128]{1,0:T(8,128)S(1)}, f32[192,128]{1,0:T(8,128)S(1)}, u32[]{:S(2)}, u32[]{:S(2)}) collective-permute-start(f32[192,128]{1,0:T(8,128)S(1)} %get-tuple-element.92), channel_id=1, source_target_pairs={{0,4},{1,5},{2,6},{3,7},{4,0},{5,1},{6,2},{7,3},{8,9},{9,8},{10,11... | collective-permute-start | bytes 294920 | tf_op jit(solution)/shard_map/ppermute | solution.py:312
  22.9 31.0 %collective-permute-start.4 = (bf16[384,128]{1,0:T(8,128)(2,1)S(1)}, bf16[384,128]{1,0:T(8,128)(2,1)S(1)}, u32[]{:S(2)}, u32[]{:S(2)}) collective-permute-start(bf16[384,128]{1,0:T(8,128)(2,1)S(1)} %get-tuple-element.76.sent), channel_id=1, source_target_pairs={{0,8},{1,12},{2,10},{3,14},{4,9},{5,13},{6,11},{7,15},{120,112},{1... | collective-permute-start | bytes 294920 | tf_op jit(solution)/shard_map/ppermute | solution.py:323
  38.8 15.1 %collective-permute-start.5 = (bf16[384,128]{1,0:T(8,128)(2,1)S(1)}, bf16[384,128]{1,0:T(8,128)(2,1)S(1)}, u32[]{:S(2)}, u32[]{:S(2)}) collective-permute-start(bf16[384,128]{1,0:T(8,128)(2,1)S(1)} %get-tuple-element.76.sent), channel_id=1, source_target_pairs={{0,14},{1,10},{2,12},{3,8},{4,15},{5,11},{6,13},{7,9},{120,115},{1... | collective-permute-start | bytes 294920 | tf_op jit(solution)/shard_map/ppermute | solution.py:323
  42.0 11.9 %collective-permute-start.6 = (bf16[384,128]{1,0:T(8,128)(2,1)S(1)}, bf16[384,128]{1,0:T(8,128)(2,1)S(1)}, u32[]{:S(2)}, u32[]{:S(2)}) collective-permute-start(bf16[384,128]{1,0:T(8,128)(2,1)S(1)} %get-tuple-element.76.sent), channel_id=1, source_target_pairs={{0,10},{1,14},{2,8},{3,12},{4,11},{5,15},{6,9},{7,13},{120,114},{1... | collective-permute-start | bytes 294920 | tf_op jit(solution)/shard_map/ppermute | solution.py:323
  47.9 6.1 %collective-permute-start.7 = (bf16[384,128]{1,0:T(8,128)(2,1)S(1)}, bf16[384,128]{1,0:T(8,128)(2,1)S(1)}, u32[]{:S(2)}, u32[]{:S(2)}) collective-permute-start(bf16[384,128]{1,0:T(8,128)(2,1)S(1)} %get-tuple-element.76.sent), channel_id=1, source_target_pairs={{0,12},{1,8},{2,14},{3,10},{4,13},{5,9},{6,15},{7,11},{120,113},{1... | collective-permute-start | bytes 294920 | tf_op jit(solution)/shard_map/ppermute | solution.py:323
  54.0 2.7 %collective-permute-start.9 = (bf16[384,128]{1,0:T(8,128)(2,1)S(1)}, bf16[384,128]{1,0:T(8,128)(2,1)S(1)}, u32[]{:S(2)}, u32[]{:S(2)}) collective-permute-start(bf16[384,128]{1,0:T(8,128)(2,1)S(1)} %get-tuple-element.43.sent), channel_id=1, source_target_pairs={{8,19},{9,23},{10,17},{11,21},{12,18},{13,22},{14,16},{15,20},{112... | collective-permute-start | bytes 294920 | tf_op jit(solution)/shard_map/ppermute | solution.py:323
  54.7 2.0 collective-permute-start.10
  55.4 1.4 collective-permute-start.8
  56.1 0.8 collective-permute-start.11
  56.9 2.7 %collective-permute-start.13 = (bf16[384,128]{1,0:T(8,128)(2,1)S(1)}, bf16[384,128]{1,0:T(8,128)(2,1)S(1)}, u32[]{:S(2)}, u32[]{:S(2)}) collective-permute-start(bf16[384,128]{1,0:T(8,128)(2,1)S(1)} %get-tuple-element.45.sent), channel_id=1, source_target_pairs={{16,30},{17,26},{18,28},{19,24},{20,31},{21,27},{22,29},{23,25},{1... | collective-permute-start | bytes 294920 | tf_op jit(solution)/shard_map/ppermute | solution.py:323
  57.5 2.0 collective-permute-start.14
  58.2 1.4 collective-permute-start.12
  58.9 0.8 collective-permute-start.15
  59.7 2.7 %collective-permute-start.17 = (bf16[384,128]{1,0:T(8,128)(2,1)S(1)}, bf16[384,128]{1,0:T(8,128)(2,1)S(1)}, u32[]{:S(2)}, u32[]{:S(2)}) collective-permute-start(bf16[384,128]{1,0:T(8,128)(2,1)S(1)} %get-tuple-element.47.sent), channel_id=1, source_target_pairs={{24,35},{25,39},{26,33},{27,37},{28,34},{29,38},{30,32},{31,36},{9... | collective-permute-start | bytes 294920 | tf_op jit(solution)/shard_map/ppermute | solution.py:323
  60.4 2.0 collective-permute-start.18
  61.1 1.4 collective-permute-start.16
  61.7 0.8 collective-permute-start.19
  62.5 27.3 %collective-permute-start.21 = (bf16[384,128]{1,0:T(8,128)(2,1)S(1)}, bf16[384,128]{1,0:T(8,128)(2,1)S(1)}, u32[]{:S(2)}, u32[]{:S(2)}) collective-permute-start(bf16[384,128]{1,0:T(8,128)(2,1)S(1)} %get-tuple-element.49.sent), channel_id=1, source_target_pairs={{0,14},{1,10},{2,12},{3,8},{4,15},{5,11},{6,13},{7,9},{120,115},{1... | collective-permute-start | bytes 294920 | tf_op jit(solution)/shard_map/ppermute | solution.py:323
  85.9 3.9 %collective-permute-start.22 = (bf16[384,128]{1,0:T(8,128)(2,1)S(1)}, bf16[384,128]{1,0:T(8,128)(2,1)S(1)}, u32[]{:S(2)}, u32[]{:S(2)}) collective-permute-start(bf16[384,128]{1,0:T(8,128)(2,1)S(1)} %get-tuple-element.49.sent), channel_id=1, source_target_pairs={{0,10},{1,14},{2,8},{3,12},{4,11},{5,15},{6,9},{7,13},{120,114},{1... | collective-permute-start | bytes 294920 | tf_op jit(solution)/shard_map/ppermute | solution.py:323
  87.3 2.9 %collective-permute-start.20 = (bf16[384,128]{1,0:T(8,128)(2,1)S(1)}, bf16[384,128]{1,0:T(8,128)(2,1)S(1)}, u32[]{:S(2)}, u32[]{:S(2)}) collective-permute-start(bf16[384,128]{1,0:T(8,128)(2,1)S(1)} %get-tuple-element.49.sent), channel_id=1, source_target_pairs={{0,8},{1,12},{2,10},{3,14},{4,9},{5,13},{6,11},{7,15},{120,112},{1... | collective-permute-start | bytes 294920 | tf_op jit(solution)/shard_map/ppermute | solution.py:323
  88.6 2.9 %collective-permute-start.23 = (bf16[384,128]{1,0:T(8,128)(2,1)S(1)}, bf16[384,128]{1,0:T(8,128)(2,1)S(1)}, u32[]{:S(2)}, u32[]{:S(2)}) collective-permute-start(bf16[384,128]{1,0:T(8,128)(2,1)S(1)} %get-tuple-element.49.sent), channel_id=1, source_target_pairs={{0,12},{1,8},{2,14},{3,10},{4,13},{5,9},{6,15},{7,11},{120,113},{1... | collective-permute-start | bytes 294920 | tf_op jit(solution)/shard_map/ppermute | solution.py:323
  94.1 28.2 %collective-permute-start.24 = (bf16[2,192,3072]{2,1,0:T(8,128)(2,1)S(1)}, bf16[2,192,3072]{2,1,0:T(8,128)(2,1)S(1)}, u32[]{:S(2)}, u32[]{:S(2)}) collective-permute-start(bf16[2,192,3072]{2,1,0:T(8,128)(2,1)S(1)} %select_bitcast_fusion.own), channel_id=1, source_target_pairs={{0,4},{1,5},{2,6},{3,7},{4,0},{5,1},{6,2},{7,3},{8,9},{9,8},{10,11... | collective-permute-start | bytes 7077896 | tf_op jit(solution)/shard_map/ppermute | solution.py:342
  95.7 2.7 %collective-permute-start.26 = (bf16[384,128]{1,0:T(8,128)(2,1)S(1)}, bf16[384,128]{1,0:T(8,128)(2,1)S(1)}, u32[]{:S(2)}, u32[]{:S(2)}) collective-permute-start(bf16[384,128]{1,0:T(8,128)(2,1)S(1)} %get-tuple-element.55.sent), channel_id=1, source_target_pairs={{8,19},{9,23},{10,17},{11,21},{12,18},{13,22},{14,16},{15,20},{112... | collective-permute-start | bytes 294920 | tf_op jit(solution)/shard_map/ppermute | solution.py:323
  96.4 2.0 collective-permute-start.27
  97.1 1.4 collective-permute-start.25
  97.7 0.8 collective-permute-start.28
  98.6 26.3 %collective-permute-start.30 = (bf16[384,128]{1,0:T(8,128)(2,1)S(1)}, bf16[384,128]{1,0:T(8,128)(2,1)S(1)}, u32[]{:S(2)}, u32[]{:S(2)}) collective-permute-start(bf16[384,128]{1,0:T(8,128)(2,1)S(1)} %get-tuple-element.57.sent), channel_id=1, source_target_pairs={{16,30},{17,26},{18,28},{19,24},{20,31},{21,27},{22,29},{23,25},{1... | collective-permute-start | bytes 294920 | tf_op jit(solution)/shard_map/ppermute | solution.py:323
  99.2 25.7 %collective-permute-start.31 = (bf16[384,128]{1,0:T(8,128)(2,1)S(1)}, bf16[384,128]{1,0:T(8,128)(2,1)S(1)}, u32[]{:S(2)}, u32[]{:S(2)}) collective-permute-start(bf16[384,128]{1,0:T(8,128)(2,1)S(1)} %get-tuple-element.57.sent), channel_id=1, source_target_pairs={{16,26},{17,30},{18,24},{19,28},{20,27},{21,31},{22,25},{23,29},{1... | collective-permute-start | bytes 294920 | tf_op jit(solution)/shard_map/ppermute | solution.py:323
  99.9 25.2 %collective-permute-start.29 = (bf16[384,128]{1,0:T(8,128)(2,1)S(1)}, bf16[384,128]{1,0:T(8,128)(2,1)S(1)}, u32[]{:S(2)}, u32[]{:S(2)}) collective-permute-start(bf16[384,128]{1,0:T(8,128)(2,1)S(1)} %get-tuple-element.57.sent), channel_id=1, source_target_pairs={{16,24},{17,28},{18,26},{19,30},{20,25},{21,29},{22,27},{23,31},{1... | collective-permute-start | bytes 294920 | tf_op jit(solution)/shard_map/ppermute | solution.py:323
  100.6 24.6 %collective-permute-start.32 = (bf16[384,128]{1,0:T(8,128)(2,1)S(1)}, bf16[384,128]{1,0:T(8,128)(2,1)S(1)}, u32[]{:S(2)}, u32[]{:S(2)}) collective-permute-start(bf16[384,128]{1,0:T(8,128)(2,1)S(1)} %get-tuple-element.57.sent), channel_id=1, source_target_pairs={{16,28},{17,24},{18,30},{19,26},{20,29},{21,25},{22,31},{23,27},{1... | collective-permute-start | bytes 294920 | tf_op jit(solution)/shard_map/ppermute | solution.py:323
  125.9 2.7 %collective-permute-start.36 = (bf16[384,128]{1,0:T(8,128)(2,1)S(1)}, bf16[384,128]{1,0:T(8,128)(2,1)S(1)}, u32[]{:S(2)}, u32[]{:S(2)}) collective-permute-start(bf16[384,128]{1,0:T(8,128)(2,1)S(1)} %collective-permute-done.34), channel_id=1, source_target_pairs={{64,67},{65,71},{66,65},{67,69},{68,66},{69,70},{70,64},{71,68},{5... | collective-permute-start | bytes 294920 | tf_op jit(solution)/shard_map/ppermute | solution.py:321
  126.6 2.0 collective-permute-start.37
  127.3 1.4 collective-permute-start.35
  127.9 0.8 collective-permute-start.38
  128.7 2.7 %collective-permute-start.40 = (bf16[384,128]{1,0:T(8,128)(2,1)S(1)}, bf16[384,128]{1,0:T(8,128)(2,1)S(1)}, u32[]{:S(2)}, u32[]{:S(2)}) collective-permute-start(bf16[384,128]{1,0:T(8,128)(2,1)S(1)} %get-tuple-element.62.sent), channel_id=1, source_target_pairs={{24,35},{25,39},{26,33},{27,37},{28,34},{29,38},{30,32},{31,36},{9... | collective-permute-start | bytes 294920 | tf_op jit(solution)/shard_map/ppermute | solution.py:323
  129.4 2.0 collective-permute-start.41
  130.1 1.4 collective-permute-start.39
  131.6 2.7 %collective-permute-start.44 = (bf16[384,128]{1,0:T(8,128)(2,1)S(1)}, bf16[384,128]{1,0:T(8,128)(2,1)S(1)}, u32[]{:S(2)}, u32[]{:S(2)}) collective-permute-start(bf16[384,128]{1,0:T(8,128)(2,1)S(1)} %get-tuple-element.64.sent), channel_id=1, source_target_pairs={{72,83},{73,87},{74,81},{75,85},{76,82},{77,86},{78,80},{79,84},{4... | collective-permute-start | bytes 294920 | tf_op jit(solution)/shard_map/ppermute | solution.py:323
  132.3 2.0 collective-permute-start.45
  132.9 1.4 collective-permute-start.43
  134.4 2.7 %collective-permute-start.48 = (bf16[384,128]{1,0:T(8,128)(2,1)S(1)}, bf16[384,128]{1,0:T(8,128)(2,1)S(1)}, u32[]{:S(2)}, u32[]{:S(2)}) collective-permute-start(bf16[384,128]{1,0:T(8,128)(2,1)S(1)} %get-tuple-element.66.sent), channel_id=1, source_target_pairs={{16,30},{17,26},{18,28},{19,24},{20,31},{21,27},{22,29},{23,25},{1... | collective-permute-start | bytes 294920 | tf_op jit(solution)/shard_map/ppermute | solution.py:323
  135.1 2.0 collective-permute-start.49
  135.8 1.4 collective-permute-start.47
  137.3 18.3 %collective-permute-start.51 = (bf16[384,128]{1,0:T(8,128)(2,1)S(1)}, bf16[384,128]{1,0:T(8,128)(2,1)S(1)}, u32[]{:S(2)}, u32[]{:S(2)}) collective-permute-start(bf16[384,128]{1,0:T(8,128)(2,1)S(1)} %get-tuple-element.68.sent), channel_id=1, source_target_pairs={{88,96},{89,100},{90,98},{91,102},{92,97},{93,101},{94,99},{95,103... | collective-permute-start | bytes 294920 | tf_op jit(solution)/shard_map/ppermute | solution.py:323
  138.6 15.9 %collective-permute-start.52 = (bf16[384,128]{1,0:T(8,128)(2,1)S(1)}, bf16[384,128]{1,0:T(8,128)(2,1)S(1)}, u32[]{:S(2)}, u32[]{:S(2)}) collective-permute-start(bf16[384,128]{1,0:T(8,128)(2,1)S(1)} %get-tuple-element.68.sent), channel_id=1, source_target_pairs={{88,99},{89,103},{90,97},{91,101},{92,98},{93,102},{94,96},{95,100... | collective-permute-start | bytes 294920 | tf_op jit(solution)/shard_map/ppermute | solution.py:323
  139.9 15.7 %collective-permute-start.53 = (bf16[384,128]{1,0:T(8,128)(2,1)S(1)}, bf16[384,128]{1,0:T(8,128)(2,1)S(1)}, u32[]{:S(2)}, u32[]{:S(2)}) collective-permute-start(bf16[384,128]{1,0:T(8,128)(2,1)S(1)} %get-tuple-element.68.sent), channel_id=1, source_target_pairs={{88,98},{89,102},{90,96},{91,100},{92,99},{93,103},{94,97},{95,101... | collective-permute-start | bytes 294920 | tf_op jit(solution)/shard_map/ppermute | solution.py:323
  141.2 15.1 %collective-permute-start.54 = (bf16[384,128]{1,0:T(8,128)(2,1)S(1)}, bf16[384,128]{1,0:T(8,128)(2,1)S(1)}, u32[]{:S(2)}, u32[]{:S(2)}) collective-permute-start(bf16[384,128]{1,0:T(8,128)(2,1)S(1)} %get-tuple-element.68.sent), channel_id=1, source_target_pairs={{88,97},{89,101},{90,99},{91,103},{92,96},{93,100},{94,98},{95,102... | collective-permute-start | bytes 294920 | tf_op jit(solution)/shard_map/ppermute | solution.py:323
  142.5 16.5 %collective-permute-start.33 = (f32[192,128]{1,0:T(8,128)S(1)}, f32[192,128]{1,0:T(8,128)S(1)}, u32[]{:S(2)}, u32[]{:S(2)}) collective-permute-start(f32[192,128]{1,0:T(8,128)S(1)} %slice_select_fusion.3), channel_id=1, source_target_pairs={{0,4},{1,5},{2,6},{3,7},{4,0},{5,1},{6,2},{7,3},{8,9},{9,8},{10,11... | collective-permute-start | bytes 294920 | tf_op jit(solution)/shard_map/ppermute | solution.py:330
  156.3 2.8 %collective-permute-start.55 = (bf16[384,128]{1,0:T(8,128)(2,1)S(1)}, bf16[384,128]{1,0:T(8,128)(2,1)S(1)}, u32[]{:S(2)}, u32[]{:S(2)}) collective-permute-start(bf16[384,128]{1,0:T(8,128)(2,1)S(1)} %get-tuple-element.70.sent), channel_id=1, source_target_pairs={{72,80},{73,84},{74,82},{75,86},{76,81},{77,85},{78,83},{79,87},{4... | collective-permute-start | bytes 294920 | tf_op jit(solution)/shard_map/ppermute | solution.py:323
  157.0 2.1 collective-permute-start.56
  157.7 1.4 collective-permute-start.57
  158.3 0.8 collective-permute-start.58
  159.2 2.9 %collective-permute-start.59 = (bf16[384,128]{1,0:T(8,128)(2,1)S(1)}, bf16[384,128]{1,0:T(8,128)(2,1)S(1)}, u32[]{:S(2)}, u32[]{:S(2)}) collective-permute-start(bf16[384,128]{1,0:T(8,128)(2,1)S(1)} %get-tuple-element.72.sent), channel_id=1, source_target_pairs={{24,32},{25,36},{26,34},{27,38},{28,33},{29,37},{30,35},{31,39},{9... | collective-permute-start | bytes 294920 | tf_op jit(solution)/shard_map/ppermute | solution.py:323
  159.9 2.1 collective-permute-start.60
  160.5 1.5 collective-permute-start.61
  161.2 0.9 collective-permute-start.62
  162.1 63.7 %collective-permute-start.63 = (bf16[384,128]{1,0:T(8,128)(2,1)S(1)}, bf16[384,128]{1,0:T(8,128)(2,1)S(1)}, u32[]{:S(2)}, u32[]{:S(2)}) collective-permute-start(bf16[384,128]{1,0:T(8,128)(2,1)S(1)} %get-tuple-element.74.sent), channel_id=1, source_target_pairs={{88,96},{89,100},{90,98},{91,102},{92,97},{93,101},{94,99},{95,103... | collective-permute-start | bytes 294920 | tf_op jit(solution)/shard_map/ppermute | solution.py:323
  163.4 60.1 %collective-permute-start.64 = (bf16[384,128]{1,0:T(8,128)(2,1)S(1)}, bf16[384,128]{1,0:T(8,128)(2,1)S(1)}, u32[]{:S(2)}, u32[]{:S(2)}) collective-permute-start(bf16[384,128]{1,0:T(8,128)(2,1)S(1)} %get-tuple-element.74.sent), channel_id=1, source_target_pairs={{88,99},{89,103},{90,97},{91,101},{92,98},{93,102},{94,96},{95,100... | collective-permute-start | bytes 294920 | tf_op jit(solution)/shard_map/ppermute | solution.py:323
  164.7 60.0 %collective-permute-start.65 = (bf16[384,128]{1,0:T(8,128)(2,1)S(1)}, bf16[384,128]{1,0:T(8,128)(2,1)S(1)}, u32[]{:S(2)}, u32[]{:S(2)}) collective-permute-start(bf16[384,128]{1,0:T(8,128)(2,1)S(1)} %get-tuple-element.74.sent), channel_id=1, source_target_pairs={{88,98},{89,102},{90,96},{91,100},{92,99},{93,103},{94,97},{95,101... | collective-permute-start | bytes 294920 | tf_op jit(solution)/shard_map/ppermute | solution.py:323
  166.0 60.5 %collective-permute-start.66 = (bf16[384,128]{1,0:T(8,128)(2,1)S(1)}, bf16[384,128]{1,0:T(8,128)(2,1)S(1)}, u32[]{:S(2)}, u32[]{:S(2)}) collective-permute-start(bf16[384,128]{1,0:T(8,128)(2,1)S(1)} %get-tuple-element.74.sent), channel_id=1, source_target_pairs={{88,97},{89,101},{90,99},{91,103},{92,96},{93,100},{94,98},{95,102... | collective-permute-start | bytes 294920 | tf_op jit(solution)/shard_map/ppermute | solution.py:323
  228.1 3.5 %collective-permute-start.67 = (f32[192,128]{1,0:T(8,128)S(1)}, f32[192,128]{1,0:T(8,128)S(1)}, u32[]{:S(2)}, u32[]{:S(2)}) collective-permute-start(f32[192,128]{1,0:T(8,128)S(1)} %slice_select_fusion.1), channel_id=1, source_target_pairs={{0,4},{1,5},{2,6},{3,7},{4,0},{5,1},{6,2},{7,3},{8,9},{9,8},{10,11... | collective-permute-start | bytes 294920 | tf_op jit(solution)/shard_map/ppermute | solution.py:330
  (8 other events, 15.1 us)

commit v2 on v1

--- a/solution.py
+++ b/solution.py
@@ -64,6 +64,10 @@
 
 
 INNER_PAIRS = [pair for pair in PAIRS if 0 < pair[0] // LATS < LAYERS - 1]
+
+MIDDLE = range(4, 12)
+MIDDLE_PAIRS = [pair for pair in PAIRS if pair[0] // LATS in MIDDLE]
+OUTER_PAIRS = [pair for pair in PAIRS if pair[0] // LATS not in MIDDLE]
 
 
 def rank_table():
@@ -127,17 +131,21 @@
     return field[:, RELAX : RELAX + slab]
 
 
-def load_kernel(info, own, other, out, first, second, sems):
+def load_kernel(info, own, *refs):
+    others, (out, first, second, sems) = refs[:-4], refs[-4:]
     slab = first.shape[1]
     cells = first.shape[2] // 2
-    copies = [
-        pltpu.make_async_copy(own, first, sems.at[0]),
-        pltpu.make_async_copy(other, second, sems.at[1]),
-    ]
-    for copy in copies:
-        copy.start()
-    for copy in copies:
-        copy.wait()
+    near = pltpu.make_async_copy(own, first, sems.at[0])
+    near.start()
+    for k, other in enumerate(others):
+
+        @pl.when(jnp.logical_or(len(others) == 1, info[FAN + 2] == k))
+        def _():
+            far = pltpu.make_async_copy(other, second, sems.at[1])
+            far.start()
+            far.wait()
+
+    near.wait()
     even = info[FAN] == 0
     band = slab // 3
 
@@ -172,13 +180,13 @@
                         )
 
 
-def loaded(info, own, other):
+def loaded(info, own, *others):
     slab, cells = own.shape[1], own.shape[2] // 2
     anywhere = pl.BlockSpec(memory_space=pl.ANY)
     return pl.pallas_call(
         load_kernel,
         out_shape=jax.ShapeDtypeStruct((FAN, 4 * slab, 2 * cells // FAN), own.dtype),
-        in_specs=[pl.BlockSpec(memory_space=pltpu.SMEM), anywhere, anywhere],
+        in_specs=[pl.BlockSpec(memory_space=pltpu.SMEM)] + [anywhere] * (1 + len(others)),
         out_specs=pl.BlockSpec(memory_space=pltpu.VMEM),
         scratch_shapes=[
             pltpu.VMEM(own.shape, own.dtype),
@@ -189,7 +197,7 @@
         cost_estimate=pl.CostEstimate(
             flops=0, bytes_accessed=8 * own.size, transcendentals=0
         ),
-    )(info, own, other)
+    )(info, own, *others)
 
 
 def is_live(step):
@@ -294,7 +302,8 @@
     upper = place == 1
     ranks = jnp.asarray(rank_table().reshape(2 * LATS, FAN))
     mine = lax.dynamic_index_in_dim(ranks, parity * LATS + lat, 0, keepdims=False)
-    info = jnp.concatenate([mine, jnp.stack([parity, place])])
+    middle = ((layer >= MIDDLE.start) & (layer < MIDDLE.stop)).astype(jnp.int32)
+    info = jnp.concatenate([mine, jnp.stack([parity, place, middle])])
 
     own_first = jnp.where(low, green_down[0], green_up[0])
     own_first, source, wavenumber = lax.optimization_barrier((own_first, source, wavenumber))
@@ -314,6 +323,10 @@
         upper, jnp.concatenate([swapped, keep], 0), jnp.concatenate([keep, swapped], 0)
     )
     green_first = loaded(info, own_first, other_first)
+    down_later, up_later, traces = lax.optimization_barrier((green_down, green_up, traces))
+    own_second = jnp.where(low, up_later[0], down_later[0])
+    own_second, other_first = lax.optimization_barrier((own_second, other_first))
+    other_middle = lax.ppermute(own_second, BOTH, MIDDLE_PAIRS)
 
     def advance(step, green, before, sent):
         if step == HALF:
@@ -337,11 +350,10 @@
     first, sent = trace, trace.astype(jnp.bfloat16)
     for step in range(1, HALF):
         if step == SWAP:
-            down_later, up_later, sent = lax.optimization_barrier((green_down, green_up, sent))
-            own_second = jnp.where(low, up_later[0], down_later[0])
-            other_second = lax.ppermute(own_second, BOTH, PAIRS)
+            own_late, sent = lax.optimization_barrier((own_second, sent))
+            other_outer = lax.ppermute(own_late, BOTH, OUTER_PAIRS)
         if step == HALF - 1:
-            green_second = loaded(info, own_second, other_second)
+            green_second = loaded(info, own_second, other_outer, other_middle)
             green_first, green_second = lax.optimization_barrier((green_first, green_second))
         first, sent = advance(step, green_first, first, sent)
     near = joined(first)

time: 234 us -> 233 us (level)
  starting transfers between devices: 107 us -> 110 us
  local copies, waits for them, and re-layouts: 3.41 us -> 1.07 us
    ppermute x1 -> x2, starting transfers between devices: 1.64 us -> 4.03 us  [the longest x1 3.22 us: local(): other_outer = lax.ppermute(own_late, BOTH, OUTER_PAIRS)]
    ppermute x1 -> x2, waiting for transfers between devices: 21 us -> 21.1 us  [the longest x1 21.1 us: local(): other_outer = lax.ppermute(own_late, BOTH, OUTER_PAIRS)]
  transfers between devices with their start and end apart: 68 -> 69, of which waited for: 11 -> 10; matrix products, arithmetic and copies ran while one was open for 1% -> 1% of each run, Pallas kernels for 4% -> 4%
where the time goes in v2:
time: 233 us; the launch traced here: 232 us
  starting transfers between devices  110 us (47%)
  waiting for transfers between devices  102 us (44%)
  Pallas kernels  11.2 us (5%)
  other arithmetic  5.43 us (2%)
    ppermute x56, starting transfers between devices, advance(): pieces = [lax.ppermute(sent, BOTH, routes(step, r)) for r in range(FAN)]  91.3 us
    ppermute x56, waiting for transfers between devices, advance(): pieces = [lax.ppermute(sent, BOTH, routes(step, r)) for r in range(FAN)]  69.9 us
    ppermute x1, waiting for transfers between devices, local(): other_outer = lax.ppermute(own_late, BOTH, OUTER_PAIRS)  21.1 us
    pallas_call x2, Pallas kernels, loaded(): pl.pallas_call(load_kernel, out_shape=jax.ShapeDtypeStruct((FAN, 4 * slab...  6.96 us
    ppermute x1, starting transfers between devices, padded_2(): lax.ppermute(lax.slice_in_dim(block, 0, width, axis=dim), axis, backward)  5.85 us
  transfers between devices with their start and end apart: 69, of which 10 were waited for; matrix products, arithmetic and copies ran while one was open for 1% of the time, Pallas kernels for 4%

profile of v2, /device:TPU:31, one launch (start us, length us, event | category | flops | bytes accessed | tf_op | source)
XLA Modules:
  0.0 231.8 jit_solution(13009279318813560030)
XLA Ops:
  0.7 2.0 select_bitcast_fusion.1.own
  2.6 2.0 collective-permute-start
  4.7 5.8 %collective-permute-start.2 = (bf16[3,4,128]{2,1,0:T(4,128)(2,1)S(1)}, bf16[3,4,128]{2,1,0:T(4,128)(2,1)S(1)}, u32[]{:S(2)}, u32[]{:S(2)}) collective-permute-start(bf16[3,4,128]{2,1,0:T(4,128)(2,1)S(1)} %get-tuple-element.106), channel_id=1, source_target_pairs={{1,0},{2,1},{3,2},{4,3},{5,4},{6,5},{7,6},{9,8},{10,9},{11,10},{12... | collective-permute-start | bytes 9224 | tf_op jit(solution)/shard_map/ppermute | solution.py:90
  10.6 1.9 collective-permute-start.1
  12.8 4.3 %collective-permute-done.1 = bf16[3,4,128]{2,1,0:T(4,128)(2,1)S(1)} collective-permute-done((bf16[3,4,128]{2,1,0:T(4,128)(2,1)S(1)}, bf16[3,4,128]{2,1,0:T(4,128)(2,1)S(1)}, u32[]{:S(2)}, u32[]{:S(2)}) %collective-permute-start.1) | collective-permute-done | bytes 3104 | tf_op jit(solution)/shard_map/ppermute | solution.py:89
  19.0 0.7 dynamic-slice_bitcast_fusion
  19.7 3.2 %collective-permute-done.3 = f32[192,128]{1,0:T(8,128)S(1)} collective-permute-done((f32[192,128]{1,0:T(8,128)S(1)}, f32[192,128]{1,0:T(8,128)S(1)}, u32[]{:S(2)}, u32[]{:S(2)}) %collective-permute-start.3) | collective-permute-done | bytes 98336 | tf_op jit(solution)/shard_map/ppermute | solution.py:321
  22.9 15.8 %collective-permute-start.4 = (bf16[384,128]{1,0:T(8,128)(2,1)S(1)}, bf16[384,128]{1,0:T(8,128)(2,1)S(1)}, u32[]{:S(2)}, u32[]{:S(2)}) collective-permute-start(bf16[384,128]{1,0:T(8,128)(2,1)S(1)} %get-tuple-element.80.sent), channel_id=1, source_target_pairs={{0,8},{1,12},{2,10},{3,14},{4,9},{5,13},{6,11},{7,15},{120,112},{1... | collective-permute-start | bytes 294920 | tf_op jit(solution)/shard_map/ppermute | solution.py:336
  38.8 3.3 %collective-permute-start.5 = (bf16[384,128]{1,0:T(8,128)(2,1)S(1)}, bf16[384,128]{1,0:T(8,128)(2,1)S(1)}, u32[]{:S(2)}, u32[]{:S(2)}) collective-permute-start(bf16[384,128]{1,0:T(8,128)(2,1)S(1)} %get-tuple-element.80.sent), channel_id=1, source_target_pairs={{0,14},{1,10},{2,12},{3,8},{4,15},{5,11},{6,13},{7,9},{120,115},{1... | collective-permute-start | bytes 294920 | tf_op jit(solution)/shard_map/ppermute | solution.py:336
  42.0 5.8 %collective-permute-start.6 = (bf16[384,128]{1,0:T(8,128)(2,1)S(1)}, bf16[384,128]{1,0:T(8,128)(2,1)S(1)}, u32[]{:S(2)}, u32[]{:S(2)}) collective-permute-start(bf16[384,128]{1,0:T(8,128)(2,1)S(1)} %get-tuple-element.80.sent), channel_id=1, source_target_pairs={{0,10},{1,14},{2,8},{3,12},{4,11},{5,15},{6,9},{7,13},{120,114},{1... | collective-permute-start | bytes 294920 | tf_op jit(solution)/shard_map/ppermute | solution.py:336
  47.9 1.8 collective-permute-start.7
  49.8 4.1 %shard_map.68.green = bf16[4,768,768]{2,1,0:T(8,128)(2,1)S(1)} custom-call(s32[7]{0:T(128)S(1)} %pad_add_fusion.info, bf16[2,192,3072]{2,1,0:T(8,128)(2,1)S(1)} %select_bitcast_fusion.1.own, bf16[2,192,3072]{2,1,0:T(8,128)(2,1)} %collective-permute-done.refs_0_), custom_call_target="tpu_custom_call" | custom-call | bytes 9437184 | tf_op jit(solution)/shard_map/pallas_call | solution.py:186
  54.0 0.7 collective-permute-start.9
  54.7 0.7 collective-permute-start.10
  55.4 0.7 collective-permute-start.8
  56.1 0.7 collective-permute-start.11
  56.9 0.7 collective-permute-start.13
  57.5 0.7 collective-permute-start.14
  58.2 0.7 collective-permute-start.12
  58.9 0.7 collective-permute-start.15
  59.7 0.7 collective-permute-start.17
  60.4 0.7 collective-permute-start.18
  61.1 0.7 collective-permute-start.16
  61.7 0.7 collective-permute-start.19
  62.6 22.9 %collective-permute-start.20 = (bf16[384,128]{1,0:T(8,128)(2,1)S(1)}, bf16[384,128]{1,0:T(8,128)(2,1)S(1)}, u32[]{:S(2)}, u32[]{:S(2)}) collective-permute-start(bf16[384,128]{1,0:T(8,128)(2,1)S(1)} %get-tuple-element.54.sent), channel_id=1, source_target_pairs={{0,8},{1,12},{2,10},{3,14},{4,9},{5,13},{6,11},{7,15},{120,112},{1... | collective-permute-start | bytes 294920 | tf_op jit(solution)/shard_map/ppermute | solution.py:336
  85.5 2.0 collective-permute-start.21
  87.5 1.3 collective-permute-start.22
  88.8 1.3 collective-permute-start.23
  90.4 0.8 collective-permute-start.25
  91.8 3.2 %collective-permute-start.24 = (bf16[2,192,3072]{2,1,0:T(8,128)(2,1)S(1)}, bf16[2,192,3072]{2,1,0:T(8,128)(2,1)S(1)}, u32[]{:S(2)}, u32[]{:S(2)}) collective-permute-start(bf16[2,192,3072]{2,1,0:T(8,128)(2,1)S(1)} %select_bitcast_fusion.own), channel_id=1, source_target_pairs={{0,4},{1,5},{2,6},{3,7},{4,0},{5,1},{6,2},{7,3},{8,9},{9,8},{10,11... | collective-permute-start | bytes 7077896 | tf_op jit(solution)/shard_map/ppermute | solution.py:354
  95.0 0.7 collective-permute-start.27
  95.7 0.7 collective-permute-start.28
  96.3 0.7 collective-permute-start.26
  97.0 0.7 collective-permute-start.29
  97.8 0.7 collective-permute-start.31
  98.5 0.7 collective-permute-start.32
  99.2 0.7 collective-permute-start.30
  99.9 0.7 collective-permute-start.33
  100.5 21.1 %collective-permute-done.24.refs_0_ = bf16[2,192,3072]{2,1,0:T(8,128)(2,1)S(1)} collective-permute-done((bf16[2,192,3072]{2,1,0:T(8,128)(2,1)S(1)}, bf16[2,192,3072]{2,1,0:T(8,128)(2,1)S(1)}, u32[]{:S(2)}, u32[]{:S(2)}) %collective-permute-start.24) | collective-permute-done | bytes 2359328 | tf_op jit(solution)/shard_map/ppermute | solution.py:354
  121.6 2.8 %shard_map.84.green = bf16[4,768,768]{2,1,0:T(8,128)(2,1)S(1)} custom-call(s32[7]{0:T(128)S(1)} %pad_add_fusion.info, bf16[2,192,3072]{2,1,0:T(8,128)(2,1)S(1)} %select_bitcast_fusion.own, bf16[2,192,3072]{2,1,0:T(8,128)(2,1)S(1)} %collective-permute-done.24.refs_0_, bf16[2,192,3072]{2,1,0:T(8,128)(2,1)S(1)} %collective-permute-done.25.refs_1_), custom_call_target="tpu_custom_call" | custom-call | bytes 9437184 | tf_op jit(solution)/shard_map/pallas_call | solution.py:186
  124.6 0.7 collective-permute-start.35
  125.3 0.7 collective-permute-start.37
  126.0 0.7 collective-permute-start.38
  126.7 0.7 collective-permute-start.36
  127.3 0.7 collective-permute-start.39
  128.1 0.7 collective-permute-start.41
  136.6 1.3 collective-permute-start.52
  137.9 1.3 collective-permute-start.53
  139.2 1.3 collective-permute-start.54
  140.5 1.3 collective-permute-start.55
  141.9 1.4 collective-permute-start.34
  143.3 10.7 %collective-permute-done.53.refs_0_ = bf16[384,128]{1,0:T(8,128)(2,1)S(1)} collective-permute-done((bf16[384,128]{1,0:T(8,128)(2,1)S(1)}, bf16[384,128]{1,0:T(8,128)(2,1)S(1)}, u32[]{:S(2)}, u32[]{:S(2)}) %collective-permute-start.53) | collective-permute-done | bytes 98336 | tf_op jit(solution)/shard_map/ppermute | solution.py:336
  154.0 1.1 collective-permute-done.54.refs_1_
  161.4 1.3 collective-permute-start.64
  162.7 1.3 collective-permute-start.65
  164.0 1.3 collective-permute-start.66
  165.3 1.3 collective-permute-start.67
  166.7 55.8 %collective-permute-done.65.refs_0_ = bf16[384,128]{1,0:T(8,128)(2,1)S(1)} collective-permute-done((bf16[384,128]{1,0:T(8,128)(2,1)S(1)}, bf16[384,128]{1,0:T(8,128)(2,1)S(1)}, u32[]{:S(2)}, u32[]{:S(2)}) %collective-permute-start.65) | collective-permute-done | bytes 98336 | tf_op jit(solution)/shard_map/ppermute | solution.py:336
  222.5 1.2 collective-permute-done.66.refs_1_
  223.7 1.1 shard_map.112.refs_1_
  224.8 0.7 shard_map.113.earlier
  225.6 1.5 shard_map.114
  227.3 3.4 %collective-permute-done.68 = f32[192,128]{1,0:T(8,128)S(1)} collective-permute-done((f32[192,128]{1,0:T(8,128)S(1)}, f32[192,128]{1,0:T(8,128)S(1)}, u32[]{:S(2)}, u32[]{:S(2)}) %collective-permute-start.68) | collective-permute-done | bytes 98336 | tf_op jit(solution)/shard_map/ppermute | solution.py:343
  231.0 0.8 fusion.15
  (169 shorter events, 17.9 us)
Async XLA Ops:
  2.6 47.1 %collective-permute-start = (bf16[2,192,3072]{2,1,0:T(8,128)(2,1)S(1)}, bf16[2,192,3072]{2,1,0:T(8,128)(2,1)}, u32[]{:S(2)}, u32[]{:S(2)}) collective-permute-start(bf16[2,192,3072]{2,1,0:T(8,128)(2,1)S(1)} %select_bitcast_fusion.1.own), channel_id=1, source_target_pairs={{8,9},{9,8},{10,11},{11,10},{12,13},{13,12},{14,15},{15,14},{16,20... | collective-permute-start | bytes 7077896 | tf_op jit(solution)/shard_map/ppermute | solution.py:310
  4.7 8.0 %collective-permute-start.2 = (bf16[3,4,128]{2,1,0:T(4,128)(2,1)S(1)}, bf16[3,4,128]{2,1,0:T(4,128)(2,1)S(1)}, u32[]{:S(2)}, u32[]{:S(2)}) collective-permute-start(bf16[3,4,128]{2,1,0:T(4,128)(2,1)S(1)} %get-tuple-element.106), channel_id=1, source_target_pairs={{1,0},{2,1},{3,2},{4,3},{5,4},{6,5},{7,6},{9,8},{10,9},{11,10},{12... | collective-permute-start | bytes 9224 | tf_op jit(solution)/shard_map/ppermute | solution.py:90
  10.6 6.5 %collective-permute-start.1 = (bf16[3,4,128]{2,1,0:T(4,128)(2,1)S(1)}, bf16[3,4,128]{2,1,0:T(4,128)(2,1)S(1)}, u32[]{:S(2)}, u32[]{:S(2)}) collective-permute-start(bf16[3,4,128]{2,1,0:T(4,128)(2,1)S(1)} %get-tuple-element.105), channel_id=1, source_target_pairs={{0,1},{1,2},{2,3},{3,4},{4,5},{5,6},{6,7},{8,9},{9,10},{10,11},{11... | collective-permute-start | bytes 9224 | tf_op jit(solution)/shard_map/ppermute | solution.py:89
  18.9 3.9 %collective-permute-start.3 = (f32[192,128]{1,0:T(8,128)S(1)}, f32[192,128]{1,0:T(8,128)S(1)}, u32[]{:S(2)}, u32[]{:S(2)}) collective-permute-start(f32[192,128]{1,0:T(8,128)S(1)} %get-tuple-element.96), channel_id=1, source_target_pairs={{0,4},{1,5},{2,6},{3,7},{4,0},{5,1},{6,2},{7,3},{8,9},{9,8},{10,11... | collective-permute-start | bytes 294920 | tf_op jit(solution)/shard_map/ppermute | solution.py:321
  22.9 31.0 %collective-permute-start.4 = (bf16[384,128]{1,0:T(8,128)(2,1)S(1)}, bf16[384,128]{1,0:T(8,128)(2,1)S(1)}, u32[]{:S(2)}, u32[]{:S(2)}) collective-permute-start(bf16[384,128]{1,0:T(8,128)(2,1)S(1)} %get-tuple-element.80.sent), channel_id=1, source_target_pairs={{0,8},{1,12},{2,10},{3,14},{4,9},{5,13},{6,11},{7,15},{120,112},{1... | collective-permute-start | bytes 294920 | tf_op jit(solution)/shard_map/ppermute | solution.py:336
  38.8 15.1 %collective-permute-start.5 = (bf16[384,128]{1,0:T(8,128)(2,1)S(1)}, bf16[384,128]{1,0:T(8,128)(2,1)S(1)}, u32[]{:S(2)}, u32[]{:S(2)}) collective-permute-start(bf16[384,128]{1,0:T(8,128)(2,1)S(1)} %get-tuple-element.80.sent), channel_id=1, source_target_pairs={{0,14},{1,10},{2,12},{3,8},{4,15},{5,11},{6,13},{7,9},{120,115},{1... | collective-permute-start | bytes 294920 | tf_op jit(solution)/shard_map/ppermute | solution.py:336
  42.0 11.9 %collective-permute-start.6 = (bf16[384,128]{1,0:T(8,128)(2,1)S(1)}, bf16[384,128]{1,0:T(8,128)(2,1)S(1)}, u32[]{:S(2)}, u32[]{:S(2)}) collective-permute-start(bf16[384,128]{1,0:T(8,128)(2,1)S(1)} %get-tuple-element.80.sent), channel_id=1, source_target_pairs={{0,10},{1,14},{2,8},{3,12},{4,11},{5,15},{6,9},{7,13},{120,114},{1... | collective-permute-start | bytes 294920 | tf_op jit(solution)/shard_map/ppermute | solution.py:336
  47.9 6.1 %collective-permute-start.7 = (bf16[384,128]{1,0:T(8,128)(2,1)S(1)}, bf16[384,128]{1,0:T(8,128)(2,1)S(1)}, u32[]{:S(2)}, u32[]{:S(2)}) collective-permute-start(bf16[384,128]{1,0:T(8,128)(2,1)S(1)} %get-tuple-element.80.sent), channel_id=1, source_target_pairs={{0,12},{1,8},{2,14},{3,10},{4,13},{5,9},{6,15},{7,11},{120,113},{1... | collective-permute-start | bytes 294920 | tf_op jit(solution)/shard_map/ppermute | solution.py:336
  54.0 2.7 %collective-permute-start.9 = (bf16[384,128]{1,0:T(8,128)(2,1)S(1)}, bf16[384,128]{1,0:T(8,128)(2,1)S(1)}, u32[]{:S(2)}, u32[]{:S(2)}) collective-permute-start(bf16[384,128]{1,0:T(8,128)(2,1)S(1)} %get-tuple-element.48.sent), channel_id=1, source_target_pairs={{8,19},{9,23},{10,17},{11,21},{12,18},{13,22},{14,16},{15,20},{112... | collective-permute-start | bytes 294920 | tf_op jit(solution)/shard_map/ppermute | solution.py:336
  54.7 2.0 collective-permute-start.10
  55.4 1.4 collective-permute-start.8
  56.1 0.8 collective-permute-start.11
  56.9 2.7 %collective-permute-start.13 = (bf16[384,128]{1,0:T(8,128)(2,1)S(1)}, bf16[384,128]{1,0:T(8,128)(2,1)S(1)}, u32[]{:S(2)}, u32[]{:S(2)}) collective-permute-start(bf16[384,128]{1,0:T(8,128)(2,1)S(1)} %get-tuple-element.50.sent), channel_id=1, source_target_pairs={{16,30},{17,26},{18,28},{19,24},{20,31},{21,27},{22,29},{23,25},{1... | collective-permute-start | bytes 294920 | tf_op jit(solution)/shard_map/ppermute | solution.py:336
  57.5 2.0 collective-permute-start.14
  58.2 1.4 collective-permute-start.12
  58.9 0.8 collective-permute-start.15
  59.7 2.7 %collective-permute-start.17 = (bf16[384,128]{1,0:T(8,128)(2,1)S(1)}, bf16[384,128]{1,0:T(8,128)(2,1)S(1)}, u32[]{:S(2)}, u32[]{:S(2)}) collective-permute-start(bf16[384,128]{1,0:T(8,128)(2,1)S(1)} %get-tuple-element.52.sent), channel_id=1, source_target_pairs={{24,35},{25,39},{26,33},{27,37},{28,34},{29,38},{30,32},{31,36},{9... | collective-permute-start | bytes 294920 | tf_op jit(solution)/shard_map/ppermute | solution.py:336
  60.4 2.0 collective-permute-start.18
  61.1 1.4 collective-permute-start.16
  61.7 0.8 collective-permute-start.19
  62.6 28.7 %collective-permute-start.20 = (bf16[384,128]{1,0:T(8,128)(2,1)S(1)}, bf16[384,128]{1,0:T(8,128)(2,1)S(1)}, u32[]{:S(2)}, u32[]{:S(2)}) collective-permute-start(bf16[384,128]{1,0:T(8,128)(2,1)S(1)} %get-tuple-element.54.sent), channel_id=1, source_target_pairs={{0,8},{1,12},{2,10},{3,14},{4,9},{5,13},{6,11},{7,15},{120,112},{1... | collective-permute-start | bytes 294920 | tf_op jit(solution)/shard_map/ppermute | solution.py:336
  85.5 5.8 %collective-permute-start.21 = (bf16[384,128]{1,0:T(8,128)(2,1)S(1)}, bf16[384,128]{1,0:T(8,128)(2,1)S(1)}, u32[]{:S(2)}, u32[]{:S(2)}) collective-permute-start(bf16[384,128]{1,0:T(8,128)(2,1)S(1)} %get-tuple-element.54.sent), channel_id=1, source_target_pairs={{0,14},{1,10},{2,12},{3,8},{4,15},{5,11},{6,13},{7,9},{120,115},{1... | collective-permute-start | bytes 294920 | tf_op jit(solution)/shard_map/ppermute | solution.py:336
  87.5 3.7 %collective-permute-start.22 = (bf16[384,128]{1,0:T(8,128)(2,1)S(1)}, bf16[384,128]{1,0:T(8,128)(2,1)S(1)}, u32[]{:S(2)}, u32[]{:S(2)}) collective-permute-start(bf16[384,128]{1,0:T(8,128)(2,1)S(1)} %get-tuple-element.54.sent), channel_id=1, source_target_pairs={{0,10},{1,14},{2,8},{3,12},{4,11},{5,15},{6,9},{7,13},{120,114},{1... | collective-permute-start | bytes 294920 | tf_op jit(solution)/shard_map/ppermute | solution.py:336
  88.8 2.9 %collective-permute-start.23 = (bf16[384,128]{1,0:T(8,128)(2,1)S(1)}, bf16[384,128]{1,0:T(8,128)(2,1)S(1)}, u32[]{:S(2)}, u32[]{:S(2)}) collective-permute-start(bf16[384,128]{1,0:T(8,128)(2,1)S(1)} %get-tuple-element.54.sent), channel_id=1, source_target_pairs={{0,12},{1,8},{2,14},{3,10},{4,13},{5,9},{6,15},{7,11},{120,113},{1... | collective-permute-start | bytes 294920 | tf_op jit(solution)/shard_map/ppermute | solution.py:336
  90.4 9.5 %collective-permute-start.25 = (bf16[2,192,3072]{2,1,0:T(8,128)(2,1)S(1)}, bf16[2,192,3072]{2,1,0:T(8,128)(2,1)S(1)}, u32[]{:S(2)}, u32[]{:S(2)}) collective-permute-start(bf16[2,192,3072]{2,1,0:T(8,128)(2,1)S(1)} %select_bitcast_fusion.own), channel_id=1, source_target_pairs={{32,36},{33,37},{34,38},{35,39},{36,32},{37,33},{38,34},{39,35},{4... | collective-permute-start | bytes 7077896 | tf_op jit(solution)/shard_map/ppermute | solution.py:329
  91.8 29.9 %collective-permute-start.24 = (bf16[2,192,3072]{2,1,0:T(8,128)(2,1)S(1)}, bf16[2,192,3072]{2,1,0:T(8,128)(2,1)S(1)}, u32[]{:S(2)}, u32[]{:S(2)}) collective-permute-start(bf16[2,192,3072]{2,1,0:T(8,128)(2,1)S(1)} %select_bitcast_fusion.own), channel_id=1, source_target_pairs={{0,4},{1,5},{2,6},{3,7},{4,0},{5,1},{6,2},{7,3},{8,9},{9,8},{10,11... | collective-permute-start | bytes 7077896 | tf_op jit(solution)/shard_map/ppermute | solution.py:354
  95.0 2.0 collective-permute-start.27
  95.7 2.0 collective-permute-start.28
  96.3 1.4 collective-permute-start.26
  97.8 26.7 %collective-permute-start.31 = (bf16[384,128]{1,0:T(8,128)(2,1)S(1)}, bf16[384,128]{1,0:T(8,128)(2,1)S(1)}, u32[]{:S(2)}, u32[]{:S(2)}) collective-permute-start(bf16[384,128]{1,0:T(8,128)(2,1)S(1)} %get-tuple-element.61.sent), channel_id=1, source_target_pairs={{16,30},{17,26},{18,28},{19,24},{20,31},{21,27},{22,29},{23,25},{1... | collective-permute-start | bytes 294920 | tf_op jit(solution)/shard_map/ppermute | solution.py:336
  98.5 26.0 %collective-permute-start.32 = (bf16[384,128]{1,0:T(8,128)(2,1)S(1)}, bf16[384,128]{1,0:T(8,128)(2,1)S(1)}, u32[]{:S(2)}, u32[]{:S(2)}) collective-permute-start(bf16[384,128]{1,0:T(8,128)(2,1)S(1)} %get-tuple-element.61.sent), channel_id=1, source_target_pairs={{16,26},{17,30},{18,24},{19,28},{20,27},{21,31},{22,25},{23,29},{1... | collective-permute-start | bytes 294920 | tf_op jit(solution)/shard_map/ppermute | solution.py:336
  99.2 25.4 %collective-permute-start.30 = (bf16[384,128]{1,0:T(8,128)(2,1)S(1)}, bf16[384,128]{1,0:T(8,128)(2,1)S(1)}, u32[]{:S(2)}, u32[]{:S(2)}) collective-permute-start(bf16[384,128]{1,0:T(8,128)(2,1)S(1)} %get-tuple-element.61.sent), channel_id=1, source_target_pairs={{16,24},{17,28},{18,26},{19,30},{20,25},{21,29},{22,27},{23,31},{1... | collective-permute-start | bytes 294920 | tf_op jit(solution)/shard_map/ppermute | solution.py:336
  99.9 24.7 %collective-permute-start.33 = (bf16[384,128]{1,0:T(8,128)(2,1)S(1)}, bf16[384,128]{1,0:T(8,128)(2,1)S(1)}, u32[]{:S(2)}, u32[]{:S(2)}) collective-permute-start(bf16[384,128]{1,0:T(8,128)(2,1)S(1)} %get-tuple-element.61.sent), channel_id=1, source_target_pairs={{16,28},{17,24},{18,30},{19,26},{20,29},{21,25},{22,31},{23,27},{1... | collective-permute-start | bytes 294920 | tf_op jit(solution)/shard_map/ppermute | solution.py:336
  125.3 2.7 %collective-permute-start.37 = (bf16[384,128]{1,0:T(8,128)(2,1)S(1)}, bf16[384,128]{1,0:T(8,128)(2,1)S(1)}, u32[]{:S(2)}, u32[]{:S(2)}) collective-permute-start(bf16[384,128]{1,0:T(8,128)(2,1)S(1)} %collective-permute-done.35), channel_id=1, source_target_pairs={{64,67},{65,71},{66,65},{67,69},{68,66},{69,70},{70,64},{71,68},{5... | collective-permute-start | bytes 294920 | tf_op jit(solution)/shard_map/ppermute | solution.py:334
  126.0 2.0 collective-permute-start.38
  126.7 1.4 collective-permute-start.36
  127.3 0.8 collective-permute-start.39
  128.1 2.7 %collective-permute-start.41 = (bf16[384,128]{1,0:T(8,128)(2,1)S(1)}, bf16[384,128]{1,0:T(8,128)(2,1)S(1)}, u32[]{:S(2)}, u32[]{:S(2)}) collective-permute-start(bf16[384,128]{1,0:T(8,128)(2,1)S(1)} %get-tuple-element.66.sent), channel_id=1, source_target_pairs={{24,35},{25,39},{26,33},{27,37},{28,34},{29,38},{30,32},{31,36},{9... | collective-permute-start | bytes 294920 | tf_op jit(solution)/shard_map/ppermute | solution.py:336
  128.8 2.0 collective-permute-start.42
  129.5 1.4 collective-permute-start.40
  131.0 2.7 %collective-permute-start.45 = (bf16[384,128]{1,0:T(8,128)(2,1)S(1)}, bf16[384,128]{1,0:T(8,128)(2,1)S(1)}, u32[]{:S(2)}, u32[]{:S(2)}) collective-permute-start(bf16[384,128]{1,0:T(8,128)(2,1)S(1)} %get-tuple-element.68.sent), channel_id=1, source_target_pairs={{72,83},{73,87},{74,81},{75,85},{76,82},{77,86},{78,80},{79,84},{4... | collective-permute-start | bytes 294920 | tf_op jit(solution)/shard_map/ppermute | solution.py:336
  131.6 2.0 collective-permute-start.46
  132.3 1.4 collective-permute-start.44
  133.8 2.7 %collective-permute-start.49 = (bf16[384,128]{1,0:T(8,128)(2,1)S(1)}, bf16[384,128]{1,0:T(8,128)(2,1)S(1)}, u32[]{:S(2)}, u32[]{:S(2)}) collective-permute-start(bf16[384,128]{1,0:T(8,128)(2,1)S(1)} %get-tuple-element.70.sent), channel_id=1, source_target_pairs={{16,30},{17,26},{18,28},{19,24},{20,31},{21,27},{22,29},{23,25},{1... | collective-permute-start | bytes 294920 | tf_op jit(solution)/shard_map/ppermute | solution.py:336
  134.5 2.0 collective-permute-start.50
  135.2 1.4 collective-permute-start.48
  136.6 18.4 %collective-permute-start.52 = (bf16[384,128]{1,0:T(8,128)(2,1)S(1)}, bf16[384,128]{1,0:T(8,128)(2,1)S(1)}, u32[]{:S(2)}, u32[]{:S(2)}) collective-permute-start(bf16[384,128]{1,0:T(8,128)(2,1)S(1)} %get-tuple-element.72.sent), channel_id=1, source_target_pairs={{88,96},{89,100},{90,98},{91,102},{92,97},{93,101},{94,99},{95,103... | collective-permute-start | bytes 294920 | tf_op jit(solution)/shard_map/ppermute | solution.py:336
  137.9 16.0 %collective-permute-start.53 = (bf16[384,128]{1,0:T(8,128)(2,1)S(1)}, bf16[384,128]{1,0:T(8,128)(2,1)S(1)}, u32[]{:S(2)}, u32[]{:S(2)}) collective-permute-start(bf16[384,128]{1,0:T(8,128)(2,1)S(1)} %get-tuple-element.72.sent), channel_id=1, source_target_pairs={{88,99},{89,103},{90,97},{91,101},{92,98},{93,102},{94,96},{95,100... | collective-permute-start | bytes 294920 | tf_op jit(solution)/shard_map/ppermute | solution.py:336
  139.2 15.8 %collective-permute-start.54 = (bf16[384,128]{1,0:T(8,128)(2,1)S(1)}, bf16[384,128]{1,0:T(8,128)(2,1)S(1)}, u32[]{:S(2)}, u32[]{:S(2)}) collective-permute-start(bf16[384,128]{1,0:T(8,128)(2,1)S(1)} %get-tuple-element.72.sent), channel_id=1, source_target_pairs={{88,98},{89,102},{90,96},{91,100},{92,99},{93,103},{94,97},{95,101... | collective-permute-start | bytes 294920 | tf_op jit(solution)/shard_map/ppermute | solution.py:336
  140.5 15.0 %collective-permute-start.55 = (bf16[384,128]{1,0:T(8,128)(2,1)S(1)}, bf16[384,128]{1,0:T(8,128)(2,1)S(1)}, u32[]{:S(2)}, u32[]{:S(2)}) collective-permute-start(bf16[384,128]{1,0:T(8,128)(2,1)S(1)} %get-tuple-element.72.sent), channel_id=1, source_target_pairs={{88,97},{89,101},{90,99},{91,103},{92,96},{93,100},{94,98},{95,102... | collective-permute-start | bytes 294920 | tf_op jit(solution)/shard_map/ppermute | solution.py:336
  141.9 16.4 %collective-permute-start.34 = (f32[192,128]{1,0:T(8,128)S(1)}, f32[192,128]{1,0:T(8,128)S(1)}, u32[]{:S(2)}, u32[]{:S(2)}) collective-permute-start(f32[192,128]{1,0:T(8,128)S(1)} %slice_select_fusion.3), channel_id=1, source_target_pairs={{0,4},{1,5},{2,6},{3,7},{4,0},{5,1},{6,2},{7,3},{8,9},{9,8},{10,11... | collective-permute-start | bytes 294920 | tf_op jit(solution)/shard_map/ppermute | solution.py:343
  155.6 2.8 %collective-permute-start.56 = (bf16[384,128]{1,0:T(8,128)(2,1)S(1)}, bf16[384,128]{1,0:T(8,128)(2,1)S(1)}, u32[]{:S(2)}, u32[]{:S(2)}) collective-permute-start(bf16[384,128]{1,0:T(8,128)(2,1)S(1)} %get-tuple-element.74.sent), channel_id=1, source_target_pairs={{72,80},{73,84},{74,82},{75,86},{76,81},{77,85},{78,83},{79,87},{4... | collective-permute-start | bytes 294920 | tf_op jit(solution)/shard_map/ppermute | solution.py:336
  156.2 2.1 collective-permute-start.57
  156.9 1.4 collective-permute-start.58
  157.6 0.8 collective-permute-start.59
  158.4 2.9 %collective-permute-start.60 = (bf16[384,128]{1,0:T(8,128)(2,1)S(1)}, bf16[384,128]{1,0:T(8,128)(2,1)S(1)}, u32[]{:S(2)}, u32[]{:S(2)}) collective-permute-start(bf16[384,128]{1,0:T(8,128)(2,1)S(1)} %get-tuple-element.76.sent), channel_id=1, source_target_pairs={{24,32},{25,36},{26,34},{27,38},{28,33},{29,37},{30,35},{31,39},{9... | collective-permute-start | bytes 294920 | tf_op jit(solution)/shard_map/ppermute | solution.py:336
  159.1 2.1 collective-permute-start.61
  159.8 1.5 collective-permute-start.62
  160.5 0.9 collective-permute-start.63
  161.4 63.4 %collective-permute-start.64 = (bf16[384,128]{1,0:T(8,128)(2,1)S(1)}, bf16[384,128]{1,0:T(8,128)(2,1)S(1)}, u32[]{:S(2)}, u32[]{:S(2)}) collective-permute-start(bf16[384,128]{1,0:T(8,128)(2,1)S(1)} %get-tuple-element.78.sent), channel_id=1, source_target_pairs={{88,96},{89,100},{90,98},{91,102},{92,97},{93,101},{94,99},{95,103... | collective-permute-start | bytes 294920 | tf_op jit(solution)/shard_map/ppermute | solution.py:336
  162.7 59.8 %collective-permute-start.65 = (bf16[384,128]{1,0:T(8,128)(2,1)S(1)}, bf16[384,128]{1,0:T(8,128)(2,1)S(1)}, u32[]{:S(2)}, u32[]{:S(2)}) collective-permute-start(bf16[384,128]{1,0:T(8,128)(2,1)S(1)} %get-tuple-element.78.sent), channel_id=1, source_target_pairs={{88,99},{89,103},{90,97},{91,101},{92,98},{93,102},{94,96},{95,100... | collective-permute-start | bytes 294920 | tf_op jit(solution)/shard_map/ppermute | solution.py:336
  164.0 59.7 %collective-permute-start.66 = (bf16[384,128]{1,0:T(8,128)(2,1)S(1)}, bf16[384,128]{1,0:T(8,128)(2,1)S(1)}, u32[]{:S(2)}, u32[]{:S(2)}) collective-permute-start(bf16[384,128]{1,0:T(8,128)(2,1)S(1)} %get-tuple-element.78.sent), channel_id=1, source_target_pairs={{88,98},{89,102},{90,96},{91,100},{92,99},{93,103},{94,97},{95,101... | collective-permute-start | bytes 294920 | tf_op jit(solution)/shard_map/ppermute | solution.py:336
  165.3 60.3 %collective-permute-start.67 = (bf16[384,128]{1,0:T(8,128)(2,1)S(1)}, bf16[384,128]{1,0:T(8,128)(2,1)S(1)}, u32[]{:S(2)}, u32[]{:S(2)}) collective-permute-start(bf16[384,128]{1,0:T(8,128)(2,1)S(1)} %get-tuple-element.78.sent), channel_id=1, source_target_pairs={{88,97},{89,101},{90,99},{91,103},{92,96},{93,100},{94,98},{95,102... | collective-permute-start | bytes 294920 | tf_op jit(solution)/shard_map/ppermute | solution.py:336
  227.1 3.5 %collective-permute-start.68 = (f32[192,128]{1,0:T(8,128)S(1)}, f32[192,128]{1,0:T(8,128)S(1)}, u32[]{:S(2)}, u32[]{:S(2)}) collective-permute-start(f32[192,128]{1,0:T(8,128)S(1)} %slice_select_fusion.1), channel_id=1, source_target_pairs={{0,4},{1,5},{2,6},{3,7},{4,0},{5,1},{6,2},{7,3},{8,9},{9,8},{10,11... | collective-permute-start | bytes 294920 | tf_op jit(solution)/shard_map/ppermute | solution.py:343
  (9 other events, 67.0 us)

commit v3 on v1

--- a/solution.py
+++ b/solution.py
@@ -15,25 +15,20 @@
 HALF = LAYERS // 2
 BOTH = ("layer", "lat")
 SHARED = ((1, 5), (2, 6), (3, 7, 11), (4, 9, 14), (10, 13), (12, 15))
+RIDERS = {(10, 13): (HALF - 1, HALF), (12, 15): (HALF, HALF - 1)}
 FAN = 4
+PLACES = (0, 2, 5, 7)
+SWAPS = (4, 1, 3)
 SWAP = 6
-BATCHES = ((3, 1), (0,), (2,))
+BATCHES = ((3, 2), (1,), (0,))
 
 
 relax_weight = 0.8
 damping = 0.5
 
 
-def partner_of(layer, lat):
-    return lat ^ 4 if layer % 2 == 0 else lat ^ 1
-
-
-def target_of(layer, lat, r):
-    y, z = lat >> 2, lat & 3
-    a, b = r >> 1, r & 1
-    if layer % 2 == 0:
-        return (((z & 1) ^ a) << 2) | (y + 2 * ((z >> 1) ^ b))
-    return ((z & 1) << 2) | ((y ^ a) + 2 * ((z >> 1) ^ b))
+def half_of(lat):
+    return (lat >> 2) ^ (lat & 1)
 
 
 def edges_of(step):
@@ -43,38 +38,29 @@
 def routes(step, r):
     steps = next(group for group in SHARED if step in group)
     edges = [edge for s in steps for edge in edges_of(s)]
+    if steps in RIDERS:
+        edges.append(RIDERS[steps])
     return [
-        (src * LATS + j, dst * LATS + target_of(src, j, r)) for src, dst in edges for j in range(LATS)
+        (src * LATS + j, dst * LATS + (j ^ PLACES[r])) for src, dst in edges for j in range(LATS)
     ]
 
 
-def spread(step, r):
-    return [
-        (dst * LATS + j, dst * LATS + target_of(src, j, r))
-        for src, dst in edges_of(step)
-        for j in range(LATS)
-    ]
-
-
-def straight(step):
-    return [(src * LATS + j, dst * LATS + j) for src, dst in edges_of(step) for j in range(LATS)]
-
-
-PAIRS = [(l * LATS + j, l * LATS + partner_of(l, j)) for l in range(LAYERS) for j in range(LATS)]
-
-
-INNER_PAIRS = [pair for pair in PAIRS if 0 < pair[0] // LATS < LAYERS - 1]
+def swap_pairs(k, layers):
+    return [(l * LATS + j, l * LATS + (j ^ SWAPS[k])) for l in layers for j in range(LATS)]
+
+
+ALL = range(LAYERS)
+INNER = range(1, LAYERS - 1)
+
+
+def sources_of(half):
+    return [j for j in range(LATS) if half_of(j) == half]
 
 
 def rank_table():
-    table = np.zeros((2, LATS, FAN), np.int32)
-    for parity in range(2):
-        source = 1 - parity
-        for j in range(LATS):
-            pair = j % 4 if source % 2 == 0 else j // 2
-            for r in range(FAN):
-                table[parity, target_of(source, j, r), pair] = r
-    return table
+    return np.array(
+        [[PLACES.index(j ^ s) for s in sources_of(half_of(j))] for j in range(LATS)], np.int32
+    )
 
 
 def padded_2(block, axis, dim, width):
@@ -127,69 +113,74 @@
     return field[:, RELAX : RELAX + slab]
 
 
-def load_kernel(info, own, other, out, first, second, sems):
-    slab = first.shape[1]
-    cells = first.shape[2] // 2
-    copies = [
-        pltpu.make_async_copy(own, first, sems.at[0]),
-        pltpu.make_async_copy(other, second, sems.at[1]),
+def load_kernel(info, low_green, high_green, *refs):
+    others, (out, both, sems) = refs[:-3], refs[-3:]
+    slab = both.shape[2]
+    cells = both.shape[3] // 2
+    third = slab // 3
+    near = [
+        pltpu.make_async_copy(green, both.at[0], sems.at[0]) for green in (low_green, high_green)
     ]
-    for copy in copies:
+    low_half = info[FAN + 1] == 1
+
+    @pl.when(low_half)
+    def _():
+        near[0].start()
+
+    @pl.when(jnp.logical_not(low_half))
+    def _():
+        near[1].start()
+
+    far = [
+        pltpu.make_async_copy(other, both.at[1, :, pl.ds(k * third, third)], sems.at[1 + k])
+        for k, other in enumerate(others)
+    ]
+    for copy in far:
         copy.start()
-    for copy in copies:
+    near[0].wait()
+    for copy in far:
         copy.wait()
-    even = info[FAN] == 0
-    band = slab // 3
-
-    @pl.loop(0, 6)
+
+    @pl.loop(0, 12)
     def _(step):
-        part = lax.div(step, 3)
-        start = lax.rem(step, 3) * band
-        near = pl.ds(pl.multiple_of(start, band), band)
-        for held, green in ((info[FAN + 1], first), (1 - info[FAN + 1], second)):
-            base = held * 2 * slab + part * slab + start
-            rows = pl.ds(pl.multiple_of(base, band), band)
-
-            @pl.when(even)
+        side = lax.div(step, 6)
+        part = lax.rem(lax.div(step, 3), 2)
+        start = pl.multiple_of(lax.rem(step, 3) * third, third)
+        near_rows = pl.ds(start, third)
+        rows = pl.ds(pl.multiple_of(step * third, third), third)
+        for half in range(2):
+
+            @pl.when(info[FAN] == half)
             def _():
-                for pair in range(FAN):
+                for k, place in enumerate(sources_of(half)):
                     for column in range(2):
-                        at = column * cells + pair * 2 * slab
-                        out[info[pair], rows, column * 2 * slab : (column + 1) * 2 * slab] = green[
-                            part, near, at : at + 2 * slab
-                        ]
-
-            @pl.when(jnp.logical_not(even))
-            def _():
-                for pair in range(FAN):
-                    for column in range(2):
-                        low = column * cells + pair * slab
-                        high = low + cells // 2
-                        left = green[part, near, low : low + slab]
-                        right = green[part, near, high : high + slab]
-                        out[info[pair], rows, column * 2 * slab : (column + 1) * 2 * slab] = (
-                            jnp.concatenate([left, right], 1)
-                        )
-
-
-def loaded(info, own, other):
-    slab, cells = own.shape[1], own.shape[2] // 2
-    anywhere = pl.BlockSpec(memory_space=pl.ANY)
+                        at = column * cells
+                        cuts = [(at + place * slab, slab)]
+                        for n, swap in enumerate(SWAPS):
+                            cuts.append((at + (place ^ swap) * slab + n * third, third))
+                        wide = [both[side, part, near_rows, low : low + size] for low, size in cuts]
+                        columns = slice(column * 2 * slab, (column + 1) * 2 * slab)
+                        out[info[k], rows, columns] = jnp.concatenate(wide, 1)
+
+
+def loaded(info, low_green, high_green, others):
+    _, slab, width = low_green.shape
+    dtype = low_green.dtype
+    anywhere = pl.BlockSpec(memory_space=pltpu.HBM)
     return pl.pallas_call(
         load_kernel,
-        out_shape=jax.ShapeDtypeStruct((FAN, 4 * slab, 2 * cells // FAN), own.dtype),
-        in_specs=[pl.BlockSpec(memory_space=pltpu.SMEM), anywhere, anywhere],
+        out_shape=jax.ShapeDtypeStruct((FAN, 4 * slab, width // FAN), dtype),
+        in_specs=[pl.BlockSpec(memory_space=pltpu.SMEM)] + [anywhere] * (2 + len(others)),
         out_specs=pl.BlockSpec(memory_space=pltpu.VMEM),
         scratch_shapes=[
-            pltpu.VMEM(own.shape, own.dtype),
-            pltpu.VMEM(own.shape, own.dtype),
-            pltpu.SemaphoreType.DMA((2,)),
+            pltpu.VMEM((2, *low_green.shape), dtype),
+            pltpu.SemaphoreType.DMA((1 + len(SWAPS),)),
         ],
         compiler_params=pltpu.CompilerParams(vmem_limit_bytes=16 * 1024 * 1024),
         cost_estimate=pl.CostEstimate(
-            flops=0, bytes_accessed=8 * own.size, transcendentals=0
+            flops=0, bytes_accessed=8 * low_green.size, transcendentals=0
         ),
-    )(info, own, other)
+    )(info, low_green, high_green, *others)
 
 
 def is_live(step):
@@ -285,23 +276,31 @@
     )(green, trace, before, sent, *sums, *[pieces[r] for r in late])
 
 
+def thirds(rows):
+    size = rows.shape[-2] // 3
+    return [rows[..., k * size : (k + 1) * size, :] for k in range(3)]
+
+
 def local(source, wavenumber, green_down, green_up):
     layer = lax.axis_index("layer")
     lat = lax.axis_index("lat")
     low = layer < HALF
-    parity = layer & 1
-    place = jnp.where(parity == 0, lat >> 2, lat & 1)
+    place = (lat >> 2) ^ (lat & 1)
     upper = place == 1
-    ranks = jnp.asarray(rank_table().reshape(2 * LATS, FAN))
-    mine = lax.dynamic_index_in_dim(ranks, parity * LATS + lat, 0, keepdims=False)
-    info = jnp.concatenate([mine, jnp.stack([parity, place])])
-
-    own_first = jnp.where(low, green_down[0], green_up[0])
-    own_first, source, wavenumber = lax.optimization_barrier((own_first, source, wavenumber))
-    other_first = lax.ppermute(own_first, BOTH, INNER_PAIRS)
+    mine = lax.dynamic_index_in_dim(jnp.asarray(rank_table()), lat, 0, keepdims=False)
+    info = jnp.concatenate([mine, jnp.stack([place, low.astype(jnp.int32)])])
+    down, up = green_down[0], green_up[0]
+
+    def swapped(parts, layers):
+        return [lax.ppermute(x, BOTH, swap_pairs(k, layers)) for k, x in enumerate(parts)]
+
+    given = [jnp.where(low, a, b) for a, b in zip(thirds(down), thirds(up))]
+    given, source, wavenumber = lax.optimization_barrier((given, source, wavenumber))
+    others_first = swapped(given, INNER)
 
     traces = relaxed(source[0], wavenumber[0])
     half = traces.shape[2] // 2
+    slab = traces.shape[1]
 
     def packed(part):
         columns = slice(part * half, (part + 1) * half)
@@ -309,25 +308,22 @@
 
     keep = jnp.where(upper, packed(1), packed(0))
     give = jnp.where(upper, packed(0), packed(1))
-    swapped = lax.ppermute(give, BOTH, PAIRS)
-    trace = jnp.where(
-        upper, jnp.concatenate([swapped, keep], 0), jnp.concatenate([keep, swapped], 0)
-    )
-    green_first = loaded(info, own_first, other_first)
+    trace = jnp.concatenate([keep, *swapped(thirds(give), ALL)], 0)
+    green_first = loaded(info, down, up, others_first)
+    down_later, up_later, traces = lax.optimization_barrier((down, up, traces))
+    given = [jnp.where(low, b, a) for a, b in zip(thirds(down_later), thirds(up_later))]
 
     def advance(step, green, before, sent):
         if step == HALF:
-            shifted = lax.ppermute(sent, BOTH, straight(step))
-            pieces = [lax.ppermute(shifted, BOTH, spread(step, r)) for r in range(FAN)]
+            ways = [[lax.ppermute(sent, BOTH, routes(s, r)) for r in range(FAN)] for s in (10, 12)]
+            pieces = [a + b for a, b in zip(*ways)]
         else:
             pieces = [lax.ppermute(sent, BOTH, routes(step, r)) for r in range(FAN)]
         return one_step(step, green, trace, before, sent, pieces)
 
-    slab = traces.shape[1]
-
     def joined(done):
-        held = jnp.where(upper, done[slab:], done[:slab])
-        got = lax.ppermute(jnp.where(upper, done[:slab], done[slab:]), BOTH, PAIRS)
+        held = done[:slab]
+        got = jnp.concatenate(swapped(thirds(done[slab:]), ALL), 0)
         left = jnp.where(upper, got, held)
         right = jnp.where(upper, held, got)
         real = jnp.concatenate([left[:, :half], right[:, :half]], 1)
@@ -337,11 +333,10 @@
     first, sent = trace, trace.astype(jnp.bfloat16)
     for step in range(1, HALF):
         if step == SWAP:
-            down_later, up_later, sent = lax.optimization_barrier((green_down, green_up, sent))
-            own_second = jnp.where(low, up_later[0], down_later[0])
-            other_second = lax.ppermute(own_second, BOTH, PAIRS)
+            given, sent = lax.optimization_barrier((given, sent))
+            others_second = swapped(given, ALL)
         if step == HALF - 1:
-            green_second = loaded(info, own_second, other_second)
+            green_second = loaded(info, up, down, others_second)
             green_first, green_second = lax.optimization_barrier((green_first, green_second))
         first, sent = advance(step, green_first, first, sent)
     near = joined(first)
@@ -349,9 +344,9 @@
     for step in range(HALF, LAYERS):
         second, sent = advance(step, green_second, second, sent)
     far = joined(second)
-    down = jnp.where(low, near, far)
-    up = jnp.where(low, far, near)
-    return (down[None], up[None])
+    down_trace = jnp.where(low, near, far)
+    up_trace = jnp.where(low, far, near)
+    return (down_trace[None], up_trace[None])
 
 
 def solution(mesh):

time: 234 us -> 255 us (1.090)
  the two profiles are of different devices: /device:TPU:31 before, /device:TPU:8 now
where the time goes in v3:
time: 255 us; the launch traced here: 254 us
  waiting for transfers between devices  121 us (47%)
  starting transfers between devices  109 us (43%)
  Pallas kernels  11.8 us (5%)
  other arithmetic  7.54 us (3%)
  local copies, waits for them, and re-layouts  2.82 us (1%)
    ppermute x56, waiting for transfers between devices, advance(): pieces = [lax.ppermute(sent, BOTH, routes(step, r)) for r in range(FAN)]  84.4 us
    ppermute x56, starting transfers between devices, advance(): pieces = [lax.ppermute(sent, BOTH, routes(step, r)) for r in range(FAN)]  77.1 us
    ppermute x15, waiting for transfers between devices, swapped(): lax.ppermute(x, BOTH, swap_pairs(k, layers))  26.7 us
    ppermute x15, starting transfers between devices, swapped(): lax.ppermute(x, BOTH, swap_pairs(k, layers))  16.1 us
    ppermute x8, starting transfers between devices, advance(): lax.ppermute(sent, BOTH, routes(s, r))  7.82 us
    pallas_call x2, Pallas kernels, loaded(): pl.pallas_call(load_kernel, out_shape=jax.ShapeDtypeStruct((FAN, 4 * slab...  7.23 us
    ppermute x1, starting transfers between devices, padded_2(): lax.ppermute(lax.slice_in_dim(block, 0, width, axis=dim), axis, backward)  5.83 us
    ppermute x1, waiting for transfers between devices, padded_2(): low = lax.ppermute(last, axis, forward)  5.52 us
  transfers between devices with their start and end apart: 81, of which 17 were waited for; matrix products, arithmetic and copies ran while one was open for 1% of the time, Pallas kernels for 4%

profile of v3, /device:TPU:8, one launch (start us, length us, event | category | flops | bytes accessed | tf_op | source)
XLA Modules:
  0.0 253.7 jit_solution(11795613886450535536)
XLA Ops:
  0.7 3.9 %slice_select_fusion = (bf16[2,64,3072]{2,1,0:T(8,128)(2,1)}, bf16[2,64,3072]{2,1,0:T(8,128)(2,1)}, bf16[2,64,3072]{2,1,0:T(8,128)(2,1)}) fusion(bf16[2,192,3072]{2,1,0:T(8,128)(2,1)} %bitcast.24, bf16[2,192,3072]{2,1,0:T(8,128)(2,1)} %bitcast.28, pred[]{:T(512)S(6)} %lt.17), kind=kLoop, calls=%fused_computation | loop fusion | flops 1179648 | bytes 7077889 | tf_op jit(solution)/shard_map/jit(_where)/select_n | solution.py:297
  4.6 0.7 collective-permute-start
  5.3 1.6 collective-permute-start.1
  6.8 1.6 collective-permute-start.2
  8.4 5.8 %collective-permute-start.4 = (bf16[3,4,128]{2,1,0:T(4,128)(2,1)S(1)}, bf16[3,4,128]{2,1,0:T(4,128)(2,1)S(1)}, u32[]{:S(2)}, u32[]{:S(2)}) collective-permute-start(bf16[3,4,128]{2,1,0:T(4,128)(2,1)S(1)} %get-tuple-element.122), channel_id=1, source_target_pairs={{1,0},{2,1},{3,2},{4,3},{5,4},{6,5},{7,6},{9,8},{10,9},{11,10},{12... | collective-permute-start | bytes 9224 | tf_op jit(solution)/shard_map/ppermute | solution.py:72
  14.3 1.9 collective-permute-start.3
  16.5 5.5 %collective-permute-done.3 = bf16[3,4,128]{2,1,0:T(4,128)(2,1)S(1)} collective-permute-done((bf16[3,4,128]{2,1,0:T(4,128)(2,1)S(1)}, bf16[3,4,128]{2,1,0:T(4,128)(2,1)S(1)}, u32[]{:S(2)}, u32[]{:S(2)}) %collective-permute-start.3) | collective-permute-done | bytes 3104 | tf_op jit(solution)/shard_map/ppermute | solution.py:71
  24.0 0.7 dynamic-slice_bitcast_fusion
  24.7 4.4 %collective-permute-done.7 = f32[64,128]{1,0:T(8,128)S(1)} collective-permute-done((f32[64,128]{1,0:T(8,128)S(1)}, f32[64,128]{1,0:T(8,128)S(1)}, u32[]{:S(2)}, u32[]{:S(2)}) %collective-permute-start.7) | collective-permute-done | bytes 32800 | tf_op jit(solution)/shard_map/ppermute | solution.py:295
  29.2 4.1 %collective-permute-done.5 = f32[64,128]{1,0:T(8,128)S(1)} collective-permute-done((f32[64,128]{1,0:T(8,128)S(1)}, f32[64,128]{1,0:T(8,128)S(1)}, u32[]{:S(2)}, u32[]{:S(2)}) %collective-permute-start.5) | collective-permute-done | bytes 32800 | tf_op jit(solution)/shard_map/ppermute | solution.py:295
  33.3 2.8 %collective-permute-start.8 = (bf16[384,128]{1,0:T(8,128)(2,1)S(1)}, bf16[384,128]{1,0:T(8,128)(2,1)S(1)}, u32[]{:S(2)}, u32[]{:S(2)}) collective-permute-start(bf16[384,128]{1,0:T(8,128)(2,1)S(1)} %fusion.27.sent), channel_id=1, source_target_pairs={{0,10},{1,11},{2,8},{3,9},{4,14},{5,15},{6,12},{7,13},{120,114},{1... | collective-permute-start | bytes 294920 | tf_op jit(solution)/shard_map/ppermute | solution.py:321
  36.1 1.3 collective-permute-start.9
  37.4 1.3 collective-permute-start.10
  38.7 1.3 collective-permute-start.11
  40.1 1.7 copy-done.1
  41.8 4.2 %shard_map.68.green = bf16[4,768,768]{2,1,0:T(8,128)(2,1)S(1)} custom-call(s32[6]{0:T(128)S(1)} %pad_add_fusion.info, bf16[2,192,3072]{2,1,0:T(8,128)(2,1)S(1)} %bitcast.29, bf16[2,192,3072]{2,1,0:T(8,128)(2,1)S(1)} %bitcast.25, bf16[2,64,3072]{2,1,0:T(8,128)(2,1)S(1)} %collective-permute-done.refs_0_, bf16[2,64,3072]{2,1,0:T(8,128)(2,1)} %collective-permute-done.1.refs_1_, ...), custom_call_target="tpu_custom_call" | custom-call | bytes 9437184 | tf_op jit(solution)/shard_map/pallas_call | solution.py:170
  46.1 0.7 collective-permute-start.13
  46.8 0.7 collective-permute-start.14
  47.5 0.7 collective-permute-start.12
  48.2 0.7 collective-permute-start.15
  49.0 0.7 collective-permute-start.17
  53.8 0.7 collective-permute-start.23
  54.7 29.5 %collective-permute-start.24 = (bf16[384,128]{1,0:T(8,128)(2,1)S(1)}, bf16[384,128]{1,0:T(8,128)(2,1)S(1)}, u32[]{:S(2)}, u32[]{:S(2)}) collective-permute-start(bf16[384,128]{1,0:T(8,128)(2,1)S(1)} %get-tuple-element.58.sent), channel_id=1, source_target_pairs={{0,10},{1,11},{2,8},{3,9},{4,14},{5,15},{6,12},{7,13},{120,114},{1... | collective-permute-start | bytes 294920 | tf_op jit(solution)/shard_map/ppermute | solution.py:321
  84.1 1.4 collective-permute-start.25
  85.5 1.3 collective-permute-start.26
  86.8 1.3 collective-permute-start.27
  89.1 1.2 collective-permute-start.28
  90.8 1.7 collective-permute-start.30
  96.2 0.7 collective-permute-start.37
  96.9 12.4 %collective-permute-done.28.refs_0_ = bf16[2,64,3072]{2,1,0:T(8,128)(2,1)S(1)} collective-permute-done((bf16[2,64,3072]{2,1,0:T(8,128)(2,1)S(1)}, bf16[2,64,3072]{2,1,0:T(8,128)(2,1)S(1)}, u32[]{:S(2)}, u32[]{:S(2)}) %collective-permute-start.28) | collective-permute-done | bytes 786464 | tf_op jit(solution)/shard_map/ppermute | solution.py:295
  110.0 0.7 collective-permute-done.29.refs_1_
  111.9 3.0 %shard_map.84.green = bf16[4,768,768]{2,1,0:T(8,128)(2,1)S(1)} custom-call(s32[6]{0:T(128)S(1)} %pad_add_fusion.info, bf16[2,192,3072]{2,1,0:T(8,128)(2,1)S(1)} %bitcast.27, bf16[2,192,3072]{2,1,0:T(8,128)(2,1)S(1)} %bitcast.31, bf16[2,64,3072]{2,1,0:T(8,128)(2,1)S(1)} %collective-permute-done.28.refs_0_, ...), custom_call_target="tpu_custom_call" | custom-call | bytes 9437184 | tf_op jit(solution)/shard_map/pallas_call | solution.py:170
  115.7 1.3 collective-permute-start.43
  117.7 1.3 collective-permute-start.45
  119.7 1.3 collective-permute-start.47
  121.0 2.2 collective-permute-done.43
  123.8 1.3 collective-permute-start.49
  125.8 0.7 collective-permute-done.47
  127.8 0.7 collective-permute-start.51
  129.8 1.2 collective-permute-start.39
  131.0 0.9 collective-permute-start.40
  134.0 0.8 collective-permute-done.39
  135.5 1.6 collective-permute-start.41
  137.2 0.7 collective-permute-start.58
  140.1 1.3 collective-permute-start.62
  141.4 1.3 collective-permute-start.63
  142.7 1.3 collective-permute-start.64
  144.0 1.3 collective-permute-start.65
  145.3 8.1 %collective-permute-done.63.refs_0_ = bf16[384,128]{1,0:T(8,128)(2,1)S(1)} collective-permute-done((bf16[384,128]{1,0:T(8,128)(2,1)S(1)}, bf16[384,128]{1,0:T(8,128)(2,1)S(1)}, u32[]{:S(2)}, u32[]{:S(2)}) %collective-permute-start.63) | collective-permute-done | bytes 98336 | tf_op jit(solution)/shard_map/ppermute | solution.py:321
  157.0 0.7 collective-permute-start.71
  159.5 1.3 collective-permute-start.74
  160.8 1.3 collective-permute-start.75
  162.1 1.3 collective-permute-start.76
  163.4 1.3 collective-permute-start.77
  164.8 75.4 %collective-permute-done.75.refs_0_ = bf16[384,128]{1,0:T(8,128)(2,1)S(1)} collective-permute-done((bf16[384,128]{1,0:T(8,128)(2,1)S(1)}, bf16[384,128]{1,0:T(8,128)(2,1)S(1)}, u32[]{:S(2)}, u32[]{:S(2)}) %collective-permute-start.75) | collective-permute-done | bytes 98336 | tf_op jit(solution)/shard_map/ppermute | solution.py:321
  240.4 1.1 shard_map.112.refs_1_
  241.5 0.7 shard_map.113.earlier
  242.2 1.5 shard_map.114
  243.8 2.0 collective-permute-start.78
  245.8 1.7 collective-permute-start.79
  247.5 1.4 collective-permute-start.80
  248.9 0.9 collective-permute-done.79
  249.8 2.8 %collective-permute-done.80 = f32[64,128]{1,0:T(8,128)S(1)} collective-permute-done((f32[64,128]{1,0:T(8,128)S(1)}, f32[64,128]{1,0:T(8,128)S(1)}, u32[]{:S(2)}, u32[]{:S(2)}) %collective-permute-start.80) | collective-permute-done | bytes 32800 | tf_op jit(solution)/shard_map/ppermute | solution.py:295
  253.0 0.8 fusion.15
  (207 shorter events, 30.2 us)
Async XLA Ops:
  4.6 32.9 %collective-permute-start = (bf16[2,64,3072]{2,1,0:T(8,128)(2,1)}, bf16[2,64,3072]{2,1,0:T(8,128)(2,1)S(1)}, u32[]{:S(2)}, u32[]{:S(2)}) collective-permute-start(bf16[2,64,3072]{2,1,0:T(8,128)(2,1)} %get-tuple-element.44), channel_id=1, source_target_pairs={{8,12},{9,13},{10,14},{11,15},{12,8},{13,9},{14,10},{15,11},{16,20... | collective-permute-start | bytes 2359304 | tf_op jit(solution)/shard_map/ppermute | solution.py:295
  5.3 33.5 %collective-permute-start.1 = (bf16[2,64,3072]{2,1,0:T(8,128)(2,1)}, bf16[2,64,3072]{2,1,0:T(8,128)(2,1)}, u32[]{:S(2)}, u32[]{:S(2)}) collective-permute-start(bf16[2,64,3072]{2,1,0:T(8,128)(2,1)} %get-tuple-element.45), channel_id=1, source_target_pairs={{8,9},{9,8},{10,11},{11,10},{12,13},{13,12},{14,15},{15,14},{16,17... | collective-permute-start | bytes 2359304 | tf_op jit(solution)/shard_map/ppermute | solution.py:295
  6.8 33.2 %collective-permute-start.2 = (bf16[2,64,3072]{2,1,0:T(8,128)(2,1)}, bf16[2,64,3072]{2,1,0:T(8,128)(2,1)}, u32[]{:S(2)}, u32[]{:S(2)}) collective-permute-start(bf16[2,64,3072]{2,1,0:T(8,128)(2,1)} %get-tuple-element.46), channel_id=1, source_target_pairs={{8,11},{9,10},{10,9},{11,8},{12,15},{13,14},{14,13},{15,12},{16,19... | collective-permute-start | bytes 2359304 | tf_op jit(solution)/shard_map/ppermute | solution.py:295
  8.4 8.0 %collective-permute-start.4 = (bf16[3,4,128]{2,1,0:T(4,128)(2,1)S(1)}, bf16[3,4,128]{2,1,0:T(4,128)(2,1)S(1)}, u32[]{:S(2)}, u32[]{:S(2)}) collective-permute-start(bf16[3,4,128]{2,1,0:T(4,128)(2,1)S(1)} %get-tuple-element.122), channel_id=1, source_target_pairs={{1,0},{2,1},{3,2},{4,3},{5,4},{6,5},{7,6},{9,8},{10,9},{11,10},{12... | collective-permute-start | bytes 9224 | tf_op jit(solution)/shard_map/ppermute | solution.py:72
  14.3 7.7 %collective-permute-start.3 = (bf16[3,4,128]{2,1,0:T(4,128)(2,1)S(1)}, bf16[3,4,128]{2,1,0:T(4,128)(2,1)S(1)}, u32[]{:S(2)}, u32[]{:S(2)}) collective-permute-start(bf16[3,4,128]{2,1,0:T(4,128)(2,1)S(1)} %get-tuple-element.121), channel_id=1, source_target_pairs={{0,1},{1,2},{2,3},{3,4},{4,5},{5,6},{6,7},{8,9},{9,10},{10,11},{11... | collective-permute-start | bytes 9224 | tf_op jit(solution)/shard_map/ppermute | solution.py:71
  23.9 5.2 %collective-permute-start.7 = (f32[64,128]{1,0:T(8,128)S(1)}, f32[64,128]{1,0:T(8,128)S(1)}, u32[]{:S(2)}, u32[]{:S(2)}) collective-permute-start(f32[64,128]{1,0:T(8,128)S(1)} %get-tuple-element.132), channel_id=1, source_target_pairs={{0,3},{1,2},{2,1},{3,0},{4,7},{5,6},{6,5},{7,4},{8,11},{9,10},{10,... | collective-permute-start | bytes 98312 | tf_op jit(solution)/shard_map/ppermute | solution.py:295
  24.7 4.5 %collective-permute-start.6 = (f32[64,128]{1,0:T(8,128)S(1)}, f32[64,128]{1,0:T(8,128)S(1)}, u32[]{:S(2)}, u32[]{:S(2)}) collective-permute-start(f32[64,128]{1,0:T(8,128)S(1)} %get-tuple-element.133), channel_id=1, source_target_pairs={{0,1},{1,0},{2,3},{3,2},{4,5},{5,4},{6,7},{7,6},{8,9},{9,8},{10,11... | collective-permute-start | bytes 98312 | tf_op jit(solution)/shard_map/ppermute | solution.py:295
  29.1 4.2 %collective-permute-start.5 = (f32[64,128]{1,0:T(8,128)S(1)}, f32[64,128]{1,0:T(8,128)S(1)}, u32[]{:S(2)}, u32[]{:S(2)}) collective-permute-start(f32[64,128]{1,0:T(8,128)S(1)} %get-tuple-element.131), channel_id=1, source_target_pairs={{0,4},{1,5},{2,6},{3,7},{4,0},{5,1},{6,2},{7,3},{8,12},{9,13},{10,... | collective-permute-start | bytes 98312 | tf_op jit(solution)/shard_map/ppermute | solution.py:295
  33.3 12.7 %collective-permute-start.8 = (bf16[384,128]{1,0:T(8,128)(2,1)S(1)}, bf16[384,128]{1,0:T(8,128)(2,1)S(1)}, u32[]{:S(2)}, u32[]{:S(2)}) collective-permute-start(bf16[384,128]{1,0:T(8,128)(2,1)S(1)} %fusion.27.sent), channel_id=1, source_target_pairs={{0,10},{1,11},{2,8},{3,9},{4,14},{5,15},{6,12},{7,13},{120,114},{1... | collective-permute-start | bytes 294920 | tf_op jit(solution)/shard_map/ppermute | solution.py:321
  36.1 9.9 %collective-permute-start.9 = (bf16[384,128]{1,0:T(8,128)(2,1)S(1)}, bf16[384,128]{1,0:T(8,128)(2,1)S(1)}, u32[]{:S(2)}, u32[]{:S(2)}) collective-permute-start(bf16[384,128]{1,0:T(8,128)(2,1)S(1)} %fusion.27.sent), channel_id=1, source_target_pairs={{0,15},{1,14},{2,13},{3,12},{4,11},{5,10},{6,9},{7,8},{120,119},{1... | collective-permute-start | bytes 294920 | tf_op jit(solution)/shard_map/ppermute | solution.py:321
  37.4 8.6 %collective-permute-start.10 = (bf16[384,128]{1,0:T(8,128)(2,1)S(1)}, bf16[384,128]{1,0:T(8,128)(2,1)S(1)}, u32[]{:S(2)}, u32[]{:S(2)}) collective-permute-start(bf16[384,128]{1,0:T(8,128)(2,1)S(1)} %fusion.27.sent), channel_id=1, source_target_pairs={{0,13},{1,12},{2,15},{3,14},{4,9},{5,8},{6,11},{7,10},{120,117},{1... | collective-permute-start | bytes 294920 | tf_op jit(solution)/shard_map/ppermute | solution.py:321
  38.7 7.3 %collective-permute-start.11 = (bf16[384,128]{1,0:T(8,128)(2,1)S(1)}, bf16[384,128]{1,0:T(8,128)(2,1)S(1)}, u32[]{:S(2)}, u32[]{:S(2)}) collective-permute-start(bf16[384,128]{1,0:T(8,128)(2,1)S(1)} %fusion.27.sent), channel_id=1, source_target_pairs={{0,8},{1,9},{2,10},{3,11},{4,12},{5,13},{6,14},{7,15},{120,112},{1... | collective-permute-start | bytes 294920 | tf_op jit(solution)/shard_map/ppermute | solution.py:321
  46.1 2.7 %collective-permute-start.13 = (bf16[384,128]{1,0:T(8,128)(2,1)S(1)}, bf16[384,128]{1,0:T(8,128)(2,1)S(1)}, u32[]{:S(2)}, u32[]{:S(2)}) collective-permute-start(bf16[384,128]{1,0:T(8,128)(2,1)S(1)} %get-tuple-element.52.sent), channel_id=1, source_target_pairs={{8,23},{9,22},{10,21},{11,20},{12,19},{13,18},{14,17},{15,16},{112... | collective-permute-start | bytes 294920 | tf_op jit(solution)/shard_map/ppermute | solution.py:321
  46.8 2.0 collective-permute-start.14
  49.0 2.7 %collective-permute-start.17 = (bf16[384,128]{1,0:T(8,128)(2,1)S(1)}, bf16[384,128]{1,0:T(8,128)(2,1)S(1)}, u32[]{:S(2)}, u32[]{:S(2)}) collective-permute-start(bf16[384,128]{1,0:T(8,128)(2,1)S(1)} %get-tuple-element.54.sent), channel_id=1, source_target_pairs={{16,31},{17,30},{18,29},{19,28},{20,27},{21,26},{22,25},{23,24},{1... | collective-permute-start | bytes 294920 | tf_op jit(solution)/shard_map/ppermute | solution.py:321
  49.6 2.0 collective-permute-start.18
  51.8 2.7 %collective-permute-start.21 = (bf16[384,128]{1,0:T(8,128)(2,1)S(1)}, bf16[384,128]{1,0:T(8,128)(2,1)S(1)}, u32[]{:S(2)}, u32[]{:S(2)}) collective-permute-start(bf16[384,128]{1,0:T(8,128)(2,1)S(1)} %get-tuple-element.56.sent), channel_id=1, source_target_pairs={{24,39},{25,38},{26,37},{27,36},{28,35},{29,34},{30,33},{31,32},{9... | collective-permute-start | bytes 294920 | tf_op jit(solution)/shard_map/ppermute | solution.py:321
  54.7 34.4 %collective-permute-start.24 = (bf16[384,128]{1,0:T(8,128)(2,1)S(1)}, bf16[384,128]{1,0:T(8,128)(2,1)S(1)}, u32[]{:S(2)}, u32[]{:S(2)}) collective-permute-start(bf16[384,128]{1,0:T(8,128)(2,1)S(1)} %get-tuple-element.58.sent), channel_id=1, source_target_pairs={{0,10},{1,11},{2,8},{3,9},{4,14},{5,15},{6,12},{7,13},{120,114},{1... | collective-permute-start | bytes 294920 | tf_op jit(solution)/shard_map/ppermute | solution.py:321
  84.1 4.4 %collective-permute-start.25 = (bf16[384,128]{1,0:T(8,128)(2,1)S(1)}, bf16[384,128]{1,0:T(8,128)(2,1)S(1)}, u32[]{:S(2)}, u32[]{:S(2)}) collective-permute-start(bf16[384,128]{1,0:T(8,128)(2,1)S(1)} %get-tuple-element.58.sent), channel_id=1, source_target_pairs={{0,15},{1,14},{2,13},{3,12},{4,11},{5,10},{6,9},{7,8},{120,119},{1... | collective-permute-start | bytes 294920 | tf_op jit(solution)/shard_map/ppermute | solution.py:321
  85.5 3.5 %collective-permute-start.26 = (bf16[384,128]{1,0:T(8,128)(2,1)S(1)}, bf16[384,128]{1,0:T(8,128)(2,1)S(1)}, u32[]{:S(2)}, u32[]{:S(2)}) collective-permute-start(bf16[384,128]{1,0:T(8,128)(2,1)S(1)} %get-tuple-element.58.sent), channel_id=1, source_target_pairs={{0,13},{1,12},{2,15},{3,14},{4,9},{5,8},{6,11},{7,10},{120,117},{1... | collective-permute-start | bytes 294920 | tf_op jit(solution)/shard_map/ppermute | solution.py:321
  86.8 2.2 collective-permute-start.27
  89.1 20.2 %collective-permute-start.28 = (bf16[2,64,3072]{2,1,0:T(8,128)(2,1)S(1)}, bf16[2,64,3072]{2,1,0:T(8,128)(2,1)S(1)}, u32[]{:S(2)}, u32[]{:S(2)}) collective-permute-start(bf16[2,64,3072]{2,1,0:T(8,128)(2,1)S(1)} %get-tuple-element.60), channel_id=1, source_target_pairs={{0,4},{1,5},{2,6},{3,7},{4,0},{5,1},{6,2},{7,3},{8,12},{9,13},{10,... | collective-permute-start | bytes 2359304 | tf_op jit(solution)/shard_map/ppermute | solution.py:295
  90.3 20.4 %collective-permute-start.29 = (bf16[2,64,3072]{2,1,0:T(8,128)(2,1)S(1)}, bf16[2,64,3072]{2,1,0:T(8,128)(2,1)S(1)}, u32[]{:S(2)}, u32[]{:S(2)}) collective-permute-start(bf16[2,64,3072]{2,1,0:T(8,128)(2,1)S(1)} %get-tuple-element.61), channel_id=1, source_target_pairs={{0,1},{1,0},{2,3},{3,2},{4,5},{5,4},{6,7},{7,6},{8,9},{9,8},{10,11... | collective-permute-start | bytes 2359304 | tf_op jit(solution)/shard_map/ppermute | solution.py:295
  90.8 21.1 %collective-permute-start.30 = (bf16[2,64,3072]{2,1,0:T(8,128)(2,1)S(1)}, bf16[2,64,3072]{2,1,0:T(8,128)(2,1)S(1)}, u32[]{:S(2)}, u32[]{:S(2)}) collective-permute-start(bf16[2,64,3072]{2,1,0:T(8,128)(2,1)S(1)} %get-tuple-element.62), channel_id=1, source_target_pairs={{0,3},{1,2},{2,1},{3,0},{4,7},{5,6},{6,5},{7,4},{8,11},{9,10},{10,... | collective-permute-start | bytes 2359304 | tf_op jit(solution)/shard_map/ppermute | solution.py:295
  95.5 19.4 %collective-permute-start.36 = (bf16[384,128]{1,0:T(8,128)(2,1)S(1)}, bf16[384,128]{1,0:T(8,128)(2,1)S(1)}, u32[]{:S(2)}, u32[]{:S(2)}) collective-permute-start(bf16[384,128]{1,0:T(8,128)(2,1)S(1)} %get-tuple-element.67.sent), channel_id=1, source_target_pairs={{16,31},{17,30},{18,29},{19,28},{20,27},{21,26},{22,25},{23,24},{1... | collective-permute-start | bytes 294920 | tf_op jit(solution)/shard_map/ppermute | solution.py:321
  96.2 18.7 %collective-permute-start.37 = (bf16[384,128]{1,0:T(8,128)(2,1)S(1)}, bf16[384,128]{1,0:T(8,128)(2,1)S(1)}, u32[]{:S(2)}, u32[]{:S(2)}) collective-permute-start(bf16[384,128]{1,0:T(8,128)(2,1)S(1)} %get-tuple-element.67.sent), channel_id=1, source_target_pairs={{16,29},{17,28},{18,31},{19,30},{20,25},{21,24},{22,27},{23,26},{1... | collective-permute-start | bytes 294920 | tf_op jit(solution)/shard_map/ppermute | solution.py:321
  109.3 5.6 %collective-permute-start.35 = (bf16[384,128]{1,0:T(8,128)(2,1)S(1)}, bf16[384,128]{1,0:T(8,128)(2,1)S(1)}, u32[]{:S(2)}, u32[]{:S(2)}) collective-permute-start(bf16[384,128]{1,0:T(8,128)(2,1)S(1)} %get-tuple-element.67.sent), channel_id=1, source_target_pairs={{16,26},{17,27},{18,24},{19,25},{20,30},{21,31},{22,28},{23,29},{1... | collective-permute-start | bytes 294920 | tf_op jit(solution)/shard_map/ppermute | solution.py:321
  110.7 4.3 %collective-permute-start.38 = (bf16[384,128]{1,0:T(8,128)(2,1)S(1)}, bf16[384,128]{1,0:T(8,128)(2,1)S(1)}, u32[]{:S(2)}, u32[]{:S(2)}) collective-permute-start(bf16[384,128]{1,0:T(8,128)(2,1)S(1)} %get-tuple-element.67.sent), channel_id=1, source_target_pairs={{16,24},{17,25},{18,26},{19,27},{20,28},{21,29},{22,30},{23,31},{1... | collective-permute-start | bytes 294920 | tf_op jit(solution)/shard_map/ppermute | solution.py:321
  115.0 4.6 %collective-permute-start.42 = (bf16[384,128]{1,0:T(8,128)(2,1)S(1)}, bf16[384,128]{1,0:T(8,128)(2,1)S(1)}, u32[]{:S(2)}, u32[]{:S(2)}) collective-permute-start(bf16[384,128]{1,0:T(8,128)(2,1)S(1)} %get-tuple-element.70.sent), channel_id=1, source_target_pairs={{72,82},{73,83},{74,80},{75,81},{76,86},{77,87},{78,84},{79,85},{4... | collective-permute-start | bytes 294920 | tf_op jit(solution)/shard_map/ppermute | solution.py:318
  115.7 7.4 %collective-permute-start.43 = (bf16[384,128]{1,0:T(8,128)(2,1)S(1)}, bf16[384,128]{1,0:T(8,128)(2,1)S(1)}, u32[]{:S(2)}, u32[]{:S(2)}) collective-permute-start(bf16[384,128]{1,0:T(8,128)(2,1)S(1)} %get-tuple-element.70.sent), channel_id=1, source_target_pairs={{88,98},{89,99},{90,96},{91,97},{92,102},{93,103},{94,100},{95,101... | collective-permute-start | bytes 294920 | tf_op jit(solution)/shard_map/ppermute | solution.py:318
  117.0 6.8 %collective-permute-start.44 = (bf16[384,128]{1,0:T(8,128)(2,1)S(1)}, bf16[384,128]{1,0:T(8,128)(2,1)S(1)}, u32[]{:S(2)}, u32[]{:S(2)}) collective-permute-start(bf16[384,128]{1,0:T(8,128)(2,1)S(1)} %get-tuple-element.70.sent), channel_id=1, source_target_pairs={{72,87},{73,86},{74,85},{75,84},{76,83},{77,82},{78,81},{79,80},{4... | collective-permute-start | bytes 294920 | tf_op jit(solution)/shard_map/ppermute | solution.py:318
  117.7 8.0 %collective-permute-start.45 = (bf16[384,128]{1,0:T(8,128)(2,1)S(1)}, bf16[384,128]{1,0:T(8,128)(2,1)S(1)}, u32[]{:S(2)}, u32[]{:S(2)}) collective-permute-start(bf16[384,128]{1,0:T(8,128)(2,1)S(1)} %get-tuple-element.70.sent), channel_id=1, source_target_pairs={{88,103},{89,102},{90,101},{91,100},{92,99},{93,98},{94,97},{95,96... | collective-permute-start | bytes 294920 | tf_op jit(solution)/shard_map/ppermute | solution.py:318
  119.0 6.8 %collective-permute-start.46 = (bf16[384,128]{1,0:T(8,128)(2,1)S(1)}, bf16[384,128]{1,0:T(8,128)(2,1)S(1)}, u32[]{:S(2)}, u32[]{:S(2)}) collective-permute-start(bf16[384,128]{1,0:T(8,128)(2,1)S(1)} %get-tuple-element.70.sent), channel_id=1, source_target_pairs={{72,85},{73,84},{74,87},{75,86},{76,81},{77,80},{78,83},{79,82},{4... | collective-permute-start | bytes 294920 | tf_op jit(solution)/shard_map/ppermute | solution.py:318
  119.7 6.8 %collective-permute-start.47 = (bf16[384,128]{1,0:T(8,128)(2,1)S(1)}, bf16[384,128]{1,0:T(8,128)(2,1)S(1)}, u32[]{:S(2)}, u32[]{:S(2)}) collective-permute-start(bf16[384,128]{1,0:T(8,128)(2,1)S(1)} %get-tuple-element.70.sent), channel_id=1, source_target_pairs={{88,101},{89,100},{90,103},{91,102},{92,97},{93,96},{94,99},{95,98... | collective-permute-start | bytes 294920 | tf_op jit(solution)/shard_map/ppermute | solution.py:318
  123.1 3.4 %collective-permute-start.48 = (bf16[384,128]{1,0:T(8,128)(2,1)S(1)}, bf16[384,128]{1,0:T(8,128)(2,1)S(1)}, u32[]{:S(2)}, u32[]{:S(2)}) collective-permute-start(bf16[384,128]{1,0:T(8,128)(2,1)S(1)} %get-tuple-element.70.sent), channel_id=1, source_target_pairs={{72,80},{73,81},{74,82},{75,83},{76,84},{77,85},{78,86},{79,87},{4... | collective-permute-start | bytes 294920 | tf_op jit(solution)/shard_map/ppermute | solution.py:318
  123.8 3.2 %collective-permute-start.49 = (bf16[384,128]{1,0:T(8,128)(2,1)S(1)}, bf16[384,128]{1,0:T(8,128)(2,1)S(1)}, u32[]{:S(2)}, u32[]{:S(2)}) collective-permute-start(bf16[384,128]{1,0:T(8,128)(2,1)S(1)} %get-tuple-element.70.sent), channel_id=1, source_target_pairs={{88,96},{89,97},{90,98},{91,99},{92,100},{93,101},{94,102},{95,103... | collective-permute-start | bytes 294920 | tf_op jit(solution)/shard_map/ppermute | solution.py:318
  127.1 4.8 %collective-permute-start.50 = (bf16[384,128]{1,0:T(8,128)(2,1)S(1)}, bf16[384,128]{1,0:T(8,128)(2,1)S(1)}, u32[]{:S(2)}, u32[]{:S(2)}) collective-permute-start(bf16[384,128]{1,0:T(8,128)(2,1)S(1)} %get-tuple-element.72.sent), channel_id=1, source_target_pairs={{24,34},{25,35},{26,32},{27,33},{28,38},{29,39},{30,36},{31,37},{9... | collective-permute-start | bytes 294920 | tf_op jit(solution)/shard_map/ppermute | solution.py:321
  127.8 3.2 %collective-permute-start.51 = (bf16[384,128]{1,0:T(8,128)(2,1)S(1)}, bf16[384,128]{1,0:T(8,128)(2,1)S(1)}, u32[]{:S(2)}, u32[]{:S(2)}) collective-permute-start(bf16[384,128]{1,0:T(8,128)(2,1)S(1)} %get-tuple-element.72.sent), channel_id=1, source_target_pairs={{24,39},{25,38},{26,37},{27,36},{28,35},{29,34},{30,33},{31,32},{9... | collective-permute-start | bytes 294920 | tf_op jit(solution)/shard_map/ppermute | solution.py:321
  128.4 3.5 %collective-permute-start.52 = (bf16[384,128]{1,0:T(8,128)(2,1)S(1)}, bf16[384,128]{1,0:T(8,128)(2,1)S(1)}, u32[]{:S(2)}, u32[]{:S(2)}) collective-permute-start(bf16[384,128]{1,0:T(8,128)(2,1)S(1)} %get-tuple-element.72.sent), channel_id=1, source_target_pairs={{24,37},{25,36},{26,39},{27,38},{28,33},{29,32},{30,35},{31,34},{9... | collective-permute-start | bytes 294920 | tf_op jit(solution)/shard_map/ppermute | solution.py:321
  129.1 2.8 %collective-permute-start.53 = (bf16[384,128]{1,0:T(8,128)(2,1)S(1)}, bf16[384,128]{1,0:T(8,128)(2,1)S(1)}, u32[]{:S(2)}, u32[]{:S(2)}) collective-permute-start(bf16[384,128]{1,0:T(8,128)(2,1)S(1)} %get-tuple-element.72.sent), channel_id=1, source_target_pairs={{24,32},{25,33},{26,34},{27,35},{28,36},{29,37},{30,38},{31,39},{9... | collective-permute-start | bytes 294920 | tf_op jit(solution)/shard_map/ppermute | solution.py:321
  129.8 5.0 %collective-permute-start.39 = (f32[64,128]{1,0:T(8,128)S(1)}, f32[64,128]{1,0:T(8,128)S(1)}, u32[]{:S(2)}, u32[]{:S(2)}) collective-permute-start(f32[64,128]{1,0:T(8,128)S(1)} %get-tuple-element.117), channel_id=1, source_target_pairs={{0,4},{1,5},{2,6},{3,7},{4,0},{5,1},{6,2},{7,3},{8,12},{9,13},{10,... | collective-permute-start | bytes 98312 | tf_op jit(solution)/shard_map/ppermute | solution.py:295
  131.0 8.2 %collective-permute-start.40 = (f32[64,128]{1,0:T(8,128)S(1)}, f32[64,128]{1,0:T(8,128)S(1)}, u32[]{:S(2)}, u32[]{:S(2)}) collective-permute-start(f32[64,128]{1,0:T(8,128)S(1)} %get-tuple-element.116), channel_id=1, source_target_pairs={{0,1},{1,0},{2,3},{3,2},{4,5},{5,4},{6,7},{7,6},{8,9},{9,8},{10,11... | collective-permute-start | bytes 98312 | tf_op jit(solution)/shard_map/ppermute | solution.py:295
  132.0 5.2 %collective-permute-start.54 = (bf16[384,128]{1,0:T(8,128)(2,1)S(1)}, bf16[384,128]{1,0:T(8,128)(2,1)S(1)}, u32[]{:S(2)}, u32[]{:S(2)}) collective-permute-start(bf16[384,128]{1,0:T(8,128)(2,1)S(1)} %get-tuple-element.74.sent), channel_id=1, source_target_pairs={{72,82},{73,83},{74,80},{75,81},{76,86},{77,87},{78,84},{79,85},{4... | collective-permute-start | bytes 294920 | tf_op jit(solution)/shard_map/ppermute | solution.py:321
  132.7 2.9 %collective-permute-start.55 = (bf16[384,128]{1,0:T(8,128)(2,1)S(1)}, bf16[384,128]{1,0:T(8,128)(2,1)S(1)}, u32[]{:S(2)}, u32[]{:S(2)}) collective-permute-start(bf16[384,128]{1,0:T(8,128)(2,1)S(1)} %get-tuple-element.74.sent), channel_id=1, source_target_pairs={{72,87},{73,86},{74,85},{75,84},{76,83},{77,82},{78,81},{79,80},{4... | collective-permute-start | bytes 294920 | tf_op jit(solution)/shard_map/ppermute | solution.py:321
  133.3 3.8 %collective-permute-start.56 = (bf16[384,128]{1,0:T(8,128)(2,1)S(1)}, bf16[384,128]{1,0:T(8,128)(2,1)S(1)}, u32[]{:S(2)}, u32[]{:S(2)}) collective-permute-start(bf16[384,128]{1,0:T(8,128)(2,1)S(1)} %get-tuple-element.74.sent), channel_id=1, source_target_pairs={{72,85},{73,84},{74,87},{75,86},{76,81},{77,80},{78,83},{79,82},{4... | collective-permute-start | bytes 294920 | tf_op jit(solution)/shard_map/ppermute | solution.py:321
  134.8 2.3 collective-permute-start.57
  135.5 9.7 %collective-permute-start.41 = (f32[64,128]{1,0:T(8,128)S(1)}, f32[64,128]{1,0:T(8,128)S(1)}, u32[]{:S(2)}, u32[]{:S(2)}) collective-permute-start(f32[64,128]{1,0:T(8,128)S(1)} %get-tuple-element.115), channel_id=1, source_target_pairs={{0,3},{1,2},{2,1},{3,0},{4,7},{5,6},{6,5},{7,4},{8,11},{9,10},{10,... | collective-permute-start | bytes 98312 | tf_op jit(solution)/shard_map/ppermute | solution.py:295
  137.2 2.8 %collective-permute-start.58 = (bf16[384,128]{1,0:T(8,128)(2,1)S(1)}, bf16[384,128]{1,0:T(8,128)(2,1)S(1)}, u32[]{:S(2)}, u32[]{:S(2)}) collective-permute-start(bf16[384,128]{1,0:T(8,128)(2,1)S(1)} %get-tuple-element.76.sent), channel_id=1, source_target_pairs={{16,26},{17,27},{18,24},{19,25},{20,30},{21,31},{22,28},{23,29},{1... | collective-permute-start | bytes 294920 | tf_op jit(solution)/shard_map/ppermute | solution.py:321
  137.9 2.1 collective-permute-start.59
  140.1 13.3 %collective-permute-start.62 = (bf16[384,128]{1,0:T(8,128)(2,1)S(1)}, bf16[384,128]{1,0:T(8,128)(2,1)S(1)}, u32[]{:S(2)}, u32[]{:S(2)}) collective-permute-start(bf16[384,128]{1,0:T(8,128)(2,1)S(1)} %get-tuple-element.78.sent), channel_id=1, source_target_pairs={{88,98},{89,99},{90,96},{91,97},{92,102},{93,103},{94,100},{95,101... | collective-permute-start | bytes 294920 | tf_op jit(solution)/shard_map/ppermute | solution.py:321
  141.4 12.0 %collective-permute-start.63 = (bf16[384,128]{1,0:T(8,128)(2,1)S(1)}, bf16[384,128]{1,0:T(8,128)(2,1)S(1)}, u32[]{:S(2)}, u32[]{:S(2)}) collective-permute-start(bf16[384,128]{1,0:T(8,128)(2,1)S(1)} %get-tuple-element.78.sent), channel_id=1, source_target_pairs={{88,103},{89,102},{90,101},{91,100},{92,99},{93,98},{94,97},{95,96... | collective-permute-start | bytes 294920 | tf_op jit(solution)/shard_map/ppermute | solution.py:321
  142.7 10.7 %collective-permute-start.64 = (bf16[384,128]{1,0:T(8,128)(2,1)S(1)}, bf16[384,128]{1,0:T(8,128)(2,1)S(1)}, u32[]{:S(2)}, u32[]{:S(2)}) collective-permute-start(bf16[384,128]{1,0:T(8,128)(2,1)S(1)} %get-tuple-element.78.sent), channel_id=1, source_target_pairs={{88,101},{89,100},{90,103},{91,102},{92,97},{93,96},{94,99},{95,98... | collective-permute-start | bytes 294920 | tf_op jit(solution)/shard_map/ppermute | solution.py:321
  144.0 9.5 %collective-permute-start.65 = (bf16[384,128]{1,0:T(8,128)(2,1)S(1)}, bf16[384,128]{1,0:T(8,128)(2,1)S(1)}, u32[]{:S(2)}, u32[]{:S(2)}) collective-permute-start(bf16[384,128]{1,0:T(8,128)(2,1)S(1)} %get-tuple-element.78.sent), channel_id=1, source_target_pairs={{88,96},{89,97},{90,98},{91,99},{92,100},{93,101},{94,102},{95,103... | collective-permute-start | bytes 294920 | tf_op jit(solution)/shard_map/ppermute | solution.py:321
  153.5 2.8 %collective-permute-start.66 = (bf16[384,128]{1,0:T(8,128)(2,1)S(1)}, bf16[384,128]{1,0:T(8,128)(2,1)S(1)}, u32[]{:S(2)}, u32[]{:S(2)}) collective-permute-start(bf16[384,128]{1,0:T(8,128)(2,1)S(1)} %get-tuple-element.80.sent), channel_id=1, source_target_pairs={{72,82},{73,83},{74,80},{75,81},{76,86},{77,87},{78,84},{79,85},{4... | collective-permute-start | bytes 294920 | tf_op jit(solution)/shard_map/ppermute | solution.py:321
  154.1 2.1 collective-permute-start.67
  156.3 2.9 %collective-permute-start.70 = (bf16[384,128]{1,0:T(8,128)(2,1)S(1)}, bf16[384,128]{1,0:T(8,128)(2,1)S(1)}, u32[]{:S(2)}, u32[]{:S(2)}) collective-permute-start(bf16[384,128]{1,0:T(8,128)(2,1)S(1)} %get-tuple-element.82.sent), channel_id=1, source_target_pairs={{24,34},{25,35},{26,32},{27,33},{28,38},{29,39},{30,36},{31,37},{9... | collective-permute-start | bytes 294920 | tf_op jit(solution)/shard_map/ppermute | solution.py:321
  157.0 2.1 collective-permute-start.71
  159.5 82.0 %collective-permute-start.74 = (bf16[384,128]{1,0:T(8,128)(2,1)S(1)}, bf16[384,128]{1,0:T(8,128)(2,1)S(1)}, u32[]{:S(2)}, u32[]{:S(2)}) collective-permute-start(bf16[384,128]{1,0:T(8,128)(2,1)S(1)} %get-tuple-element.84.sent), channel_id=1, source_target_pairs={{88,98},{89,99},{90,96},{91,97},{92,102},{93,103},{94,100},{95,101... | collective-permute-start | bytes 294920 | tf_op jit(solution)/shard_map/ppermute | solution.py:321
  160.8 79.4 %collective-permute-start.75 = (bf16[384,128]{1,0:T(8,128)(2,1)S(1)}, bf16[384,128]{1,0:T(8,128)(2,1)S(1)}, u32[]{:S(2)}, u32[]{:S(2)}) collective-permute-start(bf16[384,128]{1,0:T(8,128)(2,1)S(1)} %get-tuple-element.84.sent), channel_id=1, source_target_pairs={{88,103},{89,102},{90,101},{91,100},{92,99},{93,98},{94,97},{95,96... | collective-permute-start | bytes 294920 | tf_op jit(solution)/shard_map/ppermute | solution.py:321
  162.1 78.3 %collective-permute-start.76 = (bf16[384,128]{1,0:T(8,128)(2,1)S(1)}, bf16[384,128]{1,0:T(8,128)(2,1)S(1)}, u32[]{:S(2)}, u32[]{:S(2)}) collective-permute-start(bf16[384,128]{1,0:T(8,128)(2,1)S(1)} %get-tuple-element.84.sent), channel_id=1, source_target_pairs={{88,101},{89,100},{90,103},{91,102},{92,97},{93,96},{94,99},{95,98... | collective-permute-start | bytes 294920 | tf_op jit(solution)/shard_map/ppermute | solution.py:321
  163.4 78.8 %collective-permute-start.77 = (bf16[384,128]{1,0:T(8,128)(2,1)S(1)}, bf16[384,128]{1,0:T(8,128)(2,1)S(1)}, u32[]{:S(2)}, u32[]{:S(2)}) collective-permute-start(bf16[384,128]{1,0:T(8,128)(2,1)S(1)} %get-tuple-element.84.sent), channel_id=1, source_target_pairs={{88,96},{89,97},{90,98},{91,99},{92,100},{93,101},{94,102},{95,103... | collective-permute-start | bytes 294920 | tf_op jit(solution)/shard_map/ppermute | solution.py:321
  243.8 5.2 %collective-permute-start.78 = (f32[64,128]{1,0:T(8,128)S(1)}, f32[64,128]{1,0:T(8,128)S(1)}, u32[]{:S(2)}, u32[]{:S(2)}) collective-permute-start(f32[64,128]{1,0:T(8,128)S(1)} %get-tuple-element.120), channel_id=1, source_target_pairs={{0,4},{1,5},{2,6},{3,7},{4,0},{5,1},{6,2},{7,3},{8,12},{9,13},{10,... | collective-permute-start | bytes 98312 | tf_op jit(solution)/shard_map/ppermute | solution.py:295
  245.8 4.0 %collective-permute-start.79 = (f32[64,128]{1,0:T(8,128)S(1)}, f32[64,128]{1,0:T(8,128)S(1)}, u32[]{:S(2)}, u32[]{:S(2)}) collective-permute-start(f32[64,128]{1,0:T(8,128)S(1)} %get-tuple-element.119), channel_id=1, source_target_pairs={{0,1},{1,0},{2,3},{3,2},{4,5},{5,4},{6,7},{7,6},{8,9},{9,8},{10,11... | collective-permute-start | bytes 98312 | tf_op jit(solution)/shard_map/ppermute | solution.py:295
  247.5 5.1 %collective-permute-start.80 = (f32[64,128]{1,0:T(8,128)S(1)}, f32[64,128]{1,0:T(8,128)S(1)}, u32[]{:S(2)}, u32[]{:S(2)}) collective-permute-start(f32[64,128]{1,0:T(8,128)S(1)} %get-tuple-element.118), channel_id=1, source_target_pairs={{0,3},{1,2},{2,1},{3,0},{4,7},{5,6},{6,5},{7,4},{8,11},{9,10},{10,... | collective-permute-start | bytes 98312 | tf_op jit(solution)/shard_map/ppermute | solution.py:295
  (22 other events, 87.7 us)

commit v4 on v2

--- a/solution.py
+++ b/solution.py
@@ -14,9 +14,10 @@
 LATS = 8
 HALF = LAYERS // 2
 BOTH = ("layer", "lat")
-SHARED = ((1, 5), (2, 6), (3, 7, 11), (4, 9, 14), (10, 13), (12, 15))
+SHARED = ((1, 9), (2, 10), (3, 15), (4, 14), (5, 13), (6, 12), (7, 11))
+RIDERS = {(3, 15): (HALF - 1, HALF), (4, 14): (HALF, HALF - 1)}
 FAN = 4
-SWAP = 6
+SWAP = 7
 BATCHES = ((3, 1), (0,), (2,))
 
 
@@ -43,21 +44,11 @@
 def routes(step, r):
     steps = next(group for group in SHARED if step in group)
     edges = [edge for s in steps for edge in edges_of(s)]
+    if steps in RIDERS:
+        edges.append(RIDERS[steps])
     return [
         (src * LATS + j, dst * LATS + target_of(src, j, r)) for src, dst in edges for j in range(LATS)
     ]
-
-
-def spread(step, r):
-    return [
-        (dst * LATS + j, dst * LATS + target_of(src, j, r))
-        for src, dst in edges_of(step)
-        for j in range(LATS)
-    ]
-
-
-def straight(step):
-    return [(src * LATS + j, dst * LATS + j) for src, dst in edges_of(step) for j in range(LATS)]
 
 
 PAIRS = [(l * LATS + j, l * LATS + partner_of(l, j)) for l in range(LAYERS) for j in range(LATS)]
@@ -330,8 +321,9 @@
 
     def advance(step, green, before, sent):
         if step == HALF:
-            shifted = lax.ppermute(sent, BOTH, straight(step))
-            pieces = [lax.ppermute(shifted, BOTH, spread(step, r)) for r in range(FAN)]
+            ahead = [lax.ppermute(sent, BOTH, routes(3, r)) for r in range(FAN)]
+            back = [lax.ppermute(sent, BOTH, routes(4, r)) for r in range(FAN)]
+            pieces = [a + b for a, b in zip(ahead, back)]
         else:
             pieces = [lax.ppermute(sent, BOTH, routes(step, r)) for r in range(FAN)]
         return one_step(step, green, trace, before, sent, pieces)

time: 233 us -> 254 us (1.090)
  the two profiles are of different devices: /device:TPU:31 before, /device:TPU:1 now
where the time goes in v4:
time: 254 us; the launch traced here: 250 us
  waiting for transfers between devices  144 us (57%)
  starting transfers between devices  83.7 us (33%)
  Pallas kernels  13.6 us (5%)
  other arithmetic  5.53 us (2%)
    ppermute x56, waiting for transfers between devices, advance(): pieces = [lax.ppermute(sent, BOTH, routes(step, r)) for r in range(FAN)]  67.9 us
    ppermute x56, starting transfers between devices, advance(): pieces = [lax.ppermute(sent, BOTH, routes(step, r)) for r in range(FAN)]  57.7 us
    ppermute x1, waiting for transfers between devices, local(): other_outer = lax.ppermute(own_late, BOTH, OUTER_PAIRS)  24.8 us
    ppermute x4, waiting for transfers between devices, advance(): back = [lax.ppermute(sent, BOTH, routes(4, r)) for r in range(FAN)]  24.6 us
    ppermute x1, waiting for transfers between devices, local(): swapped = lax.ppermute(give, BOTH, PAIRS)  24.1 us
    pallas_call x2, Pallas kernels, loaded(): pl.pallas_call(load_kernel, out_shape=jax.ShapeDtypeStruct((FAN, 4 * slab...  6.96 us
    ppermute x4, starting transfers between devices, advance(): ahead = [lax.ppermute(sent, BOTH, routes(3, r)) for r in range(FAN)]  5.17 us
    ppermute x4, starting transfers between devices, advance(): back = [lax.ppermute(sent, BOTH, routes(4, r)) for r in range(FAN)]  5.17 us
  transfers between devices with their start and end apart: 72, of which 23 were waited for; matrix products, arithmetic and copies ran while one was open for 1% of the time, Pallas kernels for 4%

profile of v4, /device:TPU:1, one launch (start us, length us, event | category | flops | bytes accessed | tf_op | source)
XLA Modules:
  0.0 249.7 jit_solution(10148695885314814920)
XLA Ops:
  0.7 2.0 select_bitcast_fusion.1.own
  2.7 4.4 %collective-permute-start.1 = (bf16[3,4,128]{2,1,0:T(4,128)(2,1)S(1)}, bf16[3,4,128]{2,1,0:T(4,128)(2,1)S(1)}, u32[]{:S(2)}, u32[]{:S(2)}) collective-permute-start(bf16[3,4,128]{2,1,0:T(4,128)(2,1)S(1)} %get-tuple-element.105), channel_id=1, source_target_pairs={{0,1},{1,2},{2,3},{3,4},{4,5},{5,6},{6,7},{8,9},{9,10},{10,11},{11... | collective-permute-start | bytes 9224 | tf_op jit(solution)/shard_map/ppermute | solution.py:80
  7.1 1.3 collective-permute-start.2
  8.4 4.2 %collective-permute-start = (bf16[2,192,3072]{2,1,0:T(8,128)(2,1)S(1)}, bf16[2,192,3072]{2,1,0:T(8,128)(2,1)}, u32[]{:S(2)}, u32[]{:S(2)}) collective-permute-start(bf16[2,192,3072]{2,1,0:T(8,128)(2,1)S(1)} %select_bitcast_fusion.1.own), channel_id=1, source_target_pairs={{8,9},{9,8},{10,11},{11,10},{12,13},{13,12},{14,15},{15,14},{16,20... | collective-permute-start | bytes 7077896 | tf_op jit(solution)/shard_map/ppermute | solution.py:301
  15.7 24.1 %collective-permute-done.3 = f32[192,128]{1,0:T(8,128)S(1)} collective-permute-done((f32[192,128]{1,0:T(8,128)S(1)}, f32[192,128]{1,0:T(8,128)S(1)}, u32[]{:S(2)}, u32[]{:S(2)}) %collective-permute-start.3) | collective-permute-done | bytes 98336 | tf_op jit(solution)/shard_map/ppermute | solution.py:312
  39.9 1.3 collective-permute-start.5
  41.2 1.3 collective-permute-start.6
  42.5 1.3 collective-permute-start.4
  43.8 1.3 collective-permute-start.7
  45.1 4.1 %shard_map.68.green = bf16[4,768,768]{2,1,0:T(8,128)(2,1)S(1)} custom-call(s32[7]{0:T(128)S(1)} %pad_add_fusion.info, bf16[2,192,3072]{2,1,0:T(8,128)(2,1)S(1)} %select_bitcast_fusion.1.own, bf16[2,192,3072]{2,1,0:T(8,128)(2,1)} %collective-permute-done.refs_0_), custom_call_target="tpu_custom_call" | custom-call | bytes 9437184 | tf_op jit(solution)/shard_map/pallas_call | solution.py:177
  49.3 2.2 collective-permute-done.6.refs_1_
  54.2 1.3 collective-permute-start.10
  55.5 1.3 collective-permute-start.9
  56.8 1.3 collective-permute-start.8
  58.1 1.3 collective-permute-start.11
  59.7 1.3 collective-permute-done.11.refs_0_
  61.0 1.3 collective-permute-start.13
  62.3 1.3 collective-permute-start.14
  63.6 1.3 collective-permute-start.12
  64.9 1.3 collective-permute-start.15
  66.3 1.9 collective-permute-done.15.refs_0_
  68.2 1.3 collective-permute-start.17
  69.5 1.3 collective-permute-start.18
  70.8 1.3 collective-permute-start.16
  72.1 1.3 collective-permute-start.19
  73.4 3.6 %collective-permute-done.17.refs_0_ = bf16[384,128]{1,0:T(8,128)(2,1)S(1)} collective-permute-done((bf16[384,128]{1,0:T(8,128)(2,1)S(1)}, bf16[384,128]{1,0:T(8,128)(2,1)S(1)}, u32[]{:S(2)}, u32[]{:S(2)}) %collective-permute-start.17) | collective-permute-done | bytes 98336 | tf_op jit(solution)/shard_map/ppermute | solution.py:328
  77.1 1.8 collective-permute-done.18.refs_1_
  78.9 1.7 collective-permute-done.19.refs_0_
  87.8 2.1 collective-permute-start.28
  92.6 24.8 %collective-permute-done.28.refs_0_ = bf16[2,192,3072]{2,1,0:T(8,128)(2,1)S(1)} collective-permute-done((bf16[2,192,3072]{2,1,0:T(8,128)(2,1)S(1)}, bf16[2,192,3072]{2,1,0:T(8,128)(2,1)S(1)}, u32[]{:S(2)}, u32[]{:S(2)}) %collective-permute-start.28) | collective-permute-done | bytes 2359328 | tf_op jit(solution)/shard_map/ppermute | solution.py:346
  117.3 2.8 %shard_map.87.green = bf16[4,768,768]{2,1,0:T(8,128)(2,1)S(1)} custom-call(s32[7]{0:T(128)S(1)} %pad_add_fusion.info, bf16[2,192,3072]{2,1,0:T(8,128)(2,1)S(1)} %select_bitcast_fusion.own, bf16[2,192,3072]{2,1,0:T(8,128)(2,1)S(1)} %collective-permute-done.28.refs_0_, bf16[2,192,3072]{2,1,0:T(8,128)(2,1)S(1)} %collective-permute-done.29.refs_1_), custom_call_target="tpu_custom_call" | custom-call | bytes 9437184 | tf_op jit(solution)/shard_map/pallas_call | solution.py:177
  120.3 1.3 collective-permute-start.39
  121.6 1.3 collective-permute-start.40
  122.9 1.3 collective-permute-start.37
  124.2 1.3 collective-permute-start.38
  125.5 1.3 collective-permute-start.35
  126.8 1.3 collective-permute-start.36
  128.1 14.1 %collective-permute-done.40 = bf16[384,128]{1,0:T(8,128)(2,1)S(1)} collective-permute-done((bf16[384,128]{1,0:T(8,128)(2,1)S(1)}, bf16[384,128]{1,0:T(8,128)(2,1)S(1)}, u32[]{:S(2)}, u32[]{:S(2)}) %collective-permute-start.40) | collective-permute-done | bytes 98336 | tf_op jit(solution)/shard_map/ppermute | solution.py:325
  143.5 1.3 collective-permute-start.42
  144.9 6.4 %collective-permute-done.38 = bf16[384,128]{1,0:T(8,128)(2,1)S(1)} collective-permute-done((bf16[384,128]{1,0:T(8,128)(2,1)S(1)}, bf16[384,128]{1,0:T(8,128)(2,1)S(1)}, u32[]{:S(2)}, u32[]{:S(2)}) %collective-permute-start.38) | collective-permute-done | bytes 98336 | tf_op jit(solution)/shard_map/ppermute | solution.py:325
  151.7 3.9 %collective-permute-done.42 = bf16[384,128]{1,0:T(8,128)(2,1)S(1)} collective-permute-done((bf16[384,128]{1,0:T(8,128)(2,1)S(1)}, bf16[384,128]{1,0:T(8,128)(2,1)S(1)}, u32[]{:S(2)}, u32[]{:S(2)}) %collective-permute-start.42) | collective-permute-done | bytes 98336 | tf_op jit(solution)/shard_map/ppermute | solution.py:325
  155.6 1.3 collective-permute-start.44
  156.9 1.3 collective-permute-start.45
  160.8 1.9 collective-permute-done.44.refs_0_
  162.8 1.6 collective-permute-done.45.refs_1_
  164.4 1.4 collective-permute-done.46.refs_0_
  165.8 1.3 collective-permute-start.48
  167.1 1.3 collective-permute-start.49
  168.4 1.3 collective-permute-start.47
  169.7 1.3 collective-permute-start.50
  171.4 1.3 collective-permute-done.50.refs_0_
  181.9 1.3 collective-permute-start.64
  183.2 1.3 collective-permute-start.65
  184.5 1.3 collective-permute-start.63
  185.8 1.3 collective-permute-start.66
  187.3 44.4 %collective-permute-done.64.refs_0_ = bf16[384,128]{1,0:T(8,128)(2,1)S(1)} collective-permute-done((bf16[384,128]{1,0:T(8,128)(2,1)S(1)}, bf16[384,128]{1,0:T(8,128)(2,1)S(1)}, u32[]{:S(2)}, u32[]{:S(2)}) %collective-permute-start.64) | collective-permute-done | bytes 98336 | tf_op jit(solution)/shard_map/ppermute | solution.py:328
  231.7 1.6 collective-permute-done.65.refs_1_
  236.0 1.3 collective-permute-start.68
  237.3 1.3 collective-permute-start.69
  238.6 1.3 collective-permute-start.67
  239.9 1.3 collective-permute-start.70
  241.4 2.4 collective-permute-done.70.refs_0_
  244.4 2.1 collective-permute-start.71
  246.6 1.9 collective-permute-done.71
  (179 shorter events, 34.3 us)
Async XLA Ops:
  2.7 10.1 %collective-permute-start.1 = (bf16[3,4,128]{2,1,0:T(4,128)(2,1)S(1)}, bf16[3,4,128]{2,1,0:T(4,128)(2,1)S(1)}, u32[]{:S(2)}, u32[]{:S(2)}) collective-permute-start(bf16[3,4,128]{2,1,0:T(4,128)(2,1)S(1)} %get-tuple-element.105), channel_id=1, source_target_pairs={{0,1},{1,2},{2,3},{3,4},{4,5},{5,6},{6,7},{8,9},{9,10},{10,11},{11... | collective-permute-start | bytes 9224 | tf_op jit(solution)/shard_map/ppermute | solution.py:80
  7.1 5.8 %collective-permute-start.2 = (bf16[3,4,128]{2,1,0:T(4,128)(2,1)S(1)}, bf16[3,4,128]{2,1,0:T(4,128)(2,1)S(1)}, u32[]{:S(2)}, u32[]{:S(2)}) collective-permute-start(bf16[3,4,128]{2,1,0:T(4,128)(2,1)S(1)} %get-tuple-element.106), channel_id=1, source_target_pairs={{1,0},{2,1},{3,2},{4,3},{5,4},{6,5},{7,6},{9,8},{10,9},{11,10},{12... | collective-permute-start | bytes 9224 | tf_op jit(solution)/shard_map/ppermute | solution.py:81
  8.4 36.8 %collective-permute-start = (bf16[2,192,3072]{2,1,0:T(8,128)(2,1)S(1)}, bf16[2,192,3072]{2,1,0:T(8,128)(2,1)}, u32[]{:S(2)}, u32[]{:S(2)}) collective-permute-start(bf16[2,192,3072]{2,1,0:T(8,128)(2,1)S(1)} %select_bitcast_fusion.1.own), channel_id=1, source_target_pairs={{8,9},{9,8},{10,11},{11,10},{12,13},{13,12},{14,15},{15,14},{16,20... | collective-permute-start | bytes 7077896 | tf_op jit(solution)/shard_map/ppermute | solution.py:301
  14.7 25.1 %collective-permute-start.3 = (f32[192,128]{1,0:T(8,128)S(1)}, f32[192,128]{1,0:T(8,128)S(1)}, u32[]{:S(2)}, u32[]{:S(2)}) collective-permute-start(f32[192,128]{1,0:T(8,128)S(1)} %get-tuple-element.96), channel_id=1, source_target_pairs={{0,4},{1,5},{2,6},{3,7},{4,0},{5,1},{6,2},{7,3},{8,9},{9,8},{10,11... | collective-permute-start | bytes 294920 | tf_op jit(solution)/shard_map/ppermute | solution.py:312
  39.9 9.4 %collective-permute-start.5 = (bf16[384,128]{1,0:T(8,128)(2,1)S(1)}, bf16[384,128]{1,0:T(8,128)(2,1)S(1)}, u32[]{:S(2)}, u32[]{:S(2)}) collective-permute-start(bf16[384,128]{1,0:T(8,128)(2,1)S(1)} %get-tuple-element.80.sent), channel_id=1, source_target_pairs={{0,14},{1,10},{2,12},{3,8},{4,15},{5,11},{6,13},{7,9},{120,115},{1... | collective-permute-start | bytes 294920 | tf_op jit(solution)/shard_map/ppermute | solution.py:328
  41.2 10.3 %collective-permute-start.6 = (bf16[384,128]{1,0:T(8,128)(2,1)S(1)}, bf16[384,128]{1,0:T(8,128)(2,1)S(1)}, u32[]{:S(2)}, u32[]{:S(2)}) collective-permute-start(bf16[384,128]{1,0:T(8,128)(2,1)S(1)} %get-tuple-element.80.sent), channel_id=1, source_target_pairs={{0,10},{1,14},{2,8},{3,12},{4,11},{5,15},{6,9},{7,13},{120,114},{1... | collective-permute-start | bytes 294920 | tf_op jit(solution)/shard_map/ppermute | solution.py:328
  42.5 10.1 %collective-permute-start.4 = (bf16[384,128]{1,0:T(8,128)(2,1)S(1)}, bf16[384,128]{1,0:T(8,128)(2,1)S(1)}, u32[]{:S(2)}, u32[]{:S(2)}) collective-permute-start(bf16[384,128]{1,0:T(8,128)(2,1)S(1)} %get-tuple-element.80.sent), channel_id=1, source_target_pairs={{0,8},{1,12},{2,10},{3,14},{4,9},{5,13},{6,11},{7,15},{120,112},{1... | collective-permute-start | bytes 294920 | tf_op jit(solution)/shard_map/ppermute | solution.py:328
  43.8 9.5 %collective-permute-start.7 = (bf16[384,128]{1,0:T(8,128)(2,1)S(1)}, bf16[384,128]{1,0:T(8,128)(2,1)S(1)}, u32[]{:S(2)}, u32[]{:S(2)}) collective-permute-start(bf16[384,128]{1,0:T(8,128)(2,1)S(1)} %get-tuple-element.80.sent), channel_id=1, source_target_pairs={{0,12},{1,8},{2,14},{3,10},{4,13},{5,9},{6,15},{7,11},{120,113},{1... | collective-permute-start | bytes 294920 | tf_op jit(solution)/shard_map/ppermute | solution.py:328
  54.2 5.2 %collective-permute-start.10 = (bf16[384,128]{1,0:T(8,128)(2,1)S(1)}, bf16[384,128]{1,0:T(8,128)(2,1)S(1)}, u32[]{:S(2)}, u32[]{:S(2)}) collective-permute-start(bf16[384,128]{1,0:T(8,128)(2,1)S(1)} %get-tuple-element.48.sent), channel_id=1, source_target_pairs={{8,18},{9,22},{10,16},{11,20},{12,19},{13,23},{14,17},{15,21},{112... | collective-permute-start | bytes 294920 | tf_op jit(solution)/shard_map/ppermute | solution.py:328
  55.5 3.9 %collective-permute-start.9 = (bf16[384,128]{1,0:T(8,128)(2,1)S(1)}, bf16[384,128]{1,0:T(8,128)(2,1)S(1)}, u32[]{:S(2)}, u32[]{:S(2)}) collective-permute-start(bf16[384,128]{1,0:T(8,128)(2,1)S(1)} %get-tuple-element.48.sent), channel_id=1, source_target_pairs={{8,19},{9,23},{10,17},{11,21},{12,18},{13,22},{14,16},{15,20},{112... | collective-permute-start | bytes 294920 | tf_op jit(solution)/shard_map/ppermute | solution.py:328
  56.8 2.9 %collective-permute-start.8 = (bf16[384,128]{1,0:T(8,128)(2,1)S(1)}, bf16[384,128]{1,0:T(8,128)(2,1)S(1)}, u32[]{:S(2)}, u32[]{:S(2)}) collective-permute-start(bf16[384,128]{1,0:T(8,128)(2,1)S(1)} %get-tuple-element.48.sent), channel_id=1, source_target_pairs={{8,16},{9,20},{10,18},{11,22},{12,17},{13,21},{14,19},{15,23},{112... | collective-permute-start | bytes 294920 | tf_op jit(solution)/shard_map/ppermute | solution.py:328
  58.1 2.9 %collective-permute-start.11 = (bf16[384,128]{1,0:T(8,128)(2,1)S(1)}, bf16[384,128]{1,0:T(8,128)(2,1)S(1)}, u32[]{:S(2)}, u32[]{:S(2)}) collective-permute-start(bf16[384,128]{1,0:T(8,128)(2,1)S(1)} %get-tuple-element.48.sent), channel_id=1, source_target_pairs={{8,17},{9,21},{10,19},{11,23},{12,16},{13,20},{14,18},{15,22},{112... | collective-permute-start | bytes 294920 | tf_op jit(solution)/shard_map/ppermute | solution.py:328
  61.0 5.2 %collective-permute-start.13 = (bf16[384,128]{1,0:T(8,128)(2,1)S(1)}, bf16[384,128]{1,0:T(8,128)(2,1)S(1)}, u32[]{:S(2)}, u32[]{:S(2)}) collective-permute-start(bf16[384,128]{1,0:T(8,128)(2,1)S(1)} %get-tuple-element.50.sent), channel_id=1, source_target_pairs={{16,30},{17,26},{18,28},{19,24},{20,31},{21,27},{22,29},{23,25},{1... | collective-permute-start | bytes 294920 | tf_op jit(solution)/shard_map/ppermute | solution.py:328
  62.3 3.9 %collective-permute-start.14 = (bf16[384,128]{1,0:T(8,128)(2,1)S(1)}, bf16[384,128]{1,0:T(8,128)(2,1)S(1)}, u32[]{:S(2)}, u32[]{:S(2)}) collective-permute-start(bf16[384,128]{1,0:T(8,128)(2,1)S(1)} %get-tuple-element.50.sent), channel_id=1, source_target_pairs={{16,26},{17,30},{18,24},{19,28},{20,27},{21,31},{22,25},{23,29},{1... | collective-permute-start | bytes 294920 | tf_op jit(solution)/shard_map/ppermute | solution.py:328
  63.6 2.7 %collective-permute-start.12 = (bf16[384,128]{1,0:T(8,128)(2,1)S(1)}, bf16[384,128]{1,0:T(8,128)(2,1)S(1)}, u32[]{:S(2)}, u32[]{:S(2)}) collective-permute-start(bf16[384,128]{1,0:T(8,128)(2,1)S(1)} %get-tuple-element.50.sent), channel_id=1, source_target_pairs={{16,24},{17,28},{18,26},{19,30},{20,25},{21,29},{22,27},{23,31},{1... | collective-permute-start | bytes 294920 | tf_op jit(solution)/shard_map/ppermute | solution.py:328
  64.9 3.3 %collective-permute-start.15 = (bf16[384,128]{1,0:T(8,128)(2,1)S(1)}, bf16[384,128]{1,0:T(8,128)(2,1)S(1)}, u32[]{:S(2)}, u32[]{:S(2)}) collective-permute-start(bf16[384,128]{1,0:T(8,128)(2,1)S(1)} %get-tuple-element.50.sent), channel_id=1, source_target_pairs={{16,28},{17,24},{18,30},{19,26},{20,29},{21,25},{22,31},{23,27},{1... | collective-permute-start | bytes 294920 | tf_op jit(solution)/shard_map/ppermute | solution.py:328
  68.2 8.8 %collective-permute-start.17 = (bf16[384,128]{1,0:T(8,128)(2,1)S(1)}, bf16[384,128]{1,0:T(8,128)(2,1)S(1)}, u32[]{:S(2)}, u32[]{:S(2)}) collective-permute-start(bf16[384,128]{1,0:T(8,128)(2,1)S(1)} %get-tuple-element.52.sent), channel_id=1, source_target_pairs={{24,35},{25,39},{26,33},{27,37},{28,34},{29,38},{30,32},{31,36},{9... | collective-permute-start | bytes 294920 | tf_op jit(solution)/shard_map/ppermute | solution.py:328
  69.5 9.4 %collective-permute-start.18 = (bf16[384,128]{1,0:T(8,128)(2,1)S(1)}, bf16[384,128]{1,0:T(8,128)(2,1)S(1)}, u32[]{:S(2)}, u32[]{:S(2)}) collective-permute-start(bf16[384,128]{1,0:T(8,128)(2,1)S(1)} %get-tuple-element.52.sent), channel_id=1, source_target_pairs={{24,34},{25,38},{26,32},{27,36},{28,35},{29,39},{30,33},{31,37},{9... | collective-permute-start | bytes 294920 | tf_op jit(solution)/shard_map/ppermute | solution.py:328
  70.8 8.1 %collective-permute-start.16 = (bf16[384,128]{1,0:T(8,128)(2,1)S(1)}, bf16[384,128]{1,0:T(8,128)(2,1)S(1)}, u32[]{:S(2)}, u32[]{:S(2)}) collective-permute-start(bf16[384,128]{1,0:T(8,128)(2,1)S(1)} %get-tuple-element.52.sent), channel_id=1, source_target_pairs={{24,32},{25,36},{26,34},{27,38},{28,33},{29,37},{30,35},{31,39},{9... | collective-permute-start | bytes 294920 | tf_op jit(solution)/shard_map/ppermute | solution.py:328
  72.1 8.5 %collective-permute-start.19 = (bf16[384,128]{1,0:T(8,128)(2,1)S(1)}, bf16[384,128]{1,0:T(8,128)(2,1)S(1)}, u32[]{:S(2)}, u32[]{:S(2)}) collective-permute-start(bf16[384,128]{1,0:T(8,128)(2,1)S(1)} %get-tuple-element.52.sent), channel_id=1, source_target_pairs={{24,33},{25,37},{26,35},{27,39},{28,32},{29,36},{30,34},{31,38},{9... | collective-permute-start | bytes 294920 | tf_op jit(solution)/shard_map/ppermute | solution.py:328
  80.7 2.7 %collective-permute-start.21 = (bf16[384,128]{1,0:T(8,128)(2,1)S(1)}, bf16[384,128]{1,0:T(8,128)(2,1)S(1)}, u32[]{:S(2)}, u32[]{:S(2)}) collective-permute-start(bf16[384,128]{1,0:T(8,128)(2,1)S(1)} %get-tuple-element.54.sent), channel_id=1, source_target_pairs={{32,46},{33,42},{34,44},{35,40},{36,47},{37,43},{38,45},{39,41},{8... | collective-permute-start | bytes 294920 | tf_op jit(solution)/shard_map/ppermute | solution.py:328
  81.4 2.0 collective-permute-start.22
  83.6 4.1 %collective-permute-start.25 = (bf16[384,128]{1,0:T(8,128)(2,1)S(1)}, bf16[384,128]{1,0:T(8,128)(2,1)S(1)}, u32[]{:S(2)}, u32[]{:S(2)}) collective-permute-start(bf16[384,128]{1,0:T(8,128)(2,1)S(1)} %get-tuple-element.56.sent), channel_id=1, source_target_pairs={{40,51},{41,55},{42,49},{43,53},{44,50},{45,54},{46,48},{47,52},{8... | collective-permute-start | bytes 294920 | tf_op jit(solution)/shard_map/ppermute | solution.py:328
  84.4 3.3 %collective-permute-start.26 = (bf16[384,128]{1,0:T(8,128)(2,1)S(1)}, bf16[384,128]{1,0:T(8,128)(2,1)S(1)}, u32[]{:S(2)}, u32[]{:S(2)}) collective-permute-start(bf16[384,128]{1,0:T(8,128)(2,1)S(1)} %get-tuple-element.56.sent), channel_id=1, source_target_pairs={{40,50},{41,54},{42,48},{43,52},{44,51},{45,55},{46,49},{47,53},{8... | collective-permute-start | bytes 294920 | tf_op jit(solution)/shard_map/ppermute | solution.py:328
  85.2 2.5 collective-permute-start.24
  86.8 5.1 %collective-permute-start.29 = (bf16[2,192,3072]{2,1,0:T(8,128)(2,1)S(1)}, bf16[2,192,3072]{2,1,0:T(8,128)(2,1)S(1)}, u32[]{:S(2)}, u32[]{:S(2)}) collective-permute-start(bf16[2,192,3072]{2,1,0:T(8,128)(2,1)S(1)} %select_bitcast_fusion.own), channel_id=1, source_target_pairs={{32,36},{33,37},{34,38},{35,39},{36,32},{37,33},{38,34},{39,35},{4... | collective-permute-start | bytes 7077896 | tf_op jit(solution)/shard_map/ppermute | solution.py:320
  87.8 29.6 %collective-permute-start.28 = (bf16[2,192,3072]{2,1,0:T(8,128)(2,1)S(1)}, bf16[2,192,3072]{2,1,0:T(8,128)(2,1)S(1)}, u32[]{:S(2)}, u32[]{:S(2)}) collective-permute-start(bf16[2,192,3072]{2,1,0:T(8,128)(2,1)S(1)} %select_bitcast_fusion.own), channel_id=1, source_target_pairs={{0,4},{1,5},{2,6},{3,7},{4,0},{5,1},{6,2},{7,3},{8,9},{9,8},{10,11... | collective-permute-start | bytes 7077896 | tf_op jit(solution)/shard_map/ppermute | solution.py:346
  89.9 30.3 %collective-permute-start.31 = (bf16[384,128]{1,0:T(8,128)(2,1)S(1)}, bf16[384,128]{1,0:T(8,128)(2,1)S(1)}, u32[]{:S(2)}, u32[]{:S(2)}) collective-permute-start(bf16[384,128]{1,0:T(8,128)(2,1)S(1)} %get-tuple-element.61.sent), channel_id=1, source_target_pairs={{48,62},{49,58},{50,60},{51,56},{52,63},{53,59},{54,61},{55,57},{7... | collective-permute-start | bytes 294920 | tf_op jit(solution)/shard_map/ppermute | solution.py:328
  90.5 29.7 %collective-permute-start.32 = (bf16[384,128]{1,0:T(8,128)(2,1)S(1)}, bf16[384,128]{1,0:T(8,128)(2,1)S(1)}, u32[]{:S(2)}, u32[]{:S(2)}) collective-permute-start(bf16[384,128]{1,0:T(8,128)(2,1)S(1)} %get-tuple-element.61.sent), channel_id=1, source_target_pairs={{48,58},{49,62},{50,56},{51,60},{52,59},{53,63},{54,57},{55,61},{7... | collective-permute-start | bytes 294920 | tf_op jit(solution)/shard_map/ppermute | solution.py:328
  91.2 29.0 %collective-permute-start.30 = (bf16[384,128]{1,0:T(8,128)(2,1)S(1)}, bf16[384,128]{1,0:T(8,128)(2,1)S(1)}, u32[]{:S(2)}, u32[]{:S(2)}) collective-permute-start(bf16[384,128]{1,0:T(8,128)(2,1)S(1)} %get-tuple-element.61.sent), channel_id=1, source_target_pairs={{48,56},{49,60},{50,58},{51,62},{52,57},{53,61},{54,59},{55,63},{7... | collective-permute-start | bytes 294920 | tf_op jit(solution)/shard_map/ppermute | solution.py:328
  91.9 28.4 %collective-permute-start.33 = (bf16[384,128]{1,0:T(8,128)(2,1)S(1)}, bf16[384,128]{1,0:T(8,128)(2,1)S(1)}, u32[]{:S(2)}, u32[]{:S(2)}) collective-permute-start(bf16[384,128]{1,0:T(8,128)(2,1)S(1)} %get-tuple-element.61.sent), channel_id=1, source_target_pairs={{48,60},{49,56},{50,62},{51,58},{52,61},{53,57},{54,63},{55,59},{7... | collective-permute-start | bytes 294920 | tf_op jit(solution)/shard_map/ppermute | solution.py:328
  120.3 6.5 %collective-permute-start.39 = (bf16[384,128]{1,0:T(8,128)(2,1)S(1)}, bf16[384,128]{1,0:T(8,128)(2,1)S(1)}, u32[]{:S(2)}, u32[]{:S(2)}) collective-permute-start(bf16[384,128]{1,0:T(8,128)(2,1)S(1)} %get-tuple-element.64.sent), channel_id=1, source_target_pairs={{16,26},{17,30},{18,24},{19,28},{20,27},{21,31},{22,25},{23,29},{1... | collective-permute-start | bytes 294920 | tf_op jit(solution)/shard_map/ppermute | solution.py:324
  121.6 20.6 %collective-permute-start.40 = (bf16[384,128]{1,0:T(8,128)(2,1)S(1)}, bf16[384,128]{1,0:T(8,128)(2,1)S(1)}, u32[]{:S(2)}, u32[]{:S(2)}) collective-permute-start(bf16[384,128]{1,0:T(8,128)(2,1)S(1)} %get-tuple-element.64.sent), channel_id=1, source_target_pairs={{24,34},{25,38},{26,32},{27,36},{28,35},{29,39},{30,33},{31,37},{9... | collective-permute-start | bytes 294920 | tf_op jit(solution)/shard_map/ppermute | solution.py:325
  122.9 20.6 %collective-permute-start.37 = (bf16[384,128]{1,0:T(8,128)(2,1)S(1)}, bf16[384,128]{1,0:T(8,128)(2,1)S(1)}, u32[]{:S(2)}, u32[]{:S(2)}) collective-permute-start(bf16[384,128]{1,0:T(8,128)(2,1)S(1)} %get-tuple-element.64.sent), channel_id=1, source_target_pairs={{16,30},{17,26},{18,28},{19,24},{20,31},{21,27},{22,29},{23,25},{1... | collective-permute-start | bytes 294920 | tf_op jit(solution)/shard_map/ppermute | solution.py:324
  124.2 27.0 %collective-permute-start.38 = (bf16[384,128]{1,0:T(8,128)(2,1)S(1)}, bf16[384,128]{1,0:T(8,128)(2,1)S(1)}, u32[]{:S(2)}, u32[]{:S(2)}) collective-permute-start(bf16[384,128]{1,0:T(8,128)(2,1)S(1)} %get-tuple-element.64.sent), channel_id=1, source_target_pairs={{24,35},{25,39},{26,33},{27,37},{28,34},{29,38},{30,32},{31,36},{9... | collective-permute-start | bytes 294920 | tf_op jit(solution)/shard_map/ppermute | solution.py:325
  125.5 25.8 %collective-permute-start.35 = (bf16[384,128]{1,0:T(8,128)(2,1)S(1)}, bf16[384,128]{1,0:T(8,128)(2,1)S(1)}, u32[]{:S(2)}, u32[]{:S(2)}) collective-permute-start(bf16[384,128]{1,0:T(8,128)(2,1)S(1)} %get-tuple-element.64.sent), channel_id=1, source_target_pairs={{16,24},{17,28},{18,26},{19,30},{20,25},{21,29},{22,27},{23,31},{1... | collective-permute-start | bytes 294920 | tf_op jit(solution)/shard_map/ppermute | solution.py:324
  126.8 24.7 %collective-permute-start.36 = (bf16[384,128]{1,0:T(8,128)(2,1)S(1)}, bf16[384,128]{1,0:T(8,128)(2,1)S(1)}, u32[]{:S(2)}, u32[]{:S(2)}) collective-permute-start(bf16[384,128]{1,0:T(8,128)(2,1)S(1)} %get-tuple-element.64.sent), channel_id=1, source_target_pairs={{24,32},{25,36},{26,34},{27,38},{28,33},{29,37},{30,35},{31,39},{9... | collective-permute-start | bytes 294920 | tf_op jit(solution)/shard_map/ppermute | solution.py:325
  142.2 9.4 %collective-permute-start.41 = (bf16[384,128]{1,0:T(8,128)(2,1)S(1)}, bf16[384,128]{1,0:T(8,128)(2,1)S(1)}, u32[]{:S(2)}, u32[]{:S(2)}) collective-permute-start(bf16[384,128]{1,0:T(8,128)(2,1)S(1)} %get-tuple-element.64.sent), channel_id=1, source_target_pairs={{16,28},{17,24},{18,30},{19,26},{20,29},{21,25},{22,31},{23,27},{1... | collective-permute-start | bytes 294920 | tf_op jit(solution)/shard_map/ppermute | solution.py:324
  143.5 12.0 %collective-permute-start.42 = (bf16[384,128]{1,0:T(8,128)(2,1)S(1)}, bf16[384,128]{1,0:T(8,128)(2,1)S(1)}, u32[]{:S(2)}, u32[]{:S(2)}) collective-permute-start(bf16[384,128]{1,0:T(8,128)(2,1)S(1)} %get-tuple-element.64.sent), channel_id=1, source_target_pairs={{24,33},{25,37},{26,35},{27,39},{28,32},{29,36},{30,34},{31,38},{9... | collective-permute-start | bytes 294920 | tf_op jit(solution)/shard_map/ppermute | solution.py:325
  155.6 7.1 %collective-permute-start.44 = (bf16[384,128]{1,0:T(8,128)(2,1)S(1)}, bf16[384,128]{1,0:T(8,128)(2,1)S(1)}, u32[]{:S(2)}, u32[]{:S(2)}) collective-permute-start(bf16[384,128]{1,0:T(8,128)(2,1)S(1)} %get-tuple-element.66.sent), channel_id=1, source_target_pairs={{0,14},{1,10},{2,12},{3,8},{4,15},{5,11},{6,13},{7,9},{120,115},{1... | collective-permute-start | bytes 294920 | tf_op jit(solution)/shard_map/ppermute | solution.py:328
  156.9 7.4 %collective-permute-start.45 = (bf16[384,128]{1,0:T(8,128)(2,1)S(1)}, bf16[384,128]{1,0:T(8,128)(2,1)S(1)}, u32[]{:S(2)}, u32[]{:S(2)}) collective-permute-start(bf16[384,128]{1,0:T(8,128)(2,1)S(1)} %get-tuple-element.66.sent), channel_id=1, source_target_pairs={{0,10},{1,14},{2,8},{3,12},{4,11},{5,15},{6,9},{7,13},{120,114},{1... | collective-permute-start | bytes 294920 | tf_op jit(solution)/shard_map/ppermute | solution.py:328
  158.2 6.1 %collective-permute-start.43 = (bf16[384,128]{1,0:T(8,128)(2,1)S(1)}, bf16[384,128]{1,0:T(8,128)(2,1)S(1)}, u32[]{:S(2)}, u32[]{:S(2)}) collective-permute-start(bf16[384,128]{1,0:T(8,128)(2,1)S(1)} %get-tuple-element.66.sent), channel_id=1, source_target_pairs={{0,8},{1,12},{2,10},{3,14},{4,9},{5,13},{6,11},{7,15},{120,112},{1... | collective-permute-start | bytes 294920 | tf_op jit(solution)/shard_map/ppermute | solution.py:328
  159.5 6.3 %collective-permute-start.46 = (bf16[384,128]{1,0:T(8,128)(2,1)S(1)}, bf16[384,128]{1,0:T(8,128)(2,1)S(1)}, u32[]{:S(2)}, u32[]{:S(2)}) collective-permute-start(bf16[384,128]{1,0:T(8,128)(2,1)S(1)} %get-tuple-element.66.sent), channel_id=1, source_target_pairs={{0,12},{1,8},{2,14},{3,10},{4,13},{5,9},{6,15},{7,11},{120,113},{1... | collective-permute-start | bytes 294920 | tf_op jit(solution)/shard_map/ppermute | solution.py:328
  165.8 5.2 %collective-permute-start.48 = (bf16[384,128]{1,0:T(8,128)(2,1)S(1)}, bf16[384,128]{1,0:T(8,128)(2,1)S(1)}, u32[]{:S(2)}, u32[]{:S(2)}) collective-permute-start(bf16[384,128]{1,0:T(8,128)(2,1)S(1)} %get-tuple-element.68.sent), channel_id=1, source_target_pairs={{8,19},{9,23},{10,17},{11,21},{12,18},{13,22},{14,16},{15,20},{112... | collective-permute-start | bytes 294920 | tf_op jit(solution)/shard_map/ppermute | solution.py:328
  167.1 3.9 %collective-permute-start.49 = (bf16[384,128]{1,0:T(8,128)(2,1)S(1)}, bf16[384,128]{1,0:T(8,128)(2,1)S(1)}, u32[]{:S(2)}, u32[]{:S(2)}) collective-permute-start(bf16[384,128]{1,0:T(8,128)(2,1)S(1)} %get-tuple-element.68.sent), channel_id=1, source_target_pairs={{8,18},{9,22},{10,16},{11,20},{12,19},{13,23},{14,17},{15,21},{112... | collective-permute-start | bytes 294920 | tf_op jit(solution)/shard_map/ppermute | solution.py:328
  168.4 2.9 %collective-permute-start.47 = (bf16[384,128]{1,0:T(8,128)(2,1)S(1)}, bf16[384,128]{1,0:T(8,128)(2,1)S(1)}, u32[]{:S(2)}, u32[]{:S(2)}) collective-permute-start(bf16[384,128]{1,0:T(8,128)(2,1)S(1)} %get-tuple-element.68.sent), channel_id=1, source_target_pairs={{8,16},{9,20},{10,18},{11,22},{12,17},{13,21},{14,19},{15,23},{112... | collective-permute-start | bytes 294920 | tf_op jit(solution)/shard_map/ppermute | solution.py:328
  169.7 2.9 %collective-permute-start.50 = (bf16[384,128]{1,0:T(8,128)(2,1)S(1)}, bf16[384,128]{1,0:T(8,128)(2,1)S(1)}, u32[]{:S(2)}, u32[]{:S(2)}) collective-permute-start(bf16[384,128]{1,0:T(8,128)(2,1)S(1)} %get-tuple-element.68.sent), channel_id=1, source_target_pairs={{8,17},{9,21},{10,19},{11,23},{12,16},{13,20},{14,18},{15,22},{112... | collective-permute-start | bytes 294920 | tf_op jit(solution)/shard_map/ppermute | solution.py:328
  172.7 2.7 %collective-permute-start.52 = (bf16[384,128]{1,0:T(8,128)(2,1)S(1)}, bf16[384,128]{1,0:T(8,128)(2,1)S(1)}, u32[]{:S(2)}, u32[]{:S(2)}) collective-permute-start(bf16[384,128]{1,0:T(8,128)(2,1)S(1)} %get-tuple-element.70.sent), channel_id=1, source_target_pairs={{48,62},{49,58},{50,60},{51,56},{52,63},{53,59},{54,61},{55,57},{7... | collective-permute-start | bytes 294920 | tf_op jit(solution)/shard_map/ppermute | solution.py:328
  173.4 2.0 collective-permute-start.53
  175.5 3.3 %collective-permute-start.56 = (bf16[384,128]{1,0:T(8,128)(2,1)S(1)}, bf16[384,128]{1,0:T(8,128)(2,1)S(1)}, u32[]{:S(2)}, u32[]{:S(2)}) collective-permute-start(bf16[384,128]{1,0:T(8,128)(2,1)S(1)} %get-tuple-element.72.sent), channel_id=1, source_target_pairs={{40,51},{41,55},{42,49},{43,53},{44,50},{45,54},{46,48},{47,52},{8... | collective-permute-start | bytes 294920 | tf_op jit(solution)/shard_map/ppermute | solution.py:328
  176.2 2.6 %collective-permute-start.57 = (bf16[384,128]{1,0:T(8,128)(2,1)S(1)}, bf16[384,128]{1,0:T(8,128)(2,1)S(1)}, u32[]{:S(2)}, u32[]{:S(2)}) collective-permute-start(bf16[384,128]{1,0:T(8,128)(2,1)S(1)} %get-tuple-element.72.sent), channel_id=1, source_target_pairs={{40,50},{41,54},{42,48},{43,52},{44,51},{45,55},{46,49},{47,53},{8... | collective-permute-start | bytes 294920 | tf_op jit(solution)/shard_map/ppermute | solution.py:328
  176.9 2.0 collective-permute-start.55
  178.2 3.5 %collective-permute-start.34 = (f32[192,128]{1,0:T(8,128)S(1)}, f32[192,128]{1,0:T(8,128)S(1)}, u32[]{:S(2)}, u32[]{:S(2)}) collective-permute-start(f32[192,128]{1,0:T(8,128)S(1)} %slice_select_fusion.3), channel_id=1, source_target_pairs={{0,4},{1,5},{2,6},{3,7},{4,0},{5,1},{6,2},{7,3},{8,9},{9,8},{10,11... | collective-permute-start | bytes 294920 | tf_op jit(solution)/shard_map/ppermute | solution.py:335
  178.9 2.9 %collective-permute-start.60 = (bf16[384,128]{1,0:T(8,128)(2,1)S(1)}, bf16[384,128]{1,0:T(8,128)(2,1)S(1)}, u32[]{:S(2)}, u32[]{:S(2)}) collective-permute-start(bf16[384,128]{1,0:T(8,128)(2,1)S(1)} %get-tuple-element.74.sent), channel_id=1, source_target_pairs={{32,46},{33,42},{34,44},{35,40},{36,47},{37,43},{38,45},{39,41},{8... | collective-permute-start | bytes 294920 | tf_op jit(solution)/shard_map/ppermute | solution.py:328
  179.6 2.2 collective-permute-start.61
  181.9 49.7 %collective-permute-start.64 = (bf16[384,128]{1,0:T(8,128)(2,1)S(1)}, bf16[384,128]{1,0:T(8,128)(2,1)S(1)}, u32[]{:S(2)}, u32[]{:S(2)}) collective-permute-start(bf16[384,128]{1,0:T(8,128)(2,1)S(1)} %get-tuple-element.76.sent), channel_id=1, source_target_pairs={{24,35},{25,39},{26,33},{27,37},{28,34},{29,38},{30,32},{31,36},{9... | collective-permute-start | bytes 294920 | tf_op jit(solution)/shard_map/ppermute | solution.py:328
  183.2 50.0 %collective-permute-start.65 = (bf16[384,128]{1,0:T(8,128)(2,1)S(1)}, bf16[384,128]{1,0:T(8,128)(2,1)S(1)}, u32[]{:S(2)}, u32[]{:S(2)}) collective-permute-start(bf16[384,128]{1,0:T(8,128)(2,1)S(1)} %get-tuple-element.76.sent), channel_id=1, source_target_pairs={{24,34},{25,38},{26,32},{27,36},{28,35},{29,39},{30,33},{31,37},{9... | collective-permute-start | bytes 294920 | tf_op jit(solution)/shard_map/ppermute | solution.py:328
  184.5 49.8 %collective-permute-start.63 = (bf16[384,128]{1,0:T(8,128)(2,1)S(1)}, bf16[384,128]{1,0:T(8,128)(2,1)S(1)}, u32[]{:S(2)}, u32[]{:S(2)}) collective-permute-start(bf16[384,128]{1,0:T(8,128)(2,1)S(1)} %get-tuple-element.76.sent), channel_id=1, source_target_pairs={{24,32},{25,36},{26,34},{27,38},{28,33},{29,37},{30,35},{31,39},{9... | collective-permute-start | bytes 294920 | tf_op jit(solution)/shard_map/ppermute | solution.py:328
  185.8 49.2 %collective-permute-start.66 = (bf16[384,128]{1,0:T(8,128)(2,1)S(1)}, bf16[384,128]{1,0:T(8,128)(2,1)S(1)}, u32[]{:S(2)}, u32[]{:S(2)}) collective-permute-start(bf16[384,128]{1,0:T(8,128)(2,1)S(1)} %get-tuple-element.76.sent), channel_id=1, source_target_pairs={{24,33},{25,37},{26,35},{27,39},{28,32},{29,36},{30,34},{31,38},{9... | collective-permute-start | bytes 294920 | tf_op jit(solution)/shard_map/ppermute | solution.py:328
  236.0 5.3 %collective-permute-start.68 = (bf16[384,128]{1,0:T(8,128)(2,1)S(1)}, bf16[384,128]{1,0:T(8,128)(2,1)S(1)}, u32[]{:S(2)}, u32[]{:S(2)}) collective-permute-start(bf16[384,128]{1,0:T(8,128)(2,1)S(1)} %get-tuple-element.78.sent), channel_id=1, source_target_pairs={{16,30},{17,26},{18,28},{19,24},{20,31},{21,27},{22,29},{23,25},{1... | collective-permute-start | bytes 294920 | tf_op jit(solution)/shard_map/ppermute | solution.py:328
  237.3 4.0 %collective-permute-start.69 = (bf16[384,128]{1,0:T(8,128)(2,1)S(1)}, bf16[384,128]{1,0:T(8,128)(2,1)S(1)}, u32[]{:S(2)}, u32[]{:S(2)}) collective-permute-start(bf16[384,128]{1,0:T(8,128)(2,1)S(1)} %get-tuple-element.78.sent), channel_id=1, source_target_pairs={{16,26},{17,30},{18,24},{19,28},{20,27},{21,31},{22,25},{23,29},{1... | collective-permute-start | bytes 294920 | tf_op jit(solution)/shard_map/ppermute | solution.py:328
  238.6 2.8 %collective-permute-start.67 = (bf16[384,128]{1,0:T(8,128)(2,1)S(1)}, bf16[384,128]{1,0:T(8,128)(2,1)S(1)}, u32[]{:S(2)}, u32[]{:S(2)}) collective-permute-start(bf16[384,128]{1,0:T(8,128)(2,1)S(1)} %get-tuple-element.78.sent), channel_id=1, source_target_pairs={{16,24},{17,28},{18,26},{19,30},{20,25},{21,29},{22,27},{23,31},{1... | collective-permute-start | bytes 294920 | tf_op jit(solution)/shard_map/ppermute | solution.py:328
  239.9 3.9 %collective-permute-start.70 = (bf16[384,128]{1,0:T(8,128)(2,1)S(1)}, bf16[384,128]{1,0:T(8,128)(2,1)S(1)}, u32[]{:S(2)}, u32[]{:S(2)}) collective-permute-start(bf16[384,128]{1,0:T(8,128)(2,1)S(1)} %get-tuple-element.78.sent), channel_id=1, source_target_pairs={{16,28},{17,24},{18,30},{19,26},{20,29},{21,25},{22,31},{23,27},{1... | collective-permute-start | bytes 294920 | tf_op jit(solution)/shard_map/ppermute | solution.py:328
  244.4 4.1 %collective-permute-start.71 = (f32[192,128]{1,0:T(8,128)S(1)}, f32[192,128]{1,0:T(8,128)S(1)}, u32[]{:S(2)}, u32[]{:S(2)}) collective-permute-start(f32[192,128]{1,0:T(8,128)S(1)} %slice_select_fusion.1), channel_id=1, source_target_pairs={{0,4},{1,5},{2,6},{3,7},{4,0},{5,1},{6,2},{7,3},{8,9},{9,8},{10,11... | collective-permute-start | bytes 294920 | tf_op jit(solution)/shard_map/ppermute | solution.py:335
  (12 other events, 20.1 us)
